TPU v7x, 32 devices: a whole 2x2x4 slice. The times are simulated.
32 devices in a mesh: member: 2 (over y), lat: 4 (over z), lev: 2 (over x), lon: 2 (over core).
Axes of the slice: x: 2, y: 2, z: 4, core: 2. Of those that a mesh axis runs over, the one named last changes fastest.
Arguments:
- land_mask: int32 [72, 128, 768], P('lev', 'lat', 'lon'), may hold values 0 or 1
- diffusivity: float32 [72, 128, 768], P('lev', 'lat', 'lon'), may hold values from 0.3 to 3
- balance: float32 [72, 72], replicated, may hold values from -0.75 to 0.75
- member_id: int32 [2], P('member'), parts along dimension 0, may hold values from 0 to 63
- counter_key: int32 [2], P('member'), parts along dimension 0, may hold values from 0 to 1048575
Outputs:
- perturbation: float32 [144, 128, 768], P('member', ('lat', 'lev'), 'lon'), parts along dimension 0
There are 2 independent parts, one for each index of `member`. A program takes and returns all parts, laid end to end along the dimension named above; an argument that names none is the same for every part. Nothing has to cross between parts.
All inputs are finite; a program needn't handle non-finite values. No bound on the sum of `land_mask` on one device may be relied on, other than what follows from the above.
Results may differ from a plain program's by a relative error of at most 0.00009.
Values sent between devices are 32-bit elements; how exact they have to be, the bound alone decides.
No kernel may reach another device: no remote copies, remote signals or barrier semaphores. Data moves between devices by JAX's collectives and lax.ppermute only.
A program may use at most 192 MiB of HBM per device.

v0:
```python
import math

import jax
import jax.numpy as jnp
from jax import lax
from jax.sharding import PartitionSpec as P

SWEEPS = 12


noise_scale = math.sqrt(3.0) / 65536.0


def passed_along(block, axis, distance):
    devices = range(lax.axis_size(axis))
    route = [((i - distance) % len(devices), i) for i in devices]
    return lax.ppermute(block, axis, route)


def extended(cells, sides, width):
    for axis, dim in sides:
        count = lax.axis_size(axis)
        ends = count - 1
        head = lax.slice_in_dim(cells, 0, width, axis=dim)
        tail = lax.slice_in_dim(cells, cells.shape[dim] - width, cells.shape[dim], axis=dim)
        cells = jnp.concatenate(
            [
                lax.ppermute(tail, axis, [(i, (i + 1) % count) for i in range(ends)]),
                cells,
                lax.ppermute(head, axis, [((i + 1) % count, i) for i in range(ends)]),
            ],
            axis=dim,
        )
    return cells


def scramble(values):
    values = values * 1103515245 + 12345
    values = jnp.bitwise_xor(values, jnp.right_shift(values, 15))
    values = values * 747796405 + 1013904223
    values = jnp.bitwise_xor(values, jnp.right_shift(values, 13))
    values = values * 277803737
    return jnp.bitwise_xor(values, jnp.right_shift(values, 16))


def make_noise(level_ids, row_ids, col_ids, total_rows, total_cols, stream_base):
    global_index = (
        level_ids[:, None, None] * total_rows + row_ids[None, :, None]
    ) * total_cols + col_ids[None, None, :]
    first = scramble(jnp.bitwise_xor(global_index, stream_base))
    second = scramble(first + 1664525)
    total = (
        jnp.bitwise_and(first, 65535)
        + jnp.bitwise_and(jnp.right_shift(first, 16), 65535)
        + jnp.bitwise_and(second, 65535)
        + jnp.bitwise_and(jnp.right_shift(second, 16), 65535)
        - 131070
    )
    return total.astype(jnp.float32) * noise_scale


def with_edges(values, west_edge, east_edge):
    columns = lax.broadcasted_iota(jnp.int32, values.shape, 2)
    last_col = values.shape[2] - 1
    west_side = jnp.where(columns == 0, west_edge, jnp.roll(values, 1, axis=2))
    east_side = jnp.where(columns == last_col, east_edge, jnp.roll(values, -1, axis=2))
    return (west_side, east_side)


def field_sides(values):
    west_edge = passed_along(values[:, :, -1:], "lon", 1)
    east_edge = passed_along(values[:, :, :1], "lon", -1)
    return with_edges(values, west_edge, east_edge)


def relax(field, source, north, south, west, east, denom, rim, depth):
    offset = depth - rim
    height = field.shape[1]
    lower = offset + 1
    upper = offset + height - 1
    inner = field[:, 1:-1, :]
    west_field, east_field = field_sides(inner)
    return (
        source[:, lower:upper]
        + north[:, lower:upper] * field[:, :-2, :]
        + south[:, lower:upper] * field[:, 2:, :]
        + west[:, lower:upper] * west_field
        + east[:, lower:upper] * east_field
    ) / denom[:, lower:upper]


def per_device(land_mask, diffusivity, balance, member_id, counter_key):
    levels, rows, breadth = land_mask.shape
    depth = 1
    total_rows = rows * lax.axis_size("lat")
    total_cols = breadth * lax.axis_size("lon")
    level_start = lax.axis_index("lev") * levels
    row_start = lax.axis_index("lat") * rows
    col_start = lax.axis_index("lon") * breadth
    stream_base = counter_key[0] * 69069 + member_id[0] * 362437
    level_ids = level_start + jnp.arange(levels, dtype=jnp.int32)
    row_ids = row_start - depth + jnp.arange(rows + 2 * depth, dtype=jnp.int32)
    col_ids = col_start + jnp.arange(breadth, dtype=jnp.int32)
    source_wide = make_noise(level_ids, row_ids, col_ids, total_rows, total_cols, stream_base)
    sea_cells = land_mask.astype(jnp.float32)
    conduct = diffusivity * sea_cells
    conduct_wide = extended(conduct, (("lat", 1),), depth)
    coef_west_edge = passed_along(conduct_wide[:, :, -1:], "lon", 1)
    coef_east_edge = passed_along(conduct_wide[:, :, :1], "lon", -1)
    west_conduct, east_conduct = with_edges(conduct_wide, coef_west_edge, coef_east_edge)
    zero_row = jnp.zeros((levels, 1, breadth), jnp.float32)
    north = conduct_wide * jnp.concatenate([zero_row, conduct_wide[:, :-1, :]], axis=1)
    south = conduct_wide * jnp.concatenate([conduct_wide[:, 1:, :], zero_row], axis=1)
    west = conduct_wide * west_conduct
    east = conduct_wide * east_conduct
    denom = 1.0 + (north + south + west + east)
    field = source_wide[:, depth : depth + rows, :]

    def sweep_group(group_index, current):
        wide = extended(current, (("lat", 1),), depth)
        wide = relax(wide, source_wide, north, south, west, east, denom, depth, depth)
        return wide

    field = lax.fori_loop(0, SWEEPS // depth, sweep_group, field)
    masked = field * sea_cells
    return jnp.einsum(
        "lm,mrc->lrc",
        balance,
        lax.all_to_all(masked, "lev", split_axis=1, concat_axis=0, tiled=True),
        precision=lax.Precision.HIGHEST,
    )


def solution(mesh):
    in_specs = (P("lev", "lat", "lon"), P("lev", "lat", "lon"), P(), P("member"), P("member"))
    out_specs = P("member", ("lat", "lev"), "lon")
    return jax.shard_map(
        per_device, mesh=mesh, in_specs=in_specs, out_specs=out_specs, check_vma=False
    )
```

profile of v0, /device:TPU:0, one launch (start us, length us, event | category | flops | bytes accessed | tf_op | source)
XLA Modules:
  0.0 1002.1 jit_solution(2599376986330560703)
XLA Ops:
  77.9 884.1 %while.10 = (s32[]{:T(128)}, f32[36,32,384]{0,1,2:T(8,128)}, f32[36,34,384]{0,1,2:T(8,128)}, f32[36,34,384]{0,1,2:T(8,128)}, f32[36,34,384]{0,1,2:T(8,128)}, /*i...) while((s32[]{:T(128)}, f32[36,32,384]{0,1,2:T(8,128)}, ...), condition=%wide.region_1.2_spmd, body=%wide.region_0.1_spmd.sunk | while | flops 6636290 | bytes 55251708 | solution.py:124
  108.3 7.1 copy.213
  136.6 8.0 slice_divide_fusion.2
  182.0 7.1 copy.213
  210.2 8.0 slice_divide_fusion.2
  255.7 7.1 copy.213
  283.9 8.0 slice_divide_fusion.2
  329.4 7.1 copy.213
  357.6 8.0 slice_divide_fusion.2
  403.1 7.1 copy.213
  431.3 8.0 slice_divide_fusion.2
  476.7 7.1 copy.213
  504.9 8.0 slice_divide_fusion.2
  550.4 7.1 copy.213
  578.6 8.0 slice_divide_fusion.2
  624.1 7.1 copy.213
  652.3 8.0 slice_divide_fusion.2
  697.8 7.1 copy.213
  726.0 8.0 slice_divide_fusion.2
  771.4 7.1 copy.213
  799.6 8.0 slice_divide_fusion.2
  873.3 8.0 slice_divide_fusion.2
  947.0 8.0 slice_divide_fusion.2
  971.7 26.2 %all_to_all.18 = f32[36,32,384]{2,0,1:T(8,128)S(1)} all-to-all(f32[36,32,384]{2,0,1:T(8,128)S(1)} %copy.191), channel_id=1, replica_groups=mesh['member'=2,'lat'=4,'lev'=2,'lon'=2] {'lev'}, dimensions={1} | all-to-all | bytes 3538944 | tf_op jit(solution)/shard_map/all_to_all | solution.py:129
  (302 shorter events, 807.5 us)
Async XLA Ops:
  78.6 57.9 %collective-permute-start.3 = (f32[36,32,1]{0,1,2:T(8,128)S(1)}, f32[36,32,1]{0,1,2:T(8,128)S(1)}, u32[]{:S(2)}, u32[]{:S(2)}) collective-permute-start(f32[36,32,1]{0,1,2:T(8,128)S(1)} %get-tuple-element.226), channel_id=1, source_target_pairs={{1,0},{0,1},{3,2},{2,3},{5,4},{4,5},{7,6},{6,7},{9,8},{8,9},{11,10... | collective-permute-start | bytes 13832 | tf_op jit(solution)/shard_map/while/body/eval_jaxpr/ppermute | solution.py:17
  78.7 57.8 %collective-permute-start.2 = (f32[36,32,1]{0,1,2:T(8,128)S(1)}, f32[36,32,1]{0,1,2:T(8,128)}, u32[]{:S(2)}, u32[]{:S(2)}) collective-permute-start(f32[36,32,1]{0,1,2:T(8,128)S(1)} %get-tuple-element.227), channel_id=1, source_target_pairs={{1,0},{0,1},{3,2},{2,3},{5,4},{4,5},{7,6},{6,7},{9,8},{8,9},{11,10... | collective-permute-start | bytes 13832 | tf_op jit(solution)/shard_map/while/body/eval_jaxpr/ppermute | solution.py:17
  152.3 57.9 %collective-permute-start.3 = (f32[36,32,1]{0,1,2:T(8,128)S(1)}, f32[36,32,1]{0,1,2:T(8,128)S(1)}, u32[]{:S(2)}, u32[]{:S(2)}) collective-permute-start(f32[36,32,1]{0,1,2:T(8,128)S(1)} %get-tuple-element.226), channel_id=1, source_target_pairs={{1,0},{0,1},{3,2},{2,3},{5,4},{4,5},{7,6},{6,7},{9,8},{8,9},{11,10... | collective-permute-start | bytes 13832 | tf_op jit(solution)/shard_map/while/body/eval_jaxpr/ppermute | solution.py:17
  152.3 57.9 %collective-permute-start.2 = (f32[36,32,1]{0,1,2:T(8,128)S(1)}, f32[36,32,1]{0,1,2:T(8,128)}, u32[]{:S(2)}, u32[]{:S(2)}) collective-permute-start(f32[36,32,1]{0,1,2:T(8,128)S(1)} %get-tuple-element.227), channel_id=1, source_target_pairs={{1,0},{0,1},{3,2},{2,3},{5,4},{4,5},{7,6},{6,7},{9,8},{8,9},{11,10... | collective-permute-start | bytes 13832 | tf_op jit(solution)/shard_map/while/body/eval_jaxpr/ppermute | solution.py:17
  226.0 57.9 %collective-permute-start.3 = (f32[36,32,1]{0,1,2:T(8,128)S(1)}, f32[36,32,1]{0,1,2:T(8,128)S(1)}, u32[]{:S(2)}, u32[]{:S(2)}) collective-permute-start(f32[36,32,1]{0,1,2:T(8,128)S(1)} %get-tuple-element.226), channel_id=1, source_target_pairs={{1,0},{0,1},{3,2},{2,3},{5,4},{4,5},{7,6},{6,7},{9,8},{8,9},{11,10... | collective-permute-start | bytes 13832 | tf_op jit(solution)/shard_map/while/body/eval_jaxpr/ppermute | solution.py:17
  226.0 57.9 %collective-permute-start.2 = (f32[36,32,1]{0,1,2:T(8,128)S(1)}, f32[36,32,1]{0,1,2:T(8,128)}, u32[]{:S(2)}, u32[]{:S(2)}) collective-permute-start(f32[36,32,1]{0,1,2:T(8,128)S(1)} %get-tuple-element.227), channel_id=1, source_target_pairs={{1,0},{0,1},{3,2},{2,3},{5,4},{4,5},{7,6},{6,7},{9,8},{8,9},{11,10... | collective-permute-start | bytes 13832 | tf_op jit(solution)/shard_map/while/body/eval_jaxpr/ppermute | solution.py:17
  299.7 57.9 %collective-permute-start.3 = (f32[36,32,1]{0,1,2:T(8,128)S(1)}, f32[36,32,1]{0,1,2:T(8,128)S(1)}, u32[]{:S(2)}, u32[]{:S(2)}) collective-permute-start(f32[36,32,1]{0,1,2:T(8,128)S(1)} %get-tuple-element.226), channel_id=1, source_target_pairs={{1,0},{0,1},{3,2},{2,3},{5,4},{4,5},{7,6},{6,7},{9,8},{8,9},{11,10... | collective-permute-start | bytes 13832 | tf_op jit(solution)/shard_map/while/body/eval_jaxpr/ppermute | solution.py:17
  299.7 57.9 %collective-permute-start.2 = (f32[36,32,1]{0,1,2:T(8,128)S(1)}, f32[36,32,1]{0,1,2:T(8,128)}, u32[]{:S(2)}, u32[]{:S(2)}) collective-permute-start(f32[36,32,1]{0,1,2:T(8,128)S(1)} %get-tuple-element.227), channel_id=1, source_target_pairs={{1,0},{0,1},{3,2},{2,3},{5,4},{4,5},{7,6},{6,7},{9,8},{8,9},{11,10... | collective-permute-start | bytes 13832 | tf_op jit(solution)/shard_map/while/body/eval_jaxpr/ppermute | solution.py:17
  373.3 57.9 %collective-permute-start.3 = (f32[36,32,1]{0,1,2:T(8,128)S(1)}, f32[36,32,1]{0,1,2:T(8,128)S(1)}, u32[]{:S(2)}, u32[]{:S(2)}) collective-permute-start(f32[36,32,1]{0,1,2:T(8,128)S(1)} %get-tuple-element.226), channel_id=1, source_target_pairs={{1,0},{0,1},{3,2},{2,3},{5,4},{4,5},{7,6},{6,7},{9,8},{8,9},{11,10... | collective-permute-start | bytes 13832 | tf_op jit(solution)/shard_map/while/body/eval_jaxpr/ppermute | solution.py:17
  373.3 57.9 %collective-permute-start.2 = (f32[36,32,1]{0,1,2:T(8,128)S(1)}, f32[36,32,1]{0,1,2:T(8,128)}, u32[]{:S(2)}, u32[]{:S(2)}) collective-permute-start(f32[36,32,1]{0,1,2:T(8,128)S(1)} %get-tuple-element.227), channel_id=1, source_target_pairs={{1,0},{0,1},{3,2},{2,3},{5,4},{4,5},{7,6},{6,7},{9,8},{8,9},{11,10... | collective-permute-start | bytes 13832 | tf_op jit(solution)/shard_map/while/body/eval_jaxpr/ppermute | solution.py:17
  447.0 57.9 %collective-permute-start.3 = (f32[36,32,1]{0,1,2:T(8,128)S(1)}, f32[36,32,1]{0,1,2:T(8,128)S(1)}, u32[]{:S(2)}, u32[]{:S(2)}) collective-permute-start(f32[36,32,1]{0,1,2:T(8,128)S(1)} %get-tuple-element.226), channel_id=1, source_target_pairs={{1,0},{0,1},{3,2},{2,3},{5,4},{4,5},{7,6},{6,7},{9,8},{8,9},{11,10... | collective-permute-start | bytes 13832 | tf_op jit(solution)/shard_map/while/body/eval_jaxpr/ppermute | solution.py:17
  447.0 57.9 %collective-permute-start.2 = (f32[36,32,1]{0,1,2:T(8,128)S(1)}, f32[36,32,1]{0,1,2:T(8,128)}, u32[]{:S(2)}, u32[]{:S(2)}) collective-permute-start(f32[36,32,1]{0,1,2:T(8,128)S(1)} %get-tuple-element.227), channel_id=1, source_target_pairs={{1,0},{0,1},{3,2},{2,3},{5,4},{4,5},{7,6},{6,7},{9,8},{8,9},{11,10... | collective-permute-start | bytes 13832 | tf_op jit(solution)/shard_map/while/body/eval_jaxpr/ppermute | solution.py:17
  520.7 57.9 %collective-permute-start.3 = (f32[36,32,1]{0,1,2:T(8,128)S(1)}, f32[36,32,1]{0,1,2:T(8,128)S(1)}, u32[]{:S(2)}, u32[]{:S(2)}) collective-permute-start(f32[36,32,1]{0,1,2:T(8,128)S(1)} %get-tuple-element.226), channel_id=1, source_target_pairs={{1,0},{0,1},{3,2},{2,3},{5,4},{4,5},{7,6},{6,7},{9,8},{8,9},{11,10... | collective-permute-start | bytes 13832 | tf_op jit(solution)/shard_map/while/body/eval_jaxpr/ppermute | solution.py:17
  520.7 57.9 %collective-permute-start.2 = (f32[36,32,1]{0,1,2:T(8,128)S(1)}, f32[36,32,1]{0,1,2:T(8,128)}, u32[]{:S(2)}, u32[]{:S(2)}) collective-permute-start(f32[36,32,1]{0,1,2:T(8,128)S(1)} %get-tuple-element.227), channel_id=1, source_target_pairs={{1,0},{0,1},{3,2},{2,3},{5,4},{4,5},{7,6},{6,7},{9,8},{8,9},{11,10... | collective-permute-start | bytes 13832 | tf_op jit(solution)/shard_map/while/body/eval_jaxpr/ppermute | solution.py:17
  594.4 57.9 %collective-permute-start.3 = (f32[36,32,1]{0,1,2:T(8,128)S(1)}, f32[36,32,1]{0,1,2:T(8,128)S(1)}, u32[]{:S(2)}, u32[]{:S(2)}) collective-permute-start(f32[36,32,1]{0,1,2:T(8,128)S(1)} %get-tuple-element.226), channel_id=1, source_target_pairs={{1,0},{0,1},{3,2},{2,3},{5,4},{4,5},{7,6},{6,7},{9,8},{8,9},{11,10... | collective-permute-start | bytes 13832 | tf_op jit(solution)/shard_map/while/body/eval_jaxpr/ppermute | solution.py:17
  594.4 57.9 %collective-permute-start.2 = (f32[36,32,1]{0,1,2:T(8,128)S(1)}, f32[36,32,1]{0,1,2:T(8,128)}, u32[]{:S(2)}, u32[]{:S(2)}) collective-permute-start(f32[36,32,1]{0,1,2:T(8,128)S(1)} %get-tuple-element.227), channel_id=1, source_target_pairs={{1,0},{0,1},{3,2},{2,3},{5,4},{4,5},{7,6},{6,7},{9,8},{8,9},{11,10... | collective-permute-start | bytes 13832 | tf_op jit(solution)/shard_map/while/body/eval_jaxpr/ppermute | solution.py:17
  668.0 57.9 %collective-permute-start.3 = (f32[36,32,1]{0,1,2:T(8,128)S(1)}, f32[36,32,1]{0,1,2:T(8,128)S(1)}, u32[]{:S(2)}, u32[]{:S(2)}) collective-permute-start(f32[36,32,1]{0,1,2:T(8,128)S(1)} %get-tuple-element.226), channel_id=1, source_target_pairs={{1,0},{0,1},{3,2},{2,3},{5,4},{4,5},{7,6},{6,7},{9,8},{8,9},{11,10... | collective-permute-start | bytes 13832 | tf_op jit(solution)/shard_map/while/body/eval_jaxpr/ppermute | solution.py:17
  668.0 57.9 %collective-permute-start.2 = (f32[36,32,1]{0,1,2:T(8,128)S(1)}, f32[36,32,1]{0,1,2:T(8,128)}, u32[]{:S(2)}, u32[]{:S(2)}) collective-permute-start(f32[36,32,1]{0,1,2:T(8,128)S(1)} %get-tuple-element.227), channel_id=1, source_target_pairs={{1,0},{0,1},{3,2},{2,3},{5,4},{4,5},{7,6},{6,7},{9,8},{8,9},{11,10... | collective-permute-start | bytes 13832 | tf_op jit(solution)/shard_map/while/body/eval_jaxpr/ppermute | solution.py:17
  741.7 57.9 %collective-permute-start.3 = (f32[36,32,1]{0,1,2:T(8,128)S(1)}, f32[36,32,1]{0,1,2:T(8,128)S(1)}, u32[]{:S(2)}, u32[]{:S(2)}) collective-permute-start(f32[36,32,1]{0,1,2:T(8,128)S(1)} %get-tuple-element.226), channel_id=1, source_target_pairs={{1,0},{0,1},{3,2},{2,3},{5,4},{4,5},{7,6},{6,7},{9,8},{8,9},{11,10... | collective-permute-start | bytes 13832 | tf_op jit(solution)/shard_map/while/body/eval_jaxpr/ppermute | solution.py:17
  741.7 57.9 %collective-permute-start.2 = (f32[36,32,1]{0,1,2:T(8,128)S(1)}, f32[36,32,1]{0,1,2:T(8,128)}, u32[]{:S(2)}, u32[]{:S(2)}) collective-permute-start(f32[36,32,1]{0,1,2:T(8,128)S(1)} %get-tuple-element.227), channel_id=1, source_target_pairs={{1,0},{0,1},{3,2},{2,3},{5,4},{4,5},{7,6},{6,7},{9,8},{8,9},{11,10... | collective-permute-start | bytes 13832 | tf_op jit(solution)/shard_map/while/body/eval_jaxpr/ppermute | solution.py:17
  815.4 57.9 %collective-permute-start.3 = (f32[36,32,1]{0,1,2:T(8,128)S(1)}, f32[36,32,1]{0,1,2:T(8,128)S(1)}, u32[]{:S(2)}, u32[]{:S(2)}) collective-permute-start(f32[36,32,1]{0,1,2:T(8,128)S(1)} %get-tuple-element.226), channel_id=1, source_target_pairs={{1,0},{0,1},{3,2},{2,3},{5,4},{4,5},{7,6},{6,7},{9,8},{8,9},{11,10... | collective-permute-start | bytes 13832 | tf_op jit(solution)/shard_map/while/body/eval_jaxpr/ppermute | solution.py:17
  815.4 57.9 %collective-permute-start.2 = (f32[36,32,1]{0,1,2:T(8,128)S(1)}, f32[36,32,1]{0,1,2:T(8,128)}, u32[]{:S(2)}, u32[]{:S(2)}) collective-permute-start(f32[36,32,1]{0,1,2:T(8,128)S(1)} %get-tuple-element.227), channel_id=1, source_target_pairs={{1,0},{0,1},{3,2},{2,3},{5,4},{4,5},{7,6},{6,7},{9,8},{8,9},{11,10... | collective-permute-start | bytes 13832 | tf_op jit(solution)/shard_map/while/body/eval_jaxpr/ppermute | solution.py:17
  889.1 57.9 %collective-permute-start.3 = (f32[36,32,1]{0,1,2:T(8,128)S(1)}, f32[36,32,1]{0,1,2:T(8,128)S(1)}, u32[]{:S(2)}, u32[]{:S(2)}) collective-permute-start(f32[36,32,1]{0,1,2:T(8,128)S(1)} %get-tuple-element.226), channel_id=1, source_target_pairs={{1,0},{0,1},{3,2},{2,3},{5,4},{4,5},{7,6},{6,7},{9,8},{8,9},{11,10... | collective-permute-start | bytes 13832 | tf_op jit(solution)/shard_map/while/body/eval_jaxpr/ppermute | solution.py:17
  889.1 57.9 %collective-permute-start.2 = (f32[36,32,1]{0,1,2:T(8,128)S(1)}, f32[36,32,1]{0,1,2:T(8,128)}, u32[]{:S(2)}, u32[]{:S(2)}) collective-permute-start(f32[36,32,1]{0,1,2:T(8,128)S(1)} %get-tuple-element.227), channel_id=1, source_target_pairs={{1,0},{0,1},{3,2},{2,3},{5,4},{4,5},{7,6},{6,7},{9,8},{8,9},{11,10... | collective-permute-start | bytes 13832 | tf_op jit(solution)/shard_map/while/body/eval_jaxpr/ppermute | solution.py:17
  (33 other events, 2318.9 us)
where the time goes:
time: 1010 us; the launch traced here: 1000 us
  local copies, waits for them, and re-layouts  774 us (77%)
  other arithmetic  114 us (11%)
  starting transfers between devices  83.5 us (8%)
  blocking collectives  26.2 us (3%)
    another operation x96, local copies, waits for them, and re-layouts  656 us
    div x12, other arithmetic, relax(): (source[:, lower:upper] + north[:, lower:upper] * field[:, :-2, :] + sout...  95.8 us
    ppermute x13, starting transfers between devices, extended(): lax.ppermute(tail, axis, [(i, (i + 1) % count) for i in range(ends)])  60.2 us
    while x8, local copies, waits for them, and re-layouts, per_device(): field = lax.fori_loop(0, SWEEPS // depth, sweep_group, field)  51.1 us
    slice x12, local copies, waits for them, and re-layouts, with_edges(): jnp.roll(values, -1, axis=2)  30.8 us
    all_to_all x1, blocking collectives, per_device(): lax.all_to_all(masked, 'lev', split_axis=1, concat_axis=0, tiled=True)  26.2 us
  transfers between devices with their start and end apart: 52, of which 0 were waited for; matrix products, arithmetic and copies ran while one was open for 65% of the time, Pallas kernels for 0%

commit v1 on v0

v1 whole, which is shorter than its diff:
```python
import functools
import math

import jax
import jax.numpy as jnp
from jax import lax
from jax.experimental import pallas as pl
from jax.experimental.pallas import tpu as pltpu
from jax.sharding import PartitionSpec as P

SWEEPS = 12
noise_scale = math.sqrt(3.0) / 65536.0
LANES, SUB = 128, 8

def scramble(values):
    values = values * 1103515245 + 12345
    values = values ^ (values >> 15)
    values = values * 747796405 + 1013904223
    values = values ^ (values >> 13)
    values = values * 277803737
    return values ^ (values >> 16)

def draw(index, stream_base):
    first = scramble(index ^ stream_base)
    second = scramble(first + 1664525)
    total = ((first & 65535) + ((first >> 16) & 65535) + (second & 65535) + ((second >> 16) & 65535) - 131070)
    return total.astype(jnp.float32) * noise_scale

def noise_kernel(total_rows, total_cols, pitch, ids, out):
    levels, tiles = out.shape[0], out.shape[1]
    base, level0, row0 = ids[0], ids[1], ids[2]
    sub = lax.broadcasted_iota(jnp.int32, (SUB, LANES), 0)
    lane = lax.broadcasted_iota(jnp.int32, (SUB, LANES), 1)
    within = sub * (pitch * total_cols) + lane
    @pl.loop(0, levels)
    def _(l):
        start = ((level0 + l) * total_rows + row0) * total_cols
        for t in range(tiles):
            for k in range(pitch):
                out[l, t, k] = draw(within + (start + k * total_cols + t * LANES), base)

def neighbours(get, tiles, pitch, t, lane):
    here = [get(t, k) for k in range(pitch)]
    wt, et = (t - 1) % tiles, (t + 1) % tiles
    up = pltpu.roll(here[pitch - 1], 1, 0)
    down = pltpu.roll(here[0], SUB - 1, 0)
    sums = []
    for k in range(pitch):
        w = pltpu.roll(jnp.where(lane == LANES - 1, get(wt, k), here[k]), 1, 1)
        e = pltpu.roll(jnp.where(lane == 0, get(et, k), here[k]), LANES - 1, 1)
        n = here[k - 1] if k else up
        s = here[k + 1] if k < pitch - 1 else down
        sums.append((w + e) + (n + s))
    return here, sums

def diffuse_kernel(halo, own, top, bottom, source, out, rows, cond, gain, push, inv, u0, u1, res):
    tiles, pitch = source.shape[1], source.shape[2]
    height = own.shape[1]
    lane = lax.broadcasted_iota(jnp.int32, (SUB, LANES), 1)
    for t in range(tiles):
        cols = slice(t * LANES, (t + 1) * LANES)
        rows[t, pl.ds(0, halo), :] = top[0, :, cols]
        rows[t, pl.ds(halo, height), :] = own[0, :, cols]
        rows[t, pl.ds(halo + height, halo), :] = bottom[0, :, cols]
    for t in range(tiles):
        for k in range(pitch):
            cond[t, k] = rows[t, pl.ds(k, SUB, stride=pitch), :]
    for t in range(tiles):
        here, sums = neighbours(lambda a, b: cond[a, b], tiles, pitch, t, lane)
        for k in range(pitch):
            c, s = here[k], source[0, t, k]
            r = 1.0 / (1.0 + c * sums[k])
            q = c * r
            inv[t, k] = r
            push[t, k] = q * s
            gain[t, k] = q * c
            u0[t, k] = c * s
    def sweep(old, new):
        for t in range(tiles):
            _, sums = neighbours(lambda a, b: old[a, b], tiles, pitch, t, lane)
            for k in range(pitch):
                new[t, k] = push[t, k] + gain[t, k] * sums[k]
    @pl.loop(0, (SWEEPS - 2) // 2)
    def _(i):
        sweep(u0, u1)
        sweep(u1, u0)
    sweep(u0, u1)
    for t in range(tiles):
        _, sums = neighbours(lambda a, b: u1[a, b], tiles, pitch, t, lane)
        for k in range(pitch):
            c, s = cond[t, k], source[0, t, k]
            res[t, pl.ds(k, SUB, stride=pitch), :] = jnp.where(c != 0.0, (s + c * sums[k]) * inv[t, k], 0.0)
    for t in range(tiles):
        out[0, t] = res[t, pl.ds(halo, height), :]

def noise(ids, levels, tiles, pitch, total_rows, total_cols):
    return pl.pallas_call(
        functools.partial(noise_kernel, total_rows, total_cols, pitch),
        out_shape=jax.ShapeDtypeStruct((levels, tiles, pitch, SUB, LANES), jnp.float32),
        in_specs=[pl.BlockSpec(memory_space=pltpu.SMEM)],
        out_specs=pl.BlockSpec(memory_space=pltpu.VMEM),
    )(ids)

def diffuse(own, top, bottom, source):
    levels, height, width = own.shape
    halo = top.shape[1]
    tiles, pitch = source.shape[1:3]
    tile = pltpu.VMEM((tiles, pitch, SUB, LANES), jnp.float32)
    line = pltpu.VMEM((tiles, pitch * SUB, LANES), jnp.float32)
    return pl.pallas_call(
        functools.partial(diffuse_kernel, halo),
        out_shape=jax.ShapeDtypeStruct((levels, tiles, height, LANES), jnp.float32),
        grid=(levels,),
        in_specs=[pl.BlockSpec((1, height, width), lambda l: (l, 0, 0)),
                  pl.BlockSpec((1, halo, width), lambda l: (l, 0, 0)),
                  pl.BlockSpec((1, halo, width), lambda l: (l, 0, 0)),
                  pl.BlockSpec((1, tiles, pitch, SUB, LANES), lambda l: (l, 0, 0, 0, 0))],
        out_specs=pl.BlockSpec((1, tiles, height, LANES), lambda l: (l, 0, 0, 0)),
        scratch_shapes=[line] + [tile] * 6 + [line],
    )(own, top, bottom, source)


def balance_kernel(weights, own, other, out, columns, result):
    total, tiles, height = weights.shape[0], own.shape[1], own.shape[2]
    near, pitch = own.shape[0], tiles * height
    columns[0 : near * pitch, :] = own[...].reshape(near * pitch, LANES)
    columns[near * pitch :, :] = other[...].reshape(other.shape[0] * pitch, LANES)
    left = weights[...]
    high = left.astype(jnp.bfloat16)
    low = (left - high.astype(jnp.float32)).astype(jnp.bfloat16)
    stacked = jnp.concatenate([high, high, low], axis=1)
    for r in range(height):
        for t in range(tiles):
            column = columns[pl.ds(t * height + r, total, stride=pitch), :]
            top = column.astype(jnp.bfloat16)
            rest = (column - top.astype(jnp.float32)).astype(jnp.bfloat16)
            right = jnp.concatenate([top, rest, top], axis=0)
            result[pl.ds(t * height + r, total, stride=pitch), :] = jnp.dot(
                stacked, right, preferred_element_type=jnp.float32
            )
    for t in range(tiles):
        for l in range(total):
            start = l * pitch + t * height
            out[l, :, t * LANES : (t + 1) * LANES] = result[start : start + height, :]


def balanced(weights, own, other):
    tiles, height = own.shape[1:3]
    total = weights.shape[0]
    flat = pltpu.VMEM((total * tiles * height, LANES), jnp.float32)
    return pl.pallas_call(
        balance_kernel,
        out_shape=jax.ShapeDtypeStruct((total, height, tiles * LANES), jnp.float32),
        in_specs=[pl.BlockSpec(memory_space=pltpu.VMEM)] * 3,
        out_specs=pl.BlockSpec(memory_space=pltpu.VMEM),
        scratch_shapes=[flat, flat],
        compiler_params=pltpu.CompilerParams(vmem_limit_bytes=48 << 20),
    )(weights, own, other)


def swapped(keep, send, axis):
    count = lax.axis_size(axis)
    return keep, lax.ppermute(send, axis, [(i, count - 1 - i) for i in range(count)])


def part(block, index, size, axis):
    return lax.dynamic_slice_in_dim(block, index * size, size, axis=axis)


def per_device(land_mask, diffusivity, balance, member_id, counter_key):
    levels, height, breadth = land_mask.shape
    cores, groups, strips = (lax.axis_size(a) for a in ("lon", "lev", "lat"))
    core, group, strip = (lax.axis_index(a) for a in ("lon", "lev", "lat"))
    assert cores == 2 and height > SWEEPS
    halo = SWEEPS
    pitch = (height + 2 * halo) // SUB
    share = -(-levels // cores)
    conduct = diffusivity * land_mask.astype(jnp.float32)
    conduct = jnp.pad(conduct, ((0, share * cores - levels), (0, 0), (0, 0)))
    mine, theirs = swapped(part(conduct, core, share, 0), part(conduct, 1 - core, share, 0), "lon")
    own = jnp.concatenate([jnp.where(core == 0, mine, theirs), jnp.where(core == 0, theirs, mine)], axis=2)
    onward = [(i, i + 1) for i in range(strips - 1)]
    top = lax.ppermute(own[:, -halo:], "lat", onward)
    bottom = lax.ppermute(own[:, :halo], "lat", [(b, a) for a, b in onward])
    base = counter_key[0] * 69069 + member_id[0] * 362437
    ids = jnp.stack([base, group * levels + core * share, strip * height - halo])
    tiles = breadth * cores // LANES
    source = noise(ids, share, tiles, pitch, height * strips, breadth * cores)
    masked = diffuse(own, top, bottom, source)
    mine, theirs = swapped(part(masked, core, tiles // cores, 1), part(masked, 1 - core, tiles // cores, 1), "lon")
    column = jnp.concatenate([jnp.where(core == 0, mine, theirs), jnp.where(core == 0, theirs, mine)], axis=0)
    column = column[:levels]
    final = height // groups
    if groups == 2:
        near, far = swapped(part(column, group, final, 2), part(column, 1 - group, final, 2), "lev")
        weights = jnp.concatenate([part(balance, group, levels, 1), part(balance, 1 - group, levels, 1)], axis=1)
    else:
        near = lax.all_to_all(column, "lev", split_axis=2, concat_axis=0, tiled=True)
        near, far = near[: levels * groups // 2], near[levels * groups // 2 :]
        weights = balance
    return balanced(weights, near, far)


def solution(mesh):
    in_specs = (P("lev", "lat", "lon"), P("lev", "lat", "lon"), P(), P("member"), P("member"))
    out_specs = P("member", ("lat", "lev"), "lon")
    return jax.shard_map(
        per_device, mesh=mesh, in_specs=in_specs, out_specs=out_specs, check_vma=False
    )
```

time: 1010 us -> 104 us (0.10)
  local copies, waits for them, and re-layouts: 774 us -> 1.51 us
  other arithmetic: 114 us -> 6.21 us
  starting transfers between devices: 83.5 us -> 9.23 us
  Pallas kernels: 0 us -> 47.8 us
  waiting for transfers between devices: 0.14 us -> 37.4 us
  blocking collectives: 26.2 us -> 0 us
    another operation x96 -> x0, local copies, waits for them, and re-layouts: 656 us -> none
    div x12 -> x0, other arithmetic: 95.8 us -> none  [relax(): (source[:, lower:upper] + north[:, lower:upper] * field[:, :-2, :] + sout...]
    ppermute x52 -> x5, starting transfers between devices: 83.5 us -> 9.23 us  [the longest x1 5.8 us: per_device(): top = lax.ppermute(own[:, -halo:], 'lat', onward)]
    slice x66 -> x0, local copies, waits for them, and re-layouts: 62.9 us -> none  [the longest x12 30.8 us: with_edges(): jnp.roll(values, -1, axis=2)]
    while x8 -> x0, local copies, waits for them, and re-layouts: 51.1 us -> none  [per_device(): field = lax.fori_loop(0, SWEEPS // depth, sweep_group, field)]
    pallas_call x0 -> x3, Pallas kernels: none -> 47.8 us  [the longest x1 38.8 us: diffuse(): pl.pallas_call(functools.partial(diffuse_kernel, halo), out_shape=jax.Sha...]
    ppermute x52 -> x5, waiting for transfers between devices: 0.14 us -> 37.4 us  [the longest x3 24.6 us: swapped(): lax.ppermute(send, axis, [(i, count - 1 - i) for i in range(count)])]
    all_to_all x1 -> x0, blocking collectives: 26.2 us -> none  [per_device(): lax.all_to_all(masked, 'lev', split_axis=1, concat_axis=0, tiled=True)]
  transfers between devices with their start and end apart: 52 -> 5, of which waited for: 0 -> 5; matrix products, arithmetic and copies ran while one was open for 65% -> 2% of each run, Pallas kernels for 0% -> 6%
where the time goes in v1:
time: 104 us
  Pallas kernels  47.8 us (46%)
  waiting for transfers between devices  37.4 us (36%)
  starting transfers between devices  9.23 us (9%)
  other arithmetic  6.21 us (6%)
  local copies, waits for them, and re-layouts  1.51 us (1%)
  between operations  1.4 us (1%)
    pallas_call x1, Pallas kernels, diffuse(): pl.pallas_call(functools.partial(diffuse_kernel, halo), out_shape=jax.Sha...  38.8 us
    ppermute x3, waiting for transfers between devices, swapped(): lax.ppermute(send, axis, [(i, count - 1 - i) for i in range(count)])  24.6 us
    ppermute x1, waiting for transfers between devices, per_device(): top = lax.ppermute(own[:, -halo:], 'lat', onward)  7.6 us
    pallas_call x1, Pallas kernels, noise(): pl.pallas_call(functools.partial(noise_kernel, total_rows, total_cols, pi...  6.1 us
    ppermute x1, starting transfers between devices, per_device(): top = lax.ppermute(own[:, -halo:], 'lat', onward)  5.8 us
    ppermute x1, waiting for transfers between devices, per_device(): bottom = lax.ppermute(own[:, :halo], 'lat', [(b, a) for a, b in onward])  5.15 us
    pallas_call x1, Pallas kernels, balanced(): pl.pallas_call(balance_kernel, out_shape=jax.ShapeDtypeStruct((total, hei...  2.96 us
    mul x1, other arithmetic, per_device(): conduct = diffusivity * land_mask.astype(jnp.float32)  2.31 us
  transfers between devices with their start and end apart: 5, of which 5 were waited for; matrix products, arithmetic and copies ran while one was open for 2% of the time, Pallas kernels for 6%

profile of v1, /device:TPU:0, one launch (start us, length us, event | category | flops | bytes accessed | tf_op | source)
XLA Modules:
  0.0 103.6 jit_solution(16774462894741320910)
XLA Ops:
  0.0 2.3 %convert_multiply_fusion = f32[36,32,384]{2,1,0:T(8,128)S(1)} fusion(f32[36,32,384]{2,1,0:T(8,128)} %param.6, s32[36,32,384]{2,1,0:T(8,128)} %param.5), kind=kLoop, calls=%fused_computation.9 | loop fusion | flops 884736 | bytes 5308416 | tf_op jit(solution)/shard_map/mul | solution.py:178
  2.3 0.1 constant_dynamic-slice_fusion.1
  2.4 0.5 collective-permute-start
  2.9 2.2 %collective-permute-done = f32[18,32,384]{2,1,0:T(8,128)} collective-permute-done((f32[18,32,384]{2,1,0:T(8,128)S(1)}, f32[18,32,384]{2,1,0:T(8,128)}, u32[]{:S(2)}, u32[]{:S(2)}) %collective-permute-start) | collective-permute-done | bytes 884768 | tf_op jit(solution)/shard_map/ppermute | solution.py:163
  5.1 1.3 %dynamic-slice_select_fusion.3 = (f32[18,32,384]{2,1,0:T(8,128)S(1)}, f32[18,32,384]{2,1,0:T(8,128)S(1)}) fusion(f32[18,32,384]{2,1,0:T(8,128)} %collective-permute-done, f32[36,32,384]{2,1,0:T(8,128)S(1)} %convert_multiply_fusion, s32[]{:T(128)S(6)} %select_n.52, pred[]{:T(512)S(6)} %eq.2), kind=kLoop, calls=%fused_computation.17 | loop fusion | flops 442368 | bytes 3538949 | tf_op jit(solution)/shard_map/jit(_where)/select_n | solution.py:181
  6.4 0.2 fusion.3
  6.6 5.8 %collective-permute-start.1 = (f32[18,12,768]{2,1,0:T(8,128)S(1)}, f32[18,12,768]{2,1,0:T(8,128)}, u32[]{:S(2)}, u32[]{:S(2)}) collective-permute-start(f32[18,12,768]{2,1,0:T(8,128)S(1)} %get-tuple-element.12), channel_id=1, source_target_pairs={{0,4},{4,8},{8,12},{1,5},{5,9},{9,13},{2,6},{6,10},{10,14},{3,7},{... | collective-permute-start | bytes 1990664 | tf_op jit(solution)/shard_map/ppermute | solution.py:183
  12.4 1.3 %collective-permute-start.2 = (f32[18,12,768]{2,1,0:T(8,128)S(1)}, f32[18,12,768]{2,1,0:T(8,128)}, u32[]{:S(2)}, u32[]{:S(2)}) collective-permute-start(f32[18,12,768]{2,1,0:T(8,128)S(1)} %get-tuple-element.11), channel_id=1, source_target_pairs={{4,0},{8,4},{12,8},{5,1},{9,5},{13,9},{6,2},{10,6},{14,10},{7,3},{... | collective-permute-start | bytes 1990664 | tf_op jit(solution)/shard_map/ppermute | solution.py:184
  15.0 0.6 pad_add_fusion.ids
  15.6 6.1 %shard_map.55.source = f32[18,6,7,8,128]{4,3,2,1,0:T(8,128)} custom-call(s32[3]{0:T(128)} %pad_add_fusion.ids), custom_call_target="tpu_custom_call" | custom-call | tf_op jit(solution)/shard_map/pallas_call | solution.py:97
  21.7 1.3 %pad_maximum_fusion.own = f32[18,32,768]{2,1,0:T(8,128)} fusion(f32[18,32,384]{2,1,0:T(8,128)S(1)} %get-tuple-element.8, f32[18,32,384]{2,1,0:T(8,128)S(1)} %get-tuple-element.7), kind=kLoop, calls=%fused_computation.2 | loop fusion | flops 442368 | bytes 3538944 | tf_op jit(solution)/shard_map/concatenate | solution.py:181
  23.0 7.6 %collective-permute-done.1.top = f32[18,12,768]{2,1,0:T(8,128)} collective-permute-done((f32[18,12,768]{2,1,0:T(8,128)S(1)}, f32[18,12,768]{2,1,0:T(8,128)}, u32[]{:S(2)}, u32[]{:S(2)}) %collective-permute-start.1) | collective-permute-done | bytes 663584 | tf_op jit(solution)/shard_map/ppermute | solution.py:183
  30.6 5.2 %collective-permute-done.2.bottom = f32[18,12,768]{2,1,0:T(8,128)} collective-permute-done((f32[18,12,768]{2,1,0:T(8,128)S(1)}, f32[18,12,768]{2,1,0:T(8,128)}, u32[]{:S(2)}, u32[]{:S(2)}) %collective-permute-start.2) | collective-permute-done | bytes 663584 | tf_op jit(solution)/shard_map/ppermute | solution.py:184
  35.8 38.8 %shard_map.56 = f32[18,6,32,128]{3,2,1,0:T(8,128)} custom-call(f32[18,32,768]{2,1,0:T(8,128)} %pad_maximum_fusion.own, f32[18,12,768]{2,1,0:T(8,128)} %collective-permute-done.1.top, f32[18,12,768]{2,1,0:T(8,128)} %collective-permute-done.2.bottom, f32[18,6,7,8,128]{4,3,2,1,0:T(8,128)} %shard_map.55.source), custom_call_target="tpu_custom_call" | custom-call | tf_op jit(solution)/shard_map/pallas_call | solution.py:110
  74.6 1.4 %constant_dynamic-slice_fusion = f32[18,3,32,128]{3,2,1,0:T(8,128)S(1)} fusion(f32[18,6,32,128]{3,2,1,0:T(8,128)} %shard_map.56, s32[]{:T(128)S(6)} %select_n.57), kind=kLoop, calls=%fused_computation.19 | loop fusion | bytes 1769476 | tf_op jit(solution)/shard_map/dynamic_slice | solution.py:167
  75.9 0.1 collective-permute-start.3
  76.0 2.4 %collective-permute-done.3 = f32[18,3,32,128]{3,2,1,0:T(8,128)S(1)} collective-permute-done((f32[18,3,32,128]{3,2,1,0:T(8,128)S(1)}, f32[18,3,32,128]{3,2,1,0:T(8,128)S(1)}, u32[]{:S(2)}, u32[]{:S(2)}) %collective-permute-start.3) | collective-permute-done | bytes 884768 | tf_op jit(solution)/shard_map/ppermute | solution.py:163
  78.4 0.2 dynamic-slice_select_fusion
  78.6 0.2 fusion
  78.9 1.6 %collective-permute-start.4 = (f32[36,3,16,128]{3,2,1,0:T(8,128)S(1)}, f32[36,3,16,128]{3,2,1,0:T(8,128)S(1)}, u32[]{:S(2)}, u32[]{:S(2)}) collective-permute-start(f32[36,3,16,128]{3,2,1,0:T(8,128)S(1)} %get-tuple-element.9), channel_id=1, source_target_pairs={{0,2},{2,0},{1,3},{3,1},{4,6},{6,4},{5,7},{7,5},{8,10},{10,8},{9,1... | collective-permute-start | bytes 2654216 | tf_op jit(solution)/shard_map/ppermute | solution.py:163
  80.4 0.1 constant_dynamic-slice_fusion.3
  80.5 0.1 pad_maximum_fusion.1.weights
  80.6 20.0 %collective-permute-done.4.other = f32[36,3,16,128]{3,2,1,0:T(8,128)S(1)} collective-permute-done((f32[36,3,16,128]{3,2,1,0:T(8,128)S(1)}, f32[36,3,16,128]{3,2,1,0:T(8,128)S(1)}, u32[]{:S(2)}, u32[]{:S(2)}) %collective-permute-start.4) | collective-permute-done | bytes 884768 | tf_op jit(solution)/shard_map/ppermute | solution.py:163
  100.6 3.0 %shard_map.57 = f32[72,16,384]{2,1,0:T(8,128)} custom-call(f32[72,72]{1,0:T(8,128)S(1)} %pad_maximum_fusion.1.weights, f32[36,3,16,128]{3,2,1,0:T(8,128)S(1)} %get-tuple-element.10.own, f32[36,3,16,128]{3,2,1,0:T(8,128)S(1)} %collective-permute-done.4.other), custom_call_target="tpu_custom_call" | custom-call | tf_op jit(solution)/shard_map/pallas_call | solution.py:151
  (4 shorter events, 0.0 us)
Async XLA Ops:
  2.4 2.7 %collective-permute-start = (f32[18,32,384]{2,1,0:T(8,128)S(1)}, f32[18,32,384]{2,1,0:T(8,128)}, u32[]{:S(2)}, u32[]{:S(2)}) collective-permute-start(f32[18,32,384]{2,1,0:T(8,128)S(1)} %constant_dynamic-slice_fusion.1), channel_id=1, source_target_pairs={{0,1},{1,0},{2,3},{3,2},{4,5},{5,4},{6,7},{7,6},{8,9},{9,8},{10,11... | collective-permute-start | bytes 2654216 | tf_op jit(solution)/shard_map/ppermute | solution.py:163
  6.6 24.0 %collective-permute-start.1 = (f32[18,12,768]{2,1,0:T(8,128)S(1)}, f32[18,12,768]{2,1,0:T(8,128)}, u32[]{:S(2)}, u32[]{:S(2)}) collective-permute-start(f32[18,12,768]{2,1,0:T(8,128)S(1)} %get-tuple-element.12), channel_id=1, source_target_pairs={{0,4},{4,8},{8,12},{1,5},{5,9},{9,13},{2,6},{6,10},{10,14},{3,7},{... | collective-permute-start | bytes 1990664 | tf_op jit(solution)/shard_map/ppermute | solution.py:183
  12.4 23.4 %collective-permute-start.2 = (f32[18,12,768]{2,1,0:T(8,128)S(1)}, f32[18,12,768]{2,1,0:T(8,128)}, u32[]{:S(2)}, u32[]{:S(2)}) collective-permute-start(f32[18,12,768]{2,1,0:T(8,128)S(1)} %get-tuple-element.11), channel_id=1, source_target_pairs={{4,0},{8,4},{12,8},{5,1},{9,5},{13,9},{6,2},{10,6},{14,10},{7,3},{... | collective-permute-start | bytes 1990664 | tf_op jit(solution)/shard_map/ppermute | solution.py:184
  74.6 3.9 %copy-start = (f32[18,6,32,128]{3,2,1,0:T(8,128)S(1)}, f32[18,6,32,128]{3,2,1,0:T(8,128)}, u32[]{:S(2)}) copy-start(f32[18,6,32,128]{3,2,1,0:T(8,128)} %shard_map.56) | copy-start | bytes 5308420
  75.9 2.5 %collective-permute-start.3 = (f32[18,3,32,128]{3,2,1,0:T(8,128)S(1)}, f32[18,3,32,128]{3,2,1,0:T(8,128)S(1)}, u32[]{:S(2)}, u32[]{:S(2)}) collective-permute-start(f32[18,3,32,128]{3,2,1,0:T(8,128)S(1)} %constant_dynamic-slice_fusion), channel_id=1, source_target_pairs={{0,1},{1,0},{2,3},{3,2},{4,5},{5,4},{6,7},{7,6},{8,9},{9,8},{10,11... | collective-permute-start | bytes 2654216 | tf_op jit(solution)/shard_map/ppermute | solution.py:163
  78.6 1.8 %copy-start.1 = (f32[72,72]{1,0:T(8,128)S(1)}, f32[72,72]{1,0:T(8,128)}, u32[]{:S(2)}) copy-start(f32[72,72]{1,0:T(8,128)} %param.7) | copy-start | bytes 62212
  78.9 21.8 %collective-permute-start.4 = (f32[36,3,16,128]{3,2,1,0:T(8,128)S(1)}, f32[36,3,16,128]{3,2,1,0:T(8,128)S(1)}, u32[]{:S(2)}, u32[]{:S(2)}) collective-permute-start(f32[36,3,16,128]{3,2,1,0:T(8,128)S(1)} %get-tuple-element.9), channel_id=1, source_target_pairs={{0,2},{2,0},{1,3},{3,1},{4,6},{6,4},{5,7},{7,5},{8,10},{10,8},{9,1... | collective-permute-start | bytes 2654216 | tf_op jit(solution)/shard_map/ppermute | solution.py:163

commit v2 on v1

v2 whole, which is shorter than its diff:
```python
import functools
import math

import jax
import jax.numpy as jnp
from jax import lax
from jax.experimental import pallas as pl
from jax.experimental.pallas import tpu as pltpu
from jax.sharding import PartitionSpec as P

SWEEPS = 12
noise_scale = math.sqrt(3.0) / 65536.0
LANES, SUB = 128, 8
HALF = LANES // 2
VMEM = pltpu.VMEM
whole = functools.partial(pl.BlockSpec, memory_space=pltpu.VMEM)
scalars = functools.partial(pl.BlockSpec, memory_space=pltpu.SMEM)


def scramble(values):
    values = values * 1103515245 + 12345
    values = values ^ (values >> 15)
    values = values * 747796405 + 1013904223
    values = values ^ (values >> 13)
    values = values * 277803737
    return values ^ (values >> 16)


def draw(index, stream_base):
    first = scramble(index ^ stream_base)
    second = scramble(first + 1664525)
    total = (
        (first & 65535)
        + ((first >> 16) & 65535)
        + (second & 65535)
        + ((second >> 16) & 65535)
        - 131070
    )
    return total.astype(jnp.float32) * noise_scale


def packed_source(columns, tiles, core):
    lane = columns & (LANES - 1)
    tile = (columns // LANES) + (tiles // 2) * ((lane // HALF) ^ core)
    return (lane & (HALF - 1)) * tiles + tile


def packing(width, tiles, core, axis):
    natural = lax.broadcasted_iota(jnp.int32, (width, width), 1 - axis)
    columns = lax.broadcasted_iota(jnp.int32, (width, width), axis)
    return jnp.where(packed_source(columns, tiles, core) == natural, 1.0, 0.0).astype(jnp.bfloat16)


def split(values):
    high = values.astype(jnp.bfloat16)
    return high, (values - high.astype(jnp.float32)).astype(jnp.bfloat16)


def permuted(values, matrix):
    high, low = split(values)
    both = jnp.concatenate([high, low], axis=1)
    return jnp.dot(both, jnp.concatenate([matrix, matrix], axis=0), preferred_element_type=jnp.float32)


def conduct_kernel(ids, mask, diffusivity, out, matrix):
    levels, height, width = mask.shape
    tiles = 2 * width // LANES

    @pl.when(pl.program_id(0) == 0)
    def _():
        matrix[...] = packing(width, tiles, ids[0], 1)

    conduct = diffusivity[...] * mask[...].astype(jnp.float32)
    moved = permuted(conduct.reshape(levels * height, width), matrix[...])
    for t in range(width // LANES):
        out[:, t] = moved[:, t * LANES : (t + 1) * LANES].reshape(levels, height, LANES)


def packed_conduct(ids, mask, diffusivity):
    levels, height, width = mask.shape
    step = math.gcd(levels, 6)
    block = pl.BlockSpec((step, height, width), lambda l: (l, 0, 0))
    return pl.pallas_call(
        conduct_kernel,
        out_shape=jax.ShapeDtypeStruct((levels, width // LANES, height, LANES), jnp.float32),
        grid=(levels // step,),
        in_specs=[scalars(), block, block],
        out_specs=pl.BlockSpec((step, width // LANES, height, LANES), lambda l: (l, 0, 0, 0)),
        scratch_shapes=[VMEM((width, width), jnp.bfloat16)],
    )(ids, mask, diffusivity)


def noise_kernel(total_rows, total_cols, ids, out):
    levels, tiles, pitch = out.shape[:3]
    base, level0, row0 = ids[0], ids[1], ids[2]
    sub = lax.broadcasted_iota(jnp.int32, (SUB, LANES), 0)
    lane = lax.broadcasted_iota(jnp.int32, (SUB, LANES), 1)
    within = sub * (pitch * total_cols) + lane * tiles

    @pl.loop(0, levels)
    def _(l):
        start = ((level0 + l) * total_rows + row0) * total_cols
        for t in range(tiles):
            for k in range(pitch):
                out[l, t, k] = draw(within + (start + k * total_cols + t), base)


def noise(ids, levels, tiles, pitch, total_rows, total_cols):
    return pl.pallas_call(
        functools.partial(noise_kernel, total_rows, total_cols),
        out_shape=jax.ShapeDtypeStruct((levels, tiles, pitch, SUB, LANES), jnp.float32),
        in_specs=[scalars()],
        out_specs=whole(),
    )(ids)


def neighbour_sums(old, tiles, pitch, emit):
    first = [old[t, 0] for t in range(tiles)]
    last = [old[t, pitch - 1] for t in range(tiles)]
    above = [pltpu.roll(v, 1, 0) for v in last]
    here = first
    for k in range(pitch):
        if k == pitch - 1:
            below = [pltpu.roll(v, SUB - 1, 0) for v in first]
        elif k == pitch - 2:
            below = last
        else:
            below = [old[t, k + 1] for t in range(tiles)]
        west = [pltpu.roll(here[-1], 1, 1)] + here[:-1]
        east = here[1:] + [pltpu.roll(here[0], LANES - 1, 1)]
        for t in range(tiles):
            emit(t, k, here[t], (west[t] + east[t]) + (above[t] + below[t]))
        above, here = here, below


def diffuse_kernel(halo, ids, mine, theirs, top_mine, top_theirs, low_mine, low_theirs, source, near, far,
                   rows, cond, gain, push, inv, u0, u1, res):
    tiles, pitch = source.shape[1], source.shape[2]
    pairs, height = mine.shape[1], mine.shape[2]
    core, group = ids[0], ids[3]

    def on_left(shape):
        lane = lax.broadcasted_iota(jnp.int32, shape, len(shape) - 1)
        return (lane // HALF) == core

    for a, b, start in (
        (top_mine, top_theirs, 0), (mine, theirs, halo), (low_mine, low_theirs, halo + height),
    ):
        count = a.shape[2]
        left = on_left((count, LANES))
        for v in range(pairs):
            p, q = a[0, v], b[0, v]
            rows[v, pl.ds(start, count), :] = jnp.where(left, p, q)
            rows[v + pairs, pl.ds(start, count), :] = pltpu.roll(jnp.where(left, q, p), HALF, 1)
    for t in range(tiles):
        for k in range(pitch):
            cond[t, k] = rows[t, pl.ds(k, SUB, stride=pitch), :]

    def prepare(t, k, c, total):
        s = source[0, t, k]
        r = 1.0 / (1.0 + c * total)
        q = c * r
        inv[t, k] = r
        push[t, k] = q * s
        gain[t, k] = q * c
        u0[t, k] = c * s

    neighbour_sums(cond, tiles, pitch, prepare)

    def sweep(old, new):
        def step(t, k, value, total):
            new[t, k] = push[t, k] + gain[t, k] * total

        neighbour_sums(old, tiles, pitch, step)

    @pl.loop(0, (SWEEPS - 2) // 2)
    def _(i):
        sweep(u0, u1)
        sweep(u1, u0)

    sweep(u0, u1)

    def finish(t, k, value, total):
        c, s = cond[t, k], source[0, t, k]
        res[t, pl.ds(k, SUB, stride=pitch), :] = jnp.where(c != 0.0, (s + c * total) * inv[t, k], 0.0)

    neighbour_sums(u1, tiles, pitch, finish)
    left = on_left((height, LANES))
    final = height // 2
    for v in range(pairs):
        a = res[v, pl.ds(halo, height), :]
        b = pltpu.roll(res[v + pairs, pl.ds(halo, height), :], HALF, 1)
        keep, send = jnp.where(left, a, b), jnp.where(left, b, a)
        for value, slot in ((keep, 0), (send, 1)):
            upper, lower = value[:final], value[final:]
            first = group == 0
            near[slot, 0, v] = jnp.where(first, upper, lower)
            far[slot, 0, v] = jnp.where(first, lower, upper)


def diffuse(ids, mine, theirs, top, bottom, source):
    levels, pairs, height, _ = mine.shape
    halo = top.shape[3]
    tiles, pitch = source.shape[1:3]
    tile = VMEM((tiles, pitch, SUB, LANES), jnp.float32)
    line = VMEM((tiles, pitch * SUB, LANES), jnp.float32)
    own = pl.BlockSpec((1, pairs, height, LANES), lambda l: (l, 0, 0, 0))
    edge = [pl.BlockSpec((pl.Squeezed(), 1, pairs, halo, LANES), lambda l, i=i: (i, l, 0, 0, 0)) for i in range(2)]
    result = jax.ShapeDtypeStruct((2, levels, pairs, height // 2, LANES), jnp.float32)
    part = pl.BlockSpec((2, 1, pairs, height // 2, LANES), lambda l: (0, l, 0, 0, 0))
    return pl.pallas_call(
        functools.partial(diffuse_kernel, halo),
        out_shape=(result, result),
        grid=(levels,),
        in_specs=[scalars(), own, own, *edge, *edge,
                  pl.BlockSpec((1, tiles, pitch, SUB, LANES), lambda l: (l, 0, 0, 0, 0))],
        out_specs=(part, part),
        scratch_shapes=[line] + [tile] * 6 + [line],
    )(ids, mine, theirs, top, top, bottom, bottom, source)


def unpack(pieces, matrix, out, start):
    for piece in pieces:
        levels, tiles, height, _ = piece.shape
        values = jnp.concatenate(
            [piece[:, t].reshape(levels * height, LANES) for t in range(tiles)], axis=1
        )
        moved = permuted(values, matrix)
        for t in range(tiles):
            out[start : start + levels, t] = moved[:, t * LANES : (t + 1) * LANES].reshape(levels, height, LANES)
        start += levels


def unpack_kernel(ids, *refs):
    *pieces, out = refs
    tiles = pieces[0].shape[1]
    unpack(pieces, packing(tiles * LANES, 2 * tiles, ids[0], 0), out, 0)


def unpacked(ids, pieces):
    levels, tiles, height, _ = pieces[0].shape
    return pl.pallas_call(
        unpack_kernel,
        out_shape=jax.ShapeDtypeStruct((sum(p.shape[0] for p in pieces), tiles, height, LANES), jnp.float32),
        in_specs=[scalars()] + [whole()] * len(pieces),
        out_specs=whole(),
    )(ids, *pieces)


def balance_kernel(ids, weights, near, *refs):
    *pieces, out, columns, result = refs
    total = weights.shape[0]
    count, tiles, height, _ = columns.shape
    pitch = tiles * height
    columns[: near.shape[0]] = near[...]
    unpack(pieces, packing(tiles * LANES, 2 * tiles, ids[0], 0), columns, near.shape[0])
    flat = columns.reshape(count * pitch, LANES)
    high, low = split(weights[...])
    stacked = jnp.concatenate([high, high, low], axis=1)
    for r in range(height):
        for t in range(tiles):
            top, rest = split(flat[pl.ds(t * height + r, count, stride=pitch), :])
            right = jnp.concatenate([top, rest, top], axis=0)
            result[pl.ds(t * height + r, total, stride=pitch), :] = jnp.dot(
                stacked, right, preferred_element_type=jnp.float32
            )
    for t in range(tiles):
        for l in range(total):
            start = l * pitch + t * height
            out[l, :, t * LANES : (t + 1) * LANES] = result[start : start + height, :]


def balanced(ids, weights, near, pieces):
    _, tiles, height, _ = near.shape
    total, count = weights.shape
    return pl.pallas_call(
        balance_kernel,
        out_shape=jax.ShapeDtypeStruct((total, height, tiles * LANES), jnp.float32),
        in_specs=[scalars()] + [whole()] * (2 + len(pieces)),
        out_specs=whole(),
        scratch_shapes=[
            VMEM((count, tiles, height, LANES), jnp.float32),
            VMEM((total * tiles * height, LANES), jnp.float32),
        ],
        compiler_params=pltpu.CompilerParams(vmem_limit_bytes=48 << 20),
    )(ids, weights, near, *pieces)


def crossed(block, axis):
    count = lax.axis_size(axis)
    return lax.ppermute(block, axis, [(i, count - 1 - i) for i in range(count)])


def part(block, index, size, axis):
    return lax.dynamic_slice_in_dim(block, index * size, size, axis=axis)


def gathered(place, near, far, weights_of):
    core, groups = place[0], lax.axis_size("lev")
    rows = jnp.concatenate([near, far], axis=3)
    rows = jnp.stack([rows[0], crossed(rows[1], "lon")])
    pieces = lax.all_to_all(rows, "lev", split_axis=3, concat_axis=0, tiled=True)
    count, share, tiles, height, _ = pieces.shape
    values = pieces.transpose(0, 1, 3, 2, 4).reshape(count * share, height, tiles * LANES)
    matrix = packing(tiles * LANES, 2 * tiles, core, 0).astype(jnp.float32)
    values = jnp.einsum("mrp,pc->mrc", values, matrix, precision=lax.Precision.HIGHEST)
    weights = weights_of([(g, c) for g in range(groups) for c in (core, 1 - core)])
    return jnp.einsum("lm,mrc->lrc", weights, values, precision=lax.Precision.HIGHEST)


def per_device(land_mask, diffusivity, balance, member_id, counter_key):
    levels, height, breadth = land_mask.shape
    cores, groups, strips = (lax.axis_size(a) for a in ("lon", "lev", "lat"))
    core, group, strip = (lax.axis_index(a) for a in ("lon", "lev", "lat"))
    assert cores == 2 and height > SWEEPS
    halo = SWEEPS
    pitch = (height + 2 * halo) // SUB
    share = -(-levels // cores)
    spare = share * cores - levels
    if spare:
        land_mask, diffusivity = (jnp.pad(v, ((0, spare), (0, 0), (0, 0))) for v in (land_mask, diffusivity))
    base = counter_key[0] * 69069 + member_id[0] * 362437
    place = jnp.stack([core, core, core, group if groups == 2 else 0 * group])
    ids = jnp.stack([base, group * levels + core * share, strip * height - halo])
    conduct = packed_conduct(place, land_mask, diffusivity)
    mine, theirs = part(conduct, core, share, 0), crossed(part(conduct, 1 - core, share, 0), "lon")
    onward = [(i, i + 1) for i in range(strips - 1)]
    backward = [(b, a) for a, b in onward]
    edges = jnp.stack([mine, theirs])
    top = lax.ppermute(edges[:, :, :, -halo:], "lat", onward)
    bottom = lax.ppermute(edges[:, :, :, :halo], "lat", backward)
    tiles = breadth * cores // LANES
    source = noise(ids, share, tiles, pitch, height * strips, breadth * cores)
    near, far = diffuse(place, mine, theirs, top, bottom, source)

    def weights_of(order):
        padded = jnp.pad(balance.reshape(-1, groups, levels), ((0, 0), (0, 0), (0, spare)))
        padded = padded.reshape(-1, groups * cores * share)
        return jnp.concatenate([part(padded, g * cores + c, share, 1) for g, c in order], axis=1)

    if groups != 2:
        return gathered(place, near, far, weights_of)
    near_theirs = crossed(near[1], "lon")
    far_theirs = crossed(far[1], "lon")
    far_mine = crossed(far[0], "lev")
    far_theirs = crossed(far_theirs, "lev")
    weights = weights_of([(g, c) for g in (group, 1 - group) for c in (core, 1 - core)])
    own = unpacked(place, (near[0], near_theirs))
    return balanced(place, weights, own, (far_mine, far_theirs))


def solution(mesh):
    in_specs = (P("lev", "lat", "lon"), P("lev", "lat", "lon"), P(), P("member"), P("member"))
    out_specs = P("member", ("lat", "lev"), "lon")
    return jax.shard_map(
        per_device, mesh=mesh, in_specs=in_specs, out_specs=out_specs, check_vma=False
    )
```

time: 104 us -> 88.9 us (0.85)
  waiting for transfers between devices: 37.4 us -> 23.2 us
  local copies, waits for them, and re-layouts: 1.51 us -> 9.62 us
  Pallas kernels: 47.8 us -> 42.8 us
  other arithmetic: 6.21 us -> 1.48 us
    ppermute x5 -> x7, waiting for transfers between devices: 37.4 us -> 23.2 us  [the longest x5 17.9 us: crossed(): return lax.ppermute(block, axis, [(i, count - 1 - i) for i in range(count)])]
    pallas_call x2 -> x4, Pallas kernels: 44.9 us -> 38.8 us  [the longest x1 24.1 us: diffuse(): pl.pallas_call(functools.partial(diffuse_kernel, halo), out_shape=(result...]
    unnamed x4 -> x14, local copies, waits for them, and re-layouts: 0.01 us -> 2.73 us
    mul x1 -> x0, other arithmetic: 2.31 us -> none  [per_device(): conduct = diffusivity * land_mask.astype(jnp.float32)]
    squeeze x0 -> x2, local copies, waits for them, and re-layouts: none -> 2.12 us  [the longest x1 1.28 us: per_device(): far_theirs = crossed(far[1], 'lon')]
    ppermute x0 -> x2, local copies, waits for them, and re-layouts: none -> 2.05 us  [the longest x1 1.04 us: per_device(): bottom = lax.ppermute(edges[:, :, :, :halo], 'lat', backward)]
    concatenate x4 -> x1, other arithmetic: 1.79 us -> 0.1 us  [weights_of(): jnp.concatenate([part(padded, g * cores + c, share, 1) for g, c in order]...]
    select_n x2 -> x0, other arithmetic: 1.5 us -> none  [the longest x1 1.3 us: per_device(): jnp.where(core == 0, mine, theirs)]
  transfers between devices with their start and end apart: 5 -> 7, of which waited for: 5 -> 5; matrix products, arithmetic and copies ran while one was open for 2% -> 4% of each run, Pallas kernels for 6% -> 10%
where the time goes in v2:
time: 88.9 us; the launch traced here: 88.4 us
  Pallas kernels  42.8 us (48%)
  waiting for transfers between devices  23.2 us (26%)
  starting transfers between devices  9.93 us (11%)
  local copies, waits for them, and re-layouts  9.62 us (11%)
  other arithmetic  1.48 us (2%)
  between operations  1.43 us (2%)
    pallas_call x1, Pallas kernels, diffuse(): pl.pallas_call(functools.partial(diffuse_kernel, halo), out_shape=(result...  24.1 us
    ppermute x5, waiting for transfers between devices, crossed(): return lax.ppermute(block, axis, [(i, count - 1 - i) for i in range(count)])  17.9 us
    pallas_call x1, Pallas kernels, noise(): pl.pallas_call(functools.partial(noise_kernel, total_rows, total_cols), o...  6.12 us
    pallas_call x1, Pallas kernels, packed_conduct(): pl.pallas_call(conduct_kernel, out_shape=jax.ShapeDtypeStruct((levels, wi...  5.85 us
    ppermute x1, starting transfers between devices, per_device(): top = lax.ppermute(edges[:, :, :, -halo:], 'lat', onward)  5.51 us
    ppermute x1, waiting for transfers between devices, per_device(): bottom = lax.ppermute(edges[:, :, :, :halo], 'lat', backward)  4.69 us
    pallas_call x1, Pallas kernels, balanced(): pl.pallas_call(balance_kernel, out_shape=jax.ShapeDtypeStruct((total, hei...  4.01 us
    ppermute x5, starting transfers between devices, crossed(): return lax.ppermute(block, axis, [(i, count - 1 - i) for i in range(count)])  3.12 us
  transfers between devices with their start and end apart: 7, of which 5 were waited for; matrix products, arithmetic and copies ran while one was open for 4% of the time, Pallas kernels for 10%

profile of v2, /device:TPU:0, one launch (start us, length us, event | category | flops | bytes accessed | tf_op | source)
XLA Modules:
  0.0 88.4 jit_solution(7753147480249345352)
XLA Ops:
  0.0 0.6 pad_add_fusion.ids
  0.6 5.8 %shard_map.55 = f32[36,3,32,128]{3,2,1,0:T(8,128)} custom-call(s32[4]{0:T(128)} %pad_add_fusion.ids, s32[36,32,384]{2,1,0:T(8,128)} %mask.1, f32[36,32,384]{2,1,0:T(8,128)} %diffusivity.1), custom_call_target="tpu_custom_call" | custom-call | tf_op jit(solution)/shard_map/pallas_call | solution.py:83
  6.5 1.6 %constant_dynamic-slice_fusion = (f32[18,3,32,128]{3,2,1,0:T(8,128)S(1)}, f32[18,3,32,128]{3,2,1,0:T(8,128)S(1)}) fusion(f32[36,3,32,128]{3,2,1,0:T(8,128)} %shard_map.55, s32[]{:T(128)S(6)} %select_n.23, s32[]{:T(128)S(6)} %select_n.22), kind=kLoop, calls=%fused_computation.9 | loop fusion | bytes 3538952 | tf_op jit(solution)/shard_map/dynamic_slice | solution.py:295
  8.1 0.5 collective-permute-start
  8.6 2.1 %collective-permute-done.theirs = f32[18,3,32,128]{3,2,1,0:T(8,128)S(1)} collective-permute-done((f32[18,3,32,128]{3,2,1,0:T(8,128)S(1)}, f32[18,3,32,128]{3,2,1,0:T(8,128)S(1)}, u32[]{:S(2)}, u32[]{:S(2)}) %collective-permute-start) | collective-permute-done | bytes 884768 | tf_op jit(solution)/shard_map/ppermute | solution.py:291
  10.8 0.7 copy-done.3
  12.1 1.3 %collective-permute-start.2 = (f32[2,18,3,12,128]{4,0,3,2,1:T(2,128)S(1)}, f32[2,18,3,12,128]{4,0,3,2,1:T(2,128)S(1)}, u32[]{:S(2)}, u32[]{:S(2)}) collective-permute-start(f32[2,18,3,12,128]{4,0,3,2,1:T(2,128)S(1)} %copy.7), channel_id=1, source_target_pairs={{4,0},{8,4},{12,8},{5,1},{9,5},{13,9},{6,2},{10,6},{14,10},{7,3},{... | collective-permute-start | bytes 1990664 | tf_op jit(solution)/shard_map/ppermute | solution.py:331
  13.9 5.5 %collective-permute-start.1 = (f32[2,18,3,12,128]{4,0,3,2,1:T(2,128)S(1)}, f32[2,18,3,12,128]{4,0,3,2,1:T(2,128)S(1)}, u32[]{:S(2)}, u32[]{:S(2)}) collective-permute-start(f32[2,18,3,12,128]{4,0,3,2,1:T(2,128)S(1)} %copy.6), channel_id=1, source_target_pairs={{0,4},{4,8},{8,12},{1,5},{5,9},{9,13},{2,6},{6,10},{10,14},{3,7},{... | collective-permute-start | bytes 1990664 | tf_op jit(solution)/shard_map/ppermute | solution.py:330
  20.7 0.6 pad_add_fusion.1.ids
  21.3 6.1 %shard_map.56.source = f32[18,6,7,8,128]{4,3,2,1,0:T(8,128)} custom-call(s32[3]{0:T(128)} %pad_add_fusion.1.ids), custom_call_target="tpu_custom_call" | custom-call | tf_op jit(solution)/shard_map/pallas_call | solution.py:109
  27.5 4.7 %collective-permute-done.2 = f32[2,18,3,12,128]{4,0,3,2,1:T(2,128)S(1)} collective-permute-done((f32[2,18,3,12,128]{4,0,3,2,1:T(2,128)S(1)}, f32[2,18,3,12,128]{4,0,3,2,1:T(2,128)S(1)}, u32[]{:S(2)}, u32[]{:S(2)}) %collective-permute-start.2) | collective-permute-done | bytes 663584 | tf_op jit(solution)/shard_map/ppermute | solution.py:331
  32.1 1.0 %copy.10.low_mine.low_theirs = f32[2,18,3,12,128]{4,3,2,1,0:T(8,128)} copy(f32[2,18,3,12,128]{4,0,3,2,1:T(2,128)S(1)} %collective-permute-done.2) | data formatting | bytes 1327104 | tf_op jit(solution)/shard_map/ppermute | solution.py:331
  33.2 0.7 collective-permute-done.1
  33.8 1.0 %copy.8.top_mine.top_theirs = f32[2,18,3,12,128]{4,3,2,1,0:T(8,128)} copy(f32[2,18,3,12,128]{4,0,3,2,1:T(2,128)S(1)} %collective-permute-done.1) | data formatting | bytes 1327104 | tf_op jit(solution)/shard_map/ppermute | solution.py:330
  34.9 24.1 %shard_map.57 = (f32[2,18,3,16,128]{4,3,2,1,0:T(8,128)}, f32[2,18,3,16,128]{4,3,2,1,0:T(8,128)}) custom-call(s32[4]{0:T(128)} %pad_add_fusion.ids, f32[18,3,32,128]{3,2,1,0:T(8,128)} %copy-done.2, f32[18,3,32,128]{3,2,1,0:T(8,128)} %copy-done.3, f32[2,18,3,12,128]{4,3,2,1,0:T(8,128)} %copy.8.top_mine.top_theirs, ...), custom_call_target="tpu_custom_call" | custom-call | tf_op jit(solution)/shard_map/pallas_call | solution.py:211
  58.9 1.3 %slice_bitcast_fusion = (f32[18,3,16,128]{3,2,1,0:T(8,128)S(1)}, f32[18,3,16,128]{3,2,1,0:T(8,128)S(1)}) fusion(f32[2,18,3,16,128]{4,3,2,1,0:T(8,128)} %get-tuple-element.8), kind=kLoop, calls=%fused_computation.4 | loop fusion | bytes 1769472 | tf_op jit(solution)/shard_map/squeeze | solution.py:344
  60.4 0.8 slice_bitcast_fusion.2
  61.6 1.7 %collective-permute-start.4 = (f32[18,3,16,128]{3,2,1,0:T(8,128)S(1)}, f32[18,3,16,128]{3,2,1,0:T(8,128)S(1)}, u32[]{:S(2)}, u32[]{:S(2)}) collective-permute-start(f32[18,3,16,128]{3,2,1,0:T(8,128)S(1)} %get-tuple-element.14), channel_id=1, source_target_pairs={{0,2},{2,0},{1,3},{3,1},{4,6},{6,4},{5,7},{7,5},{8,10},{10,8},{9,1... | collective-permute-start | bytes 1327112 | tf_op jit(solution)/shard_map/ppermute | solution.py:291
  64.0 0.7 copy-done.6
  64.7 2.7 %shard_map.58.near = f32[36,3,16,128]{3,2,1,0:T(8,128)} custom-call(s32[4]{0:T(128)} %pad_add_fusion.ids, f32[18,3,16,128]{3,2,1,0:T(8,128)} %get-tuple-element.16.refs_0_, f32[18,3,16,128]{3,2,1,0:T(8,128)} %copy-done.6), custom_call_target="tpu_custom_call" | custom-call | tf_op jit(solution)/shard_map/pallas_call | solution.py:242
  67.5 7.2 %collective-permute-done.4.refs_0_ = f32[18,3,16,128]{3,2,1,0:T(8,128)S(1)} collective-permute-done((f32[18,3,16,128]{3,2,1,0:T(8,128)S(1)}, f32[18,3,16,128]{3,2,1,0:T(8,128)S(1)}, u32[]{:S(2)}, u32[]{:S(2)}) %collective-permute-start.4) | collective-permute-done | bytes 442400 | tf_op jit(solution)/shard_map/ppermute | solution.py:291
  74.7 8.6 %collective-permute-done.6.refs_1_ = f32[18,3,16,128]{3,2,1,0:T(8,128)S(1)} collective-permute-done((f32[18,3,16,128]{3,2,1,0:T(8,128)S(1)}, f32[18,3,16,128]{3,2,1,0:T(8,128)S(1)}, u32[]{:S(2)}, u32[]{:S(2)}) %collective-permute-start.6) | collective-permute-done | bytes 442400 | tf_op jit(solution)/shard_map/ppermute | solution.py:291
  83.3 1.2 %copy-done = f32[36,3,16,128]{3,2,1,0:T(8,128)S(1)} copy-done((f32[36,3,16,128]{3,2,1,0:T(8,128)S(1)}, f32[36,3,16,128]{3,2,1,0:T(8,128)}, u32[]{:S(2)}) %copy-start) | copy-done | bytes 884760
  84.4 4.0 %shard_map.59 = f32[72,16,384]{2,1,0:T(8,128)} custom-call(s32[4]{0:T(128)S(1)} %copy-done.1, f32[72,72]{1,0:T(8,128)S(1)} %pad_maximum_fusion.1.weights, f32[36,3,16,128]{3,2,1,0:T(8,128)S(1)} %copy-done, f32[18,3,16,128]{3,2,1,0:T(8,128)S(1)} %collective-permute-done.4.refs_0_, f32[18,3,16,128]{3,2,1,0:T(8,128)S(1)} %collective-permute-done.6.refs_1_), custom_call_target="tpu_custom_call" | custom-call | tf_op jit(solution)/shard_map/pallas_call | solution.py:276
  (21 shorter events, 2.4 us)
Async XLA Ops:
  8.1 2.8 %copy-start.2 = (f32[18,3,32,128]{3,2,1,0:T(8,128)}, f32[18,3,32,128]{3,2,1,0:T(8,128)S(1)}, u32[]{:S(2)}) copy-start(f32[18,3,32,128]{3,2,1,0:T(8,128)S(1)} %get-tuple-element.12.mine) | copy-start | bytes 2654212
  8.1 2.6 %collective-permute-start = (f32[18,3,32,128]{3,2,1,0:T(8,128)S(1)}, f32[18,3,32,128]{3,2,1,0:T(8,128)S(1)}, u32[]{:S(2)}, u32[]{:S(2)}) collective-permute-start(f32[18,3,32,128]{3,2,1,0:T(8,128)S(1)} %get-tuple-element.11), channel_id=1, source_target_pairs={{0,1},{1,0},{2,3},{3,2},{4,5},{5,4},{6,7},{7,6},{8,9},{9,8},{10,11... | collective-permute-start | bytes 2654216 | tf_op jit(solution)/shard_map/ppermute | solution.py:291
  10.6 0.9 %copy-start.3 = (f32[18,3,32,128]{3,2,1,0:T(8,128)}, f32[18,3,32,128]{3,2,1,0:T(8,128)S(1)}, u32[]{:S(2)}) copy-start(f32[18,3,32,128]{3,2,1,0:T(8,128)S(1)} %collective-permute-done.theirs) | copy-start | bytes 2654212
  12.1 20.0 %collective-permute-start.2 = (f32[2,18,3,12,128]{4,0,3,2,1:T(2,128)S(1)}, f32[2,18,3,12,128]{4,0,3,2,1:T(2,128)S(1)}, u32[]{:S(2)}, u32[]{:S(2)}) collective-permute-start(f32[2,18,3,12,128]{4,0,3,2,1:T(2,128)S(1)} %copy.7), channel_id=1, source_target_pairs={{4,0},{8,4},{12,8},{5,1},{9,5},{13,9},{6,2},{10,6},{14,10},{7,3},{... | collective-permute-start | bytes 1990664 | tf_op jit(solution)/shard_map/ppermute | solution.py:331
  13.9 19.9 %collective-permute-start.1 = (f32[2,18,3,12,128]{4,0,3,2,1:T(2,128)S(1)}, f32[2,18,3,12,128]{4,0,3,2,1:T(2,128)S(1)}, u32[]{:S(2)}, u32[]{:S(2)}) collective-permute-start(f32[2,18,3,12,128]{4,0,3,2,1:T(2,128)S(1)} %copy.6), channel_id=1, source_target_pairs={{0,4},{4,8},{8,12},{1,5},{5,9},{9,13},{2,6},{6,10},{10,14},{3,7},{... | collective-permute-start | bytes 1990664 | tf_op jit(solution)/shard_map/ppermute | solution.py:330
  58.9 1.4 %copy-start.4 = (f32[2,18,3,16,128]{4,3,2,1,0:T(8,128)S(1)}, f32[2,18,3,16,128]{4,3,2,1,0:T(8,128)}, u32[]{:S(2)}) copy-start(f32[2,18,3,16,128]{4,3,2,1,0:T(8,128)} %get-tuple-element.7) | copy-start | bytes 2654212
  58.9 4.8 %copy-start.5 = (f32[72,72]{1,0:T(8,128)S(1)}, f32[72,72]{1,0:T(8,128)}, u32[]{:S(2)}) copy-start(f32[72,72]{1,0:T(8,128)} %param.7) | copy-start | bytes 62212
  60.2 3.1 %collective-permute-start.5 = (f32[18,3,16,128]{3,2,1,0:T(8,128)S(1)}, f32[18,3,16,128]{3,2,1,0:T(8,128)S(1)}, u32[]{:S(2)}, u32[]{:S(2)}) collective-permute-start(f32[18,3,16,128]{3,2,1,0:T(8,128)S(1)} %get-tuple-element.13), channel_id=1, source_target_pairs={{0,1},{1,0},{2,3},{3,2},{4,5},{5,4},{6,7},{7,6},{8,9},{9,8},{10,11... | collective-permute-start | bytes 1327112 | tf_op jit(solution)/shard_map/ppermute | solution.py:291
  60.3 22.9 %copy-start.1 = (s32[4]{0:T(128)S(1)}, s32[4]{0:T(128)}, u32[]{:S(2)}) copy-start(s32[4]{0:T(128)} %pad_add_fusion.ids) | copy-start | bytes 52
  61.2 2.8 %collective-permute-start.3 = (f32[18,3,16,128]{3,2,1,0:T(8,128)S(1)}, f32[18,3,16,128]{3,2,1,0:T(8,128)S(1)}, u32[]{:S(2)}, u32[]{:S(2)}) collective-permute-start(f32[18,3,16,128]{3,2,1,0:T(8,128)S(1)} %get-tuple-element.15), channel_id=1, source_target_pairs={{0,1},{1,0},{2,3},{3,2},{4,5},{5,4},{6,7},{7,6},{8,9},{9,8},{10,11... | collective-permute-start | bytes 1327112 | tf_op jit(solution)/shard_map/ppermute | solution.py:291
  61.6 13.0 %collective-permute-start.4 = (f32[18,3,16,128]{3,2,1,0:T(8,128)S(1)}, f32[18,3,16,128]{3,2,1,0:T(8,128)S(1)}, u32[]{:S(2)}, u32[]{:S(2)}) collective-permute-start(f32[18,3,16,128]{3,2,1,0:T(8,128)S(1)} %get-tuple-element.14), channel_id=1, source_target_pairs={{0,2},{2,0},{1,3},{3,1},{4,6},{6,4},{5,7},{7,5},{8,10},{10,8},{9,1... | collective-permute-start | bytes 1327112 | tf_op jit(solution)/shard_map/ppermute | solution.py:291
  63.3 20.0 %collective-permute-start.6 = (f32[18,3,16,128]{3,2,1,0:T(8,128)S(1)}, f32[18,3,16,128]{3,2,1,0:T(8,128)S(1)}, u32[]{:S(2)}, u32[]{:S(2)}) collective-permute-start(f32[18,3,16,128]{3,2,1,0:T(8,128)S(1)} %collective-permute-done.5), channel_id=1, source_target_pairs={{0,2},{2,0},{1,3},{3,1},{4,6},{6,4},{5,7},{7,5},{8,10},{10,8},{9,1... | collective-permute-start | bytes 1327112 | tf_op jit(solution)/shard_map/ppermute | solution.py:291
  64.0 0.8 copy-start.6
  83.3 1.2 %copy-start = (f32[36,3,16,128]{3,2,1,0:T(8,128)S(1)}, f32[36,3,16,128]{3,2,1,0:T(8,128)}, u32[]{:S(2)}) copy-start(f32[36,3,16,128]{3,2,1,0:T(8,128)} %shard_map.58.near) | copy-start | bytes 2654212

commit v3 on v2

v3 whole, which is shorter than its diff:
```python
import functools
import math

import jax
import jax.numpy as jnp
from jax import lax
from jax.experimental import pallas as pl
from jax.experimental.pallas import tpu as pltpu
from jax.sharding import PartitionSpec as P

SWEEPS = 12
SOME = 3
noise_scale = math.sqrt(3.0) / 65536.0
LANES, SUB = 128, 8
HALF = LANES // 2
VMEM = pltpu.VMEM
whole = functools.partial(pl.BlockSpec, memory_space=pltpu.VMEM)
scalars = functools.partial(pl.BlockSpec, memory_space=pltpu.SMEM)


def scramble(values):
    values = values * 1103515245 + 12345
    values = values ^ (values >> 15)
    values = values * 747796405 + 1013904223
    values = values ^ (values >> 13)
    values = values * 277803737
    return values ^ (values >> 16)


def draw(index, stream_base):
    first = scramble(index ^ stream_base)
    second = scramble(first + 1664525)
    total = (
        (first & 65535)
        + ((first >> 16) & 65535)
        + (second & 65535)
        + ((second >> 16) & 65535)
        - 131070
    )
    return total.astype(jnp.float32) * noise_scale


def packed_source(columns, tiles, core):
    lane = columns & (LANES - 1)
    tile = (columns // LANES) + (tiles // 2) * ((lane // HALF) ^ core)
    return (lane & (HALF - 1)) * tiles + tile


def packing(width, tiles, core, axis):
    natural = lax.broadcasted_iota(jnp.int32, (width, width), 1 - axis)
    columns = lax.broadcasted_iota(jnp.int32, (width, width), axis)
    return jnp.where(packed_source(columns, tiles, core) == natural, 1.0, 0.0).astype(jnp.bfloat16)


def split(values):
    high = values.astype(jnp.bfloat16)
    return high, (values - high.astype(jnp.float32)).astype(jnp.bfloat16)


def permuted(values, matrix):
    rows = values.shape[0]
    both = jnp.dot(jnp.concatenate(split(values), axis=0), matrix, preferred_element_type=jnp.float32)
    return both[:rows] + both[rows:]


def quarter(keep):
    core = lax.axis_index("lon")
    return lax.axis_index("member") * 2 + (core if keep else 1 - core)


def edge_rows(some, pairs, halo):
    return -(-some * pairs * halo // SUB) * SUB


def conduct_kernel(halo, mask_mine, mine_in, mask_send, send_in, *refs):
    *outs, matrix = refs
    levels, height, width = mask_mine.shape
    pairs = width // LANES

    @pl.when(pl.program_id(0) == 0)
    def _():
        matrix[...] = packing(width, 2 * pairs, lax.axis_index("lon"), 1)

    both = [d[...] * m[...].astype(jnp.float32) for m, d in ((mask_mine, mine_in), (mask_send, send_in))]
    values = jnp.concatenate([v.reshape(levels * height, width) for v in both], axis=0)
    moved = permuted(values, matrix[...])
    for i in range(2):
        rows, top, bottom = outs[i], outs[2 + i], outs[4 + i]
        for g in range(levels):
            for v in range(pairs):
                start = (i * levels + g) * height
                value = moved[start : start + height, v * LANES : (v + 1) * LANES]
                rows[g, v] = value
                here = pl.ds((g * pairs + v) * halo, halo)
                top[0, here, :] = value[height - halo :]
                bottom[0, here, :] = value[:halo]


def packed_conduct(halo, share, mask, diffusivity):
    _, height, width = mask.shape
    some, pairs = math.gcd(share, SOME), width // LANES
    steps = share // some
    extent = edge_rows(some, pairs, halo)
    ins = [
        pl.BlockSpec((some, height, width), lambda l, keep=keep: (quarter(keep) * steps + l, 0, 0))
        for keep in (True, True, False, False)
    ]
    rows = jax.ShapeDtypeStruct((share, pairs, height, LANES), jnp.float32)
    edge = jax.ShapeDtypeStruct((steps, extent, LANES), jnp.float32)
    return pl.pallas_call(
        functools.partial(conduct_kernel, halo),
        out_shape=(rows,) * 2 + (edge,) * 4,
        grid=(steps,),
        in_specs=ins,
        out_specs=[pl.BlockSpec((some, pairs, height, LANES), lambda l: (l, 0, 0, 0))] * 2
        + [pl.BlockSpec((1, extent, LANES), lambda l: (l, 0, 0))] * 4,
        scratch_shapes=[VMEM((width, width), jnp.bfloat16)],
    )(mask, diffusivity, mask, diffusivity)


def noise_kernel(levels_here, halo, total_rows, total_cols, key, member, out):
    levels, tiles, pitch = out.shape[:3]
    base = key[0] * 69069 + member[0] * 362437
    level0 = lax.axis_index("lev") * levels_here + quarter(True) * levels
    row0 = lax.axis_index("lat") * (total_rows // lax.axis_size("lat")) - halo
    sub = lax.broadcasted_iota(jnp.int32, (SUB, LANES), 0)
    lane = lax.broadcasted_iota(jnp.int32, (SUB, LANES), 1)
    within = sub * (pitch * total_cols) + lane * tiles

    @pl.loop(0, levels)
    def _(l):
        start = ((level0 + l) * total_rows + row0) * total_cols
        for t in range(tiles):
            for k in range(pitch):
                out[l, t, k] = draw(within + (start + k * total_cols + t), base)


def noise(key, member, levels_here, halo, shape, total_rows, total_cols):
    return pl.pallas_call(
        functools.partial(noise_kernel, levels_here, halo, total_rows, total_cols),
        out_shape=jax.ShapeDtypeStruct(shape, jnp.float32),
        in_specs=[scalars()] * 2,
        out_specs=whole(),
    )(key, member)


def neighbour_sums(old, tiles, pitch, emit):
    some = range(old.shape[0])
    first = [[old[g, t, 0] for t in range(tiles)] for g in some]
    last = [[old[g, t, pitch - 1] for t in range(tiles)] for g in some]
    above = [[pltpu.roll(v, 1, 0) for v in last[g]] for g in some]
    here = first
    for k in range(pitch):
        if k == pitch - 1:
            below = [[pltpu.roll(v, SUB - 1, 0) for v in first[g]] for g in some]
        elif k == pitch - 2:
            below = last
        else:
            below = [[old[g, t, k + 1] for t in range(tiles)] for g in some]
        for g in some:
            row = here[g]
            west = [pltpu.roll(row[-1], 1, 1)] + row[:-1]
            east = row[1:] + [pltpu.roll(row[0], LANES - 1, 1)]
            for t in ORDER(tiles):
                emit(g, t, k, row[t], (west[t] + east[t]) + (above[g][t] + below[g][t]))
        above, here = here, below


def ORDER(tiles):
    return [*range(1, tiles - 1), 0, tiles - 1]


def diffuse_kernel(halo, halves, mine, theirs, top_mine, top_theirs, bottom_mine, bottom_theirs,
                   other_source, own_source, *refs):
    outs, (rows, cond, gain, push, inv, u0, u1, res) = refs[:8], refs[8:]
    sources = (other_source, own_source)
    levels, tiles, pitch = own_source.shape[:3]
    pairs, height = mine.shape[1], mine.shape[2]
    final = height // 2
    core = lax.axis_index("lon")
    group = lax.axis_index("lev") if halves else 0
    some = cond.shape[0]

    def on_left(shape):
        lane = lax.broadcasted_iota(jnp.int32, shape, len(shape) - 1)
        return (lane // HALF) == core

    def sweep(old, new):
        def step(g, t, k, value, total):
            new[g, t, k] = push[g, t, k] + gain[g % some, t, k] * total

        neighbour_sums(old, tiles, pitch, step)

    @pl.loop(0, levels // some)
    def _(block):
        for g in range(some):
            l = block * some + g
            for v in range(pairs):
                edge = pl.ds((g * pairs + v) * halo, halo)
                for p, q, start in (
                    (top_mine[block, edge, :], top_theirs[block, edge, :], 0),
                    (mine[l, v], theirs[l, v], halo),
                    (bottom_mine[block, edge, :], bottom_theirs[block, edge, :], halo + height),
                ):
                    count = p.shape[0]
                    left = on_left(p.shape)
                    rows[g, v, pl.ds(start, count), :] = jnp.where(left, p, q)
                    rows[g, v + pairs, pl.ds(start, count), :] = pltpu.roll(jnp.where(left, q, p), HALF, 1)
            for t in range(tiles):
                for k in range(pitch):
                    cond[g, t, k] = rows[g, t, pl.ds(k, SUB, stride=pitch), :]

        def prepare(g, t, k, c, total):
            r = 1.0 / (1.0 + c * total)
            q = c * r
            inv[g, t, k] = r
            gain[g, t, k] = q * c
            for i, source in enumerate(sources):
                s = source[block * some + g, t, k]
                push[i * some + g, t, k] = q * s
                u0[i * some + g, t, k] = c * s

        neighbour_sums(cond, tiles, pitch, prepare)

        @pl.loop(0, (SWEEPS - 2) // 2)
        def _(i):
            sweep(u0, u1)
            sweep(u1, u0)

        sweep(u0, u1)

        def finish(g, t, k, value, total):
            i, g = divmod(g, some)
            c, s = cond[g, t, k], sources[i][block * some + g, t, k]
            value = jnp.where(c != 0.0, (s + c * total) * inv[g, t, k], 0.0)
            res[i * some + g, t, pl.ds(k, SUB, stride=pitch), :] = value

        neighbour_sums(u1, tiles, pitch, finish)
        left = on_left((height, LANES))
        first = group == 0
        for i in range(2):
            near, far, near_send, far_send = outs[4 * i : 4 * i + 4]
            for g in range(some):
                l = block * some + g
                for v in range(pairs):
                    a = res[i * some + g, v, pl.ds(halo, height), :]
                    b = pltpu.roll(res[i * some + g, v + pairs, pl.ds(halo, height), :], HALF, 1)
                    keep, send = jnp.where(left, a, b), jnp.where(left, b, a)
                    for value, close, away in ((keep, near, far), (send, near_send, far_send)):
                        upper, lower = value[:final], value[final:]
                        close[l, v] = jnp.where(first, upper, lower)
                        away[l, v] = jnp.where(first, lower, upper)


def diffuse(halo, halves, *operands):
    levels, pairs, height, _ = operands[0].shape
    tiles, pitch = operands[-1].shape[1:3]
    some = math.gcd(levels, SOME)
    tile = VMEM((some, tiles, pitch, SUB, LANES), jnp.float32)
    both = VMEM((2 * some, tiles, pitch, SUB, LANES), jnp.float32)
    line = VMEM((2 * some, tiles, pitch * SUB, LANES), jnp.float32)
    result = jax.ShapeDtypeStruct((levels, pairs, height // 2, LANES), jnp.float32)
    return pl.pallas_call(
        functools.partial(diffuse_kernel, halo, halves),
        out_shape=(result,) * 8,
        in_specs=[whole()] * len(operands),
        out_specs=(whole(),) * 8,
        scratch_shapes=[line, tile, tile, both, tile, both, both, line],
    )(*operands)


def unpack(pieces, matrix, out, start):
    for piece in pieces:
        levels, tiles, height, _ = piece.shape
        values = jnp.concatenate(
            [piece[:, t].reshape(levels * height, LANES) for t in range(tiles)], axis=1
        )
        moved = permuted(values, matrix)
        for t in range(tiles):
            out[start : start + levels, t] = moved[:, t * LANES : (t + 1) * LANES].reshape(levels, height, LANES)
        start += levels


def unpack_kernel(*refs):
    *pieces, out = refs
    tiles = pieces[0].shape[1]
    unpack(pieces, packing(tiles * LANES, 2 * tiles, lax.axis_index("lon"), 0), out, 0)


def unpacked(pieces):
    levels, tiles, height, _ = pieces[0].shape
    return pl.pallas_call(
        unpack_kernel,
        out_shape=jax.ShapeDtypeStruct((sum(p.shape[0] for p in pieces), tiles, height, LANES), jnp.float32),
        in_specs=[whole()] * len(pieces),
        out_specs=whole(),
    )(*pieces)


def balance_kernel(weights, near, *refs):
    *pieces, out, columns, result = refs
    total = weights.shape[0]
    count, tiles, height, _ = columns.shape
    pitch = tiles * height
    columns[: near.shape[0]] = near[...]
    unpack(pieces, packing(tiles * LANES, 2 * tiles, lax.axis_index("lon"), 0), columns, near.shape[0])
    flat = columns.reshape(count * pitch, LANES)
    high, low = split(weights[...])
    stacked = jnp.concatenate([high, high, low], axis=1)
    for r in range(height):
        for t in range(tiles):
            top, rest = split(flat[pl.ds(t * height + r, count, stride=pitch), :])
            right = jnp.concatenate([top, rest, top], axis=0)
            result[pl.ds(t * height + r, total, stride=pitch), :] = jnp.dot(
                stacked, right, preferred_element_type=jnp.float32
            )
    for t in range(tiles):
        for l in range(total):
            start = l * pitch + t * height
            out[l, :, t * LANES : (t + 1) * LANES] = result[start : start + height, :]


def balanced(weights, near, pieces):
    _, tiles, height, _ = near.shape
    total, count = weights.shape
    return pl.pallas_call(
        balance_kernel,
        out_shape=jax.ShapeDtypeStruct((total, height, tiles * LANES), jnp.float32),
        in_specs=[whole()] * (2 + len(pieces)),
        out_specs=whole(),
        scratch_shapes=[
            VMEM((count, tiles, height, LANES), jnp.float32),
            VMEM((total * tiles * height, LANES), jnp.float32),
        ],
        compiler_params=pltpu.CompilerParams(vmem_limit_bytes=48 << 20),
    )(weights, near, *pieces)


def crossed(block, *axes):
    count = math.prod(lax.axis_size(a) for a in axes)
    return lax.ppermute(block, axes, [(i, count - 1 - i) for i in range(count)])


def shifted(block, step, cross):
    strips = lax.axis_size("lat")
    route = [
        (2 * i + c, 2 * (i + step) + (1 - c if cross else c))
        for i in range(strips) if 0 <= i + step < strips for c in range(2)
    ]
    return lax.ppermute(block, ("lat", "lon"), route)


def part(block, index, size, axis):
    return lax.dynamic_slice_in_dim(block, index * size, size, axis=axis)


def gathered(kept, came, weights_of):
    core, member, groups = (lax.axis_index("lon"), lax.axis_index("member"), lax.axis_size("lev"))
    halves = [jnp.concatenate(half, axis=2) for half in (kept[2:], came[2:], kept[:2], came[:2])]
    rows = jnp.concatenate([jnp.stack(halves[:2]), crossed(jnp.stack(halves[2:]), "member")])
    pieces = lax.all_to_all(rows, "lev", split_axis=3, concat_axis=0, tiled=True)
    count, share, tiles, height, _ = pieces.shape
    values = pieces.transpose(0, 1, 3, 2, 4).reshape(count * share, height, tiles * LANES)
    matrix = packing(tiles * LANES, 2 * tiles, core, 0).astype(jnp.float32)
    values = jnp.einsum("mrp,pc->mrc", values, matrix, precision=lax.Precision.HIGHEST)
    weights = weights_of(
        [(g, m, c) for g in range(groups) for m in (member, 1 - member) for c in (core, 1 - core)]
    )
    return jnp.einsum("lm,mrc->lrc", weights, values, precision=lax.Precision.HIGHEST)


def per_device(land_mask, diffusivity, balance, member_id, counter_key):
    levels, height, breadth = land_mask.shape
    members, cores, groups, strips = (lax.axis_size(a) for a in ("member", "lon", "lev", "lat"))
    core, member, group = (lax.axis_index(a) for a in ("lon", "member", "lev"))
    assert members == 2 and cores == 2 and height > SWEEPS
    halo = SWEEPS
    pitch = (height + 2 * halo) // SUB
    share = -(-levels // 4)
    spare = share * 4 - levels
    if spare:
        land_mask, diffusivity = (jnp.pad(v, ((0, spare), (0, 0), (0, 0))) for v in (land_mask, diffusivity))
    mine, send, top, top_cross, bottom, bottom_cross = packed_conduct(halo, share, land_mask, diffusivity)
    top, bottom = shifted(top, 1, False), shifted(bottom, -1, False)
    top_cross, bottom_cross = shifted(top_cross, 1, True), shifted(bottom_cross, -1, True)
    theirs = crossed(send, "lon")
    tiles = breadth * cores // LANES
    sizes = (levels, halo, (share, tiles, pitch, SUB, LANES), height * strips, breadth * cores)
    own = noise(counter_key, member_id, *sizes)
    other = noise(crossed(counter_key, "member"), crossed(member_id, "member"), *sizes)
    outs = diffuse(halo, groups == 2, mine, theirs, top, top_cross, bottom, bottom_cross, other, own)

    def weights_of(order):
        padded = jnp.pad(balance.reshape(-1, groups, levels), ((0, 0), (0, 0), (0, spare)))
        padded = padded.reshape(-1, groups * 4 * share)
        return jnp.concatenate([part(padded, g * 4 + m * 2 + c, share, 1) for g, m, c in order], axis=1)

    other_near, other_far, other_near_send, other_far_send, near, far, near_send, far_send = outs
    came = [crossed(v, "lon") for v in (other_near_send, other_far_send, near_send, far_send)]
    if groups != 2:
        return gathered((other_near, other_far, near, far), came, weights_of)
    here = (near, came[2])
    along_x = [crossed(v, "lev") for v in (far, came[3])]
    along_y = [crossed(v, "member") for v in (other_near, came[0])]
    diagonal = [crossed(v, "member", "lev") for v in (other_far, came[1])]
    places = [(group, member), (group, 1 - member), (1 - group, 1 - member), (1 - group, member)]
    weights = weights_of([(g, m, c) for g, m in places for c in (core, 1 - core)])
    near = unpacked((*here, *along_y))
    return balanced(weights, near, (*diagonal, *along_x))


def solution(mesh):
    in_specs = (P("lev", "lat", "lon"), P("lev", "lat", "lon"), P(), P("member"), P("member"))
    out_specs = P("member", ("lat", "lev"), "lon")
    return jax.shard_map(
        per_device, mesh=mesh, in_specs=in_specs, out_specs=out_specs, check_vma=False
    )
```

time: 88.9 us -> 81.7 us (0.919); the launches traced: 88.4 us -> 80.2 us
  starting transfers between devices: 9.93 us -> 24 us
  Pallas kernels: 42.8 us -> 32.1 us
  local copies, waits for them, and re-layouts: 9.62 us -> 3.07 us
  waiting for transfers between devices: 23.2 us -> 19.6 us
  other arithmetic: 1.48 us -> 0 us
    ppermute x7 -> x17, starting transfers between devices: 9.93 us -> 24 us  [the longest x13 13.6 us: crossed(): return lax.ppermute(block, axes, [(i, count - 1 - i) for i in range(count)])]
    pallas_call x3 -> x4, Pallas kernels: 36 us -> 25.6 us  [the longest x1 14.2 us: diffuse(): pl.pallas_call(functools.partial(diffuse_kernel, halo, halves), out_shape...]
    ppermute x7 -> x17, waiting for transfers between devices: 23.2 us -> 19.6 us  [the longest x13 19.6 us: crossed(): return lax.ppermute(block, axes, [(i, count - 1 - i) for i in range(count)])]
    squeeze x2 -> x0, local copies, waits for them, and re-layouts: 2.12 us -> none  [the longest x1 1.28 us: per_device(): far_theirs = crossed(far[1], 'lon')]
    ppermute x2 -> x0, local copies, waits for them, and re-layouts: 2.05 us -> none  [the longest x1 1.04 us: per_device(): bottom = lax.ppermute(edges[:, :, :, :halo], 'lat', backward)]
    dynamic_slice x2 -> x1, local copies, waits for them, and re-layouts: 1.69 us -> 0.15 us  [part(): return lax.dynamic_slice_in_dim(block, index * size, size, axis=axis)]
    another operation x3 -> x0, other arithmetic: 1.38 us -> none  [the longest x1 0.62 us: per_device(): place = jnp.stack([core, core, core, group if groups == 2 else 0 * group])]
    slice x2 -> x0, local copies, waits for them, and re-layouts: 1.03 us -> none  [the longest x1 0.51 us: per_device(): top = lax.ppermute(edges[:, :, :, -halo:], 'lat', onward)]
  transfers between devices with their start and end apart: 7 -> 17, of which waited for: 5 -> 6; matrix products, arithmetic and copies ran while one was open for 4% -> 0% of each run, Pallas kernels for 10% -> 13%
where the time goes in v3:
time: 81.7 us; the launch traced here: 80.2 us
  Pallas kernels  32.1 us (39%)
  starting transfers between devices  24 us (29%)
  waiting for transfers between devices  19.6 us (24%)
  local copies, waits for them, and re-layouts  3.07 us (4%)
  between operations  1.45 us (2%)
    ppermute x13, waiting for transfers between devices, crossed(): return lax.ppermute(block, axes, [(i, count - 1 - i) for i in range(count)])  19.6 us
    pallas_call x1, Pallas kernels, diffuse(): pl.pallas_call(functools.partial(diffuse_kernel, halo, halves), out_shape...  14.2 us
    ppermute x13, starting transfers between devices, crossed(): return lax.ppermute(block, axes, [(i, count - 1 - i) for i in range(count)])  13.6 us
    ppermute x4, starting transfers between devices, shifted(): return lax.ppermute(block, ('lat', 'lon'), route)  10.4 us
    pallas_call x2, Pallas kernels, noise(): pl.pallas_call(functools.partial(noise_kernel, levels_here, halo, total_r...  7.39 us
    pallas_call x1, Pallas kernels, packed_conduct(): pl.pallas_call(functools.partial(conduct_kernel, halo), out_shape=(rows,)...  4.02 us
    pallas_call x1, Pallas kernels, balanced(): pl.pallas_call(balance_kernel, out_shape=jax.ShapeDtypeStruct((total, hei...  3.58 us
    pallas_call x1, Pallas kernels, unpacked(): pl.pallas_call(unpack_kernel, out_shape=jax.ShapeDtypeStruct((sum((p.shap...  2.94 us
  transfers between devices with their start and end apart: 17, of which 6 were waited for; matrix products, arithmetic and copies ran while one was open for 0% of the time, Pallas kernels for 13%

profile of v3, /device:TPU:0, one launch (start us, length us, event | category | flops | bytes accessed | tf_op | source)
XLA Modules:
  0.0 80.2 jit_solution(14434452869041178049)
XLA Ops:
  0.0 4.0 %shard_map.55 = (f32[9,3,32,128]{3,2,1,0:T(8,128)}, f32[9,3,32,128]{3,2,1,0:T(8,128)}, f32[3,112,128]{2,1,0:T(8,128)}, f32[3,112,128]{2,1,0:T(8,128)}, f32[3,112,128]{2,1,0:T(8,128)}, /*index=5*/f32[3,112,128]{2,1,0:T(8,128)}) custom-call(s32[36,32,384]{2,1,0:T(8,128)} %mask_send.1, f32[36,32,384]{2,1,0:T(8,128)} %send_in.1, s32[36,32,384]{2,1,0:T(8,128)} %mask_send.1, ...), custom_call_target="tpu_custom_call" | custom-call | tf_op jit(solution)/shard_map/pallas_call | solution.py:110
  4.6 4.5 %collective-permute-start.1 = (f32[3,112,128]{2,1,0:T(8,128)}, f32[3,112,128]{2,1,0:T(8,128)S(1)}, u32[]{:S(2)}, u32[]{:S(2)}) collective-permute-start(f32[3,112,128]{2,1,0:T(8,128)} %get-tuple-element.21), channel_id=1, source_target_pairs={{0,4},{1,5},{4,8},{5,9},{8,12},{9,13},{2,6},{3,7},{6,10},{7,11},{1... | collective-permute-start | bytes 516104 | tf_op jit(solution)/shard_map/ppermute | solution.py:350
  9.1 3.3 %collective-permute-start.2 = (f32[3,112,128]{2,1,0:T(8,128)}, f32[3,112,128]{2,1,0:T(8,128)S(1)}, u32[]{:S(2)}, u32[]{:S(2)}) collective-permute-start(f32[3,112,128]{2,1,0:T(8,128)} %get-tuple-element.22), channel_id=1, source_target_pairs={{0,5},{1,4},{4,9},{5,8},{8,13},{9,12},{2,7},{3,6},{6,11},{7,10},{1... | collective-permute-start | bytes 516104 | tf_op jit(solution)/shard_map/ppermute | solution.py:350
  12.4 1.3 %collective-permute-start.3 = (f32[3,112,128]{2,1,0:T(8,128)}, f32[3,112,128]{2,1,0:T(8,128)S(1)}, u32[]{:S(2)}, u32[]{:S(2)}) collective-permute-start(f32[3,112,128]{2,1,0:T(8,128)} %get-tuple-element.23), channel_id=1, source_target_pairs={{4,0},{5,1},{8,4},{9,5},{12,8},{13,9},{6,2},{7,3},{10,6},{11,7},{1... | collective-permute-start | bytes 516104 | tf_op jit(solution)/shard_map/ppermute | solution.py:350
  13.7 1.6 %collective-permute-start.5 = (s32[1]{0:T(128)}, s32[1]{0:T(128)}, u32[]{:S(2)}, u32[]{:S(2)}) collective-permute-start(s32[1]{0:T(128)} %param.9), channel_id=1, source_target_pairs={{0,16},{16,0},{1,17},{17,1},{2,18},{18,2},{3,19},{19,3},{4,20},{20... | collective-permute-start | bytes 20 | tf_op jit(solution)/shard_map/ppermute | solution.py:341
  15.3 2.1 %collective-permute-done.5.key = s32[1]{0:T(128)} collective-permute-done((s32[1]{0:T(128)}, s32[1]{0:T(128)}, u32[]{:S(2)}, u32[]{:S(2)}) %collective-permute-start.5) | collective-permute-done | bytes 36 | tf_op jit(solution)/shard_map/ppermute | solution.py:341
  17.4 1.5 %collective-permute-start.6 = (s32[1]{0:T(128)}, s32[1]{0:T(128)}, u32[]{:S(2)}, u32[]{:S(2)}) collective-permute-start(s32[1]{0:T(128)} %param.8), channel_id=1, source_target_pairs={{0,16},{16,0},{1,17},{17,1},{2,18},{18,2},{3,19},{19,3},{4,20},{20... | collective-permute-start | bytes 20 | tf_op jit(solution)/shard_map/ppermute | solution.py:341
  18.9 2.3 %collective-permute-done.6.member = s32[1]{0:T(128)} collective-permute-done((s32[1]{0:T(128)}, s32[1]{0:T(128)}, u32[]{:S(2)}, u32[]{:S(2)}) %collective-permute-start.6) | collective-permute-done | bytes 36 | tf_op jit(solution)/shard_map/ppermute | solution.py:341
  21.1 1.3 %collective-permute-start.4 = (f32[3,112,128]{2,1,0:T(8,128)}, f32[3,112,128]{2,1,0:T(8,128)S(1)}, u32[]{:S(2)}, u32[]{:S(2)}) collective-permute-start(f32[3,112,128]{2,1,0:T(8,128)} %get-tuple-element.24), channel_id=1, source_target_pairs={{4,1},{5,0},{8,5},{9,4},{12,9},{13,8},{6,3},{7,2},{10,7},{11,6},{1... | collective-permute-start | bytes 516104 | tf_op jit(solution)/shard_map/ppermute | solution.py:350
  23.7 3.1 %shard_map.57.own_source = f32[9,6,7,8,128]{4,3,2,1,0:T(8,128)} custom-call(s32[1]{0:T(128)S(6)} %copy.7.key, s32[1]{0:T(128)S(6)} %copy.6.member), custom_call_target="tpu_custom_call" | custom-call | tf_op jit(solution)/shard_map/pallas_call | solution.py:139
  26.8 4.3 %shard_map.56.other_source = f32[9,6,7,8,128]{4,3,2,1,0:T(8,128)} custom-call(s32[1]{0:T(128)} %collective-permute-done.5.key, s32[1]{0:T(128)} %collective-permute-done.6.member), custom_call_target="tpu_custom_call" | custom-call | tf_op jit(solution)/shard_map/pallas_call | solution.py:139
  32.1 14.2 %shard_map.58 = (f32[9,3,16,128]{3,2,1,0:T(8,128)}, f32[9,3,16,128]{3,2,1,0:T(8,128)}, f32[9,3,16,128]{3,2,1,0:T(8,128)}, f32[9,3,16,128]{3,2,1,0:T(8,128)}, f32...) custom-call(f32[9,3,32,128]{3,2,1,0:T(8,128)} %get-tuple-element.19.m, ...), custom_call_target="tpu_custom_call" | custom-call | tf_op jit(solution)/shard_map/pallas_call | solution.py:263
  46.8 1.5 %collective-permute-start.8 = (f32[9,3,16,128]{3,2,1,0:T(8,128)}, f32[9,3,16,128]{3,2,1,0:T(8,128)S(1)}, u32[]{:S(2)}, u32[]{:S(2)}) collective-permute-start(f32[9,3,16,128]{3,2,1,0:T(8,128)} %get-tuple-element.27), channel_id=1, source_target_pairs={{0,16},{16,0},{1,17},{17,1},{2,18},{18,2},{3,19},{19,3},{4,20},{20... | collective-permute-start | bytes 663560 | tf_op jit(solution)/shard_map/ppermute | solution.py:341
  48.9 1.6 %collective-permute-start.11 = (f32[9,3,16,128]{3,2,1,0:T(8,128)}, f32[9,3,16,128]{3,2,1,0:T(8,128)S(1)}, u32[]{:S(2)}, u32[]{:S(2)}) collective-permute-start(f32[9,3,16,128]{3,2,1,0:T(8,128)} %get-tuple-element.29), channel_id=1, source_target_pairs={{0,18},{2,16},{16,2},{18,0},{1,19},{3,17},{17,3},{19,1},{4,22},{6,... | collective-permute-start | bytes 663560 | tf_op jit(solution)/shard_map/ppermute | solution.py:341
  50.5 1.4 %collective-permute-start.10 = (f32[9,3,16,128]{3,2,1,0:T(8,128)S(1)}, f32[9,3,16,128]{3,2,1,0:T(8,128)S(1)}, u32[]{:S(2)}, u32[]{:S(2)}) collective-permute-start(f32[9,3,16,128]{3,2,1,0:T(8,128)S(1)} %collective-permute-done.9), channel_id=1, source_target_pairs={{0,16},{16,0},{1,17},{17,1},{2,18},{18,2},{3,19},{19,3},{4,20},{20... | collective-permute-start | bytes 663560 | tf_op jit(solution)/shard_map/ppermute | solution.py:341
  51.8 8.2 %collective-permute-done.8.refs_2_ = f32[9,3,16,128]{3,2,1,0:T(8,128)S(1)} collective-permute-done((f32[9,3,16,128]{3,2,1,0:T(8,128)}, f32[9,3,16,128]{3,2,1,0:T(8,128)S(1)}, u32[]{:S(2)}, u32[]{:S(2)}) %collective-permute-start.8) | collective-permute-done | bytes 221216 | tf_op jit(solution)/shard_map/ppermute | solution.py:341
  60.1 1.5 %collective-permute-start.14 = (f32[9,3,16,128]{3,2,1,0:T(8,128)}, f32[9,3,16,128]{3,2,1,0:T(8,128)S(1)}, u32[]{:S(2)}, u32[]{:S(2)}) collective-permute-start(f32[9,3,16,128]{3,2,1,0:T(8,128)} %get-tuple-element.31), channel_id=1, source_target_pairs={{0,2},{2,0},{1,3},{3,1},{4,6},{6,4},{5,7},{7,5},{8,10},{10,8},{9,1... | collective-permute-start | bytes 663560 | tf_op jit(solution)/shard_map/ppermute | solution.py:341
  61.6 1.5 %collective-permute-start.13 = (f32[9,3,16,128]{3,2,1,0:T(8,128)S(1)}, f32[9,3,16,128]{3,2,1,0:T(8,128)S(1)}, u32[]{:S(2)}, u32[]{:S(2)}) collective-permute-start(f32[9,3,16,128]{3,2,1,0:T(8,128)S(1)} %collective-permute-done.12), channel_id=1, source_target_pairs={{0,18},{2,16},{16,2},{18,0},{1,19},{3,17},{17,3},{19,1},{4,22},{6,... | collective-permute-start | bytes 663560 | tf_op jit(solution)/shard_map/ppermute | solution.py:341
  63.0 1.5 %collective-permute-start.16 = (f32[9,3,16,128]{3,2,1,0:T(8,128)S(1)}, f32[9,3,16,128]{3,2,1,0:T(8,128)S(1)}, u32[]{:S(2)}, u32[]{:S(2)}) collective-permute-start(f32[9,3,16,128]{3,2,1,0:T(8,128)S(1)} %collective-permute-done.15), channel_id=1, source_target_pairs={{0,2},{2,0},{1,3},{3,1},{4,6},{6,4},{5,7},{7,5},{8,10},{10,8},{9,1... | collective-permute-start | bytes 663560 | tf_op jit(solution)/shard_map/ppermute | solution.py:341
  65.5 2.9 %shard_map.59.near = f32[36,3,16,128]{3,2,1,0:T(8,128)} custom-call(f32[9,3,16,128]{3,2,1,0:T(8,128)} %get-tuple-element.25.refs_0_, f32[9,3,16,128]{3,2,1,0:T(8,128)} %copy-done.3, f32[9,3,16,128]{3,2,1,0:T(8,128)} %copy-done.4, f32[9,3,16,128]{3,2,1,0:T(8,128)} %copy-done.5), custom_call_target="tpu_custom_call" | custom-call | tf_op jit(solution)/shard_map/pallas_call | solution.py:292
  68.6 5.4 %collective-permute-done.13.refs_1_ = f32[9,3,16,128]{3,2,1,0:T(8,128)S(1)} collective-permute-done((f32[9,3,16,128]{3,2,1,0:T(8,128)S(1)}, f32[9,3,16,128]{3,2,1,0:T(8,128)S(1)}, u32[]{:S(2)}, u32[]{:S(2)}) %collective-permute-start.13) | collective-permute-done | bytes 221216 | tf_op jit(solution)/shard_map/ppermute | solution.py:341
  74.0 1.4 %collective-permute-done.16.refs_3_ = f32[9,3,16,128]{3,2,1,0:T(8,128)S(1)} collective-permute-done((f32[9,3,16,128]{3,2,1,0:T(8,128)S(1)}, f32[9,3,16,128]{3,2,1,0:T(8,128)S(1)}, u32[]{:S(2)}, u32[]{:S(2)}) %collective-permute-start.16) | collective-permute-done | bytes 221216 | tf_op jit(solution)/shard_map/ppermute | solution.py:341
  75.4 1.2 %copy-done = f32[36,3,16,128]{3,2,1,0:T(8,128)S(1)} copy-done((f32[36,3,16,128]{3,2,1,0:T(8,128)S(1)}, f32[36,3,16,128]{3,2,1,0:T(8,128)}, u32[]{:S(2)}) %copy-start) | copy-done | bytes 884760
  76.6 3.6 %shard_map.60 = f32[72,16,384]{2,1,0:T(8,128)} custom-call(f32[72,72]{1,0:T(8,128)S(1)} %concatenate.3.weights, f32[36,3,16,128]{3,2,1,0:T(8,128)S(1)} %copy-done, f32[9,3,16,128]{3,2,1,0:T(8,128)S(1)} %collective-permute-done.11.refs_0_, f32[9,3,16,128]{3,2,1,0:T(8,128)S(1)} %collective-permute-done.13.refs_1_, ...), custom_call_target="tpu_custom_call" | custom-call | tf_op jit(solution)/shard_map/pallas_call | solution.py:326
  (38 shorter events, 3.6 us)
Async XLA Ops:
  4.0 27.2 %collective-permute-start = (f32[9,3,32,128]{3,2,1,0:T(8,128)}, f32[9,3,32,128]{3,2,1,0:T(8,128)S(1)}, u32[]{:S(2)}, u32[]{:S(2)}) collective-permute-start(f32[9,3,32,128]{3,2,1,0:T(8,128)} %get-tuple-element.20), channel_id=1, source_target_pairs={{0,1},{1,0},{2,3},{3,2},{4,5},{5,4},{6,7},{7,6},{8,9},{9,8},{10,11... | collective-permute-start | bytes 1327112 | tf_op jit(solution)/shard_map/ppermute | solution.py:341
  4.6 26.6 %collective-permute-start.1 = (f32[3,112,128]{2,1,0:T(8,128)}, f32[3,112,128]{2,1,0:T(8,128)S(1)}, u32[]{:S(2)}, u32[]{:S(2)}) collective-permute-start(f32[3,112,128]{2,1,0:T(8,128)} %get-tuple-element.21), channel_id=1, source_target_pairs={{0,4},{1,5},{4,8},{5,9},{8,12},{9,13},{2,6},{3,7},{6,10},{7,11},{1... | collective-permute-start | bytes 516104 | tf_op jit(solution)/shard_map/ppermute | solution.py:350
  9.1 22.1 %collective-permute-start.2 = (f32[3,112,128]{2,1,0:T(8,128)}, f32[3,112,128]{2,1,0:T(8,128)S(1)}, u32[]{:S(2)}, u32[]{:S(2)}) collective-permute-start(f32[3,112,128]{2,1,0:T(8,128)} %get-tuple-element.22), channel_id=1, source_target_pairs={{0,5},{1,4},{4,9},{5,8},{8,13},{9,12},{2,7},{3,6},{6,11},{7,10},{1... | collective-permute-start | bytes 516104 | tf_op jit(solution)/shard_map/ppermute | solution.py:350
  12.4 18.8 %collective-permute-start.3 = (f32[3,112,128]{2,1,0:T(8,128)}, f32[3,112,128]{2,1,0:T(8,128)S(1)}, u32[]{:S(2)}, u32[]{:S(2)}) collective-permute-start(f32[3,112,128]{2,1,0:T(8,128)} %get-tuple-element.23), channel_id=1, source_target_pairs={{4,0},{5,1},{8,4},{9,5},{12,8},{13,9},{6,2},{7,3},{10,6},{11,7},{1... | collective-permute-start | bytes 516104 | tf_op jit(solution)/shard_map/ppermute | solution.py:350
  13.7 3.7 %collective-permute-start.5 = (s32[1]{0:T(128)}, s32[1]{0:T(128)}, u32[]{:S(2)}, u32[]{:S(2)}) collective-permute-start(s32[1]{0:T(128)} %param.9), channel_id=1, source_target_pairs={{0,16},{16,0},{1,17},{17,1},{2,18},{18,2},{3,19},{19,3},{4,20},{20... | collective-permute-start | bytes 20 | tf_op jit(solution)/shard_map/ppermute | solution.py:341
  17.4 3.8 %collective-permute-start.6 = (s32[1]{0:T(128)}, s32[1]{0:T(128)}, u32[]{:S(2)}, u32[]{:S(2)}) collective-permute-start(s32[1]{0:T(128)} %param.8), channel_id=1, source_target_pairs={{0,16},{16,0},{1,17},{17,1},{2,18},{18,2},{3,19},{19,3},{4,20},{20... | collective-permute-start | bytes 20 | tf_op jit(solution)/shard_map/ppermute | solution.py:341
  21.1 10.0 %collective-permute-start.4 = (f32[3,112,128]{2,1,0:T(8,128)}, f32[3,112,128]{2,1,0:T(8,128)S(1)}, u32[]{:S(2)}, u32[]{:S(2)}) collective-permute-start(f32[3,112,128]{2,1,0:T(8,128)} %get-tuple-element.24), channel_id=1, source_target_pairs={{4,1},{5,0},{8,5},{9,4},{12,9},{13,8},{6,3},{7,2},{10,7},{11,6},{1... | collective-permute-start | bytes 516104 | tf_op jit(solution)/shard_map/ppermute | solution.py:350
  31.1 0.8 copy-start.8
  31.2 0.8 %copy-start.9 = (f32[3,112,128]{2,1,0:T(8,128)}, f32[3,112,128]{2,1,0:T(8,128)S(1)}, u32[]{:S(2)}) copy-start(f32[3,112,128]{2,1,0:T(8,128)S(1)} %collective-permute-done.4.bottom_theirs) | copy-start | bytes 516100
  31.2 0.9 %copy-start.2 = (f32[9,3,32,128]{3,2,1,0:T(8,128)}, f32[9,3,32,128]{3,2,1,0:T(8,128)S(1)}, u32[]{:S(2)}) copy-start(f32[9,3,32,128]{3,2,1,0:T(8,128)S(1)} %collective-permute-done.theirs) | copy-start | bytes 1327108
  32.1 32.4 %copy-start.1 = (f32[72,72]{1,0:T(8,128)S(1)}, f32[72,72]{1,0:T(8,128)}, u32[]{:S(2)}) copy-start(f32[72,72]{1,0:T(8,128)} %param.7) | copy-start | bytes 62212
  46.3 2.5 %collective-permute-start.9 = (f32[9,3,16,128]{3,2,1,0:T(8,128)}, f32[9,3,16,128]{3,2,1,0:T(8,128)S(1)}, u32[]{:S(2)}, u32[]{:S(2)}) collective-permute-start(f32[9,3,16,128]{3,2,1,0:T(8,128)} %get-tuple-element.28), channel_id=1, source_target_pairs={{0,1},{1,0},{2,3},{3,2},{4,5},{5,4},{6,7},{7,6},{8,9},{9,8},{10,11... | collective-permute-start | bytes 663560 | tf_op jit(solution)/shard_map/ppermute | solution.py:341
  46.3 4.1 %collective-permute-start.7 = (f32[9,3,16,128]{3,2,1,0:T(8,128)}, f32[9,3,16,128]{3,2,1,0:T(8,128)S(1)}, u32[]{:S(2)}, u32[]{:S(2)}) collective-permute-start(f32[9,3,16,128]{3,2,1,0:T(8,128)} %get-tuple-element.26), channel_id=1, source_target_pairs={{0,1},{1,0},{2,3},{3,2},{4,5},{5,4},{6,7},{7,6},{8,9},{9,8},{10,11... | collective-permute-start | bytes 663560 | tf_op jit(solution)/shard_map/ppermute | solution.py:341
  46.8 13.2 %collective-permute-start.8 = (f32[9,3,16,128]{3,2,1,0:T(8,128)}, f32[9,3,16,128]{3,2,1,0:T(8,128)S(1)}, u32[]{:S(2)}, u32[]{:S(2)}) collective-permute-start(f32[9,3,16,128]{3,2,1,0:T(8,128)} %get-tuple-element.27), channel_id=1, source_target_pairs={{0,16},{16,0},{1,17},{17,1},{2,18},{18,2},{3,19},{19,3},{4,20},{20... | collective-permute-start | bytes 663560 | tf_op jit(solution)/shard_map/ppermute | solution.py:341
  48.3 13.2 %collective-permute-start.12 = (f32[9,3,16,128]{3,2,1,0:T(8,128)}, f32[9,3,16,128]{3,2,1,0:T(8,128)S(1)}, u32[]{:S(2)}, u32[]{:S(2)}) collective-permute-start(f32[9,3,16,128]{3,2,1,0:T(8,128)} %get-tuple-element.30), channel_id=1, source_target_pairs={{0,1},{1,0},{2,3},{3,2},{4,5},{5,4},{6,7},{7,6},{8,9},{9,8},{10,11... | collective-permute-start | bytes 663560 | tf_op jit(solution)/shard_map/ppermute | solution.py:341
  48.3 14.7 %collective-permute-start.15 = (f32[9,3,16,128]{3,2,1,0:T(8,128)}, f32[9,3,16,128]{3,2,1,0:T(8,128)S(1)}, u32[]{:S(2)}, u32[]{:S(2)}) collective-permute-start(f32[9,3,16,128]{3,2,1,0:T(8,128)} %get-tuple-element.32), channel_id=1, source_target_pairs={{0,1},{1,0},{2,3},{3,2},{4,5},{5,4},{6,7},{7,6},{8,9},{9,8},{10,11... | collective-permute-start | bytes 663560 | tf_op jit(solution)/shard_map/ppermute | solution.py:341
  48.9 19.6 %collective-permute-start.11 = (f32[9,3,16,128]{3,2,1,0:T(8,128)}, f32[9,3,16,128]{3,2,1,0:T(8,128)S(1)}, u32[]{:S(2)}, u32[]{:S(2)}) collective-permute-start(f32[9,3,16,128]{3,2,1,0:T(8,128)} %get-tuple-element.29), channel_id=1, source_target_pairs={{0,18},{2,16},{16,2},{18,0},{1,19},{3,17},{17,3},{19,1},{4,22},{6,... | collective-permute-start | bytes 663560 | tf_op jit(solution)/shard_map/ppermute | solution.py:341
  50.5 14.4 %copy-start.3 = (f32[9,3,16,128]{3,2,1,0:T(8,128)}, f32[9,3,16,128]{3,2,1,0:T(8,128)S(1)}, u32[]{:S(2)}) copy-start(f32[9,3,16,128]{3,2,1,0:T(8,128)S(1)} %collective-permute-done.7.refs_1_) | copy-start | bytes 663556
  50.5 14.4 %collective-permute-start.10 = (f32[9,3,16,128]{3,2,1,0:T(8,128)S(1)}, f32[9,3,16,128]{3,2,1,0:T(8,128)S(1)}, u32[]{:S(2)}, u32[]{:S(2)}) collective-permute-start(f32[9,3,16,128]{3,2,1,0:T(8,128)S(1)} %collective-permute-done.9), channel_id=1, source_target_pairs={{0,16},{16,0},{1,17},{17,1},{2,18},{18,2},{3,19},{19,3},{4,20},{20... | collective-permute-start | bytes 663560 | tf_op jit(solution)/shard_map/ppermute | solution.py:341
  60.1 4.8 %copy-start.4 = (f32[9,3,16,128]{3,2,1,0:T(8,128)}, f32[9,3,16,128]{3,2,1,0:T(8,128)S(1)}, u32[]{:S(2)}) copy-start(f32[9,3,16,128]{3,2,1,0:T(8,128)S(1)} %collective-permute-done.8.refs_2_) | copy-start | bytes 663556
  60.1 8.6 %collective-permute-start.14 = (f32[9,3,16,128]{3,2,1,0:T(8,128)}, f32[9,3,16,128]{3,2,1,0:T(8,128)S(1)}, u32[]{:S(2)}, u32[]{:S(2)}) collective-permute-start(f32[9,3,16,128]{3,2,1,0:T(8,128)} %get-tuple-element.31), channel_id=1, source_target_pairs={{0,2},{2,0},{1,3},{3,1},{4,6},{6,4},{5,7},{7,5},{8,10},{10,8},{9,1... | collective-permute-start | bytes 663560 | tf_op jit(solution)/shard_map/ppermute | solution.py:341
  61.6 12.4 %collective-permute-start.13 = (f32[9,3,16,128]{3,2,1,0:T(8,128)S(1)}, f32[9,3,16,128]{3,2,1,0:T(8,128)S(1)}, u32[]{:S(2)}, u32[]{:S(2)}) collective-permute-start(f32[9,3,16,128]{3,2,1,0:T(8,128)S(1)} %collective-permute-done.12), channel_id=1, source_target_pairs={{0,18},{2,16},{16,2},{18,0},{1,19},{3,17},{17,3},{19,1},{4,22},{6,... | collective-permute-start | bytes 663560 | tf_op jit(solution)/shard_map/ppermute | solution.py:341
  63.0 12.4 %collective-permute-start.16 = (f32[9,3,16,128]{3,2,1,0:T(8,128)S(1)}, f32[9,3,16,128]{3,2,1,0:T(8,128)S(1)}, u32[]{:S(2)}, u32[]{:S(2)}) collective-permute-start(f32[9,3,16,128]{3,2,1,0:T(8,128)S(1)} %collective-permute-done.15), channel_id=1, source_target_pairs={{0,2},{2,0},{1,3},{3,1},{4,6},{6,4},{5,7},{7,5},{8,10},{10,8},{9,1... | collective-permute-start | bytes 663560 | tf_op jit(solution)/shard_map/ppermute | solution.py:341
  75.4 1.2 %copy-start = (f32[36,3,16,128]{3,2,1,0:T(8,128)S(1)}, f32[36,3,16,128]{3,2,1,0:T(8,128)}, u32[]{:S(2)}) copy-start(f32[36,3,16,128]{3,2,1,0:T(8,128)} %shard_map.59.near) | copy-start | bytes 2654212
  (3 other events, 2.1 us)

commit v4 on v3

--- a/solution.py
+++ b/solution.py
@@ -16,6 +16,10 @@
 VMEM = pltpu.VMEM
 whole = functools.partial(pl.BlockSpec, memory_space=pltpu.VMEM)
 scalars = functools.partial(pl.BlockSpec, memory_space=pltpu.SMEM)
+
+
+def budget(mebibytes):
+    return pltpu.CompilerParams(vmem_limit_bytes=mebibytes << 20)
 
 
 def scramble(values):
@@ -115,33 +119,36 @@
         out_specs=[pl.BlockSpec((some, pairs, height, LANES), lambda l: (l, 0, 0, 0))] * 2
         + [pl.BlockSpec((1, extent, LANES), lambda l: (l, 0, 0))] * 4,
         scratch_shapes=[VMEM((width, width), jnp.bfloat16)],
+        compiler_params=budget(12),
     )(mask, diffusivity, mask, diffusivity)
 
 
-def noise_kernel(levels_here, halo, total_rows, total_cols, key, member, out):
-    levels, tiles, pitch = out.shape[:3]
-    base = key[0] * 69069 + member[0] * 362437
+def noise_kernel(levels_here, halo, total_rows, total_cols, other, own, out):
+    _, levels, tiles, pitch = out.shape[:4]
     level0 = lax.axis_index("lev") * levels_here + quarter(True) * levels
     row0 = lax.axis_index("lat") * (total_rows // lax.axis_size("lat")) - halo
     sub = lax.broadcasted_iota(jnp.int32, (SUB, LANES), 0)
     lane = lax.broadcasted_iota(jnp.int32, (SUB, LANES), 1)
     within = sub * (pitch * total_cols) + lane * tiles
+    bases = [ids[0] * 69069 + ids[1] * 362437 for ids in (other, own)]
 
     @pl.loop(0, levels)
     def _(l):
         start = ((level0 + l) * total_rows + row0) * total_cols
-        for t in range(tiles):
-            for k in range(pitch):
-                out[l, t, k] = draw(within + (start + k * total_cols + t), base)
-
-
-def noise(key, member, levels_here, halo, shape, total_rows, total_cols):
+        for i, base in enumerate(bases):
+            for t in range(tiles):
+                for k in range(pitch):
+                    out[i, l, t, k] = draw(within + (start + k * total_cols + t), base)
+
+
+def noise(other, own, levels_here, halo, shape, total_rows, total_cols):
     return pl.pallas_call(
         functools.partial(noise_kernel, levels_here, halo, total_rows, total_cols),
-        out_shape=jax.ShapeDtypeStruct(shape, jnp.float32),
+        out_shape=jax.ShapeDtypeStruct((2, *shape), jnp.float32),
         in_specs=[scalars()] * 2,
         out_specs=whole(),
-    )(key, member)
+        compiler_params=budget(8),
+    )(other, own)
 
 
 def neighbour_sums(old, tiles, pitch, emit):
@@ -171,10 +178,9 @@
 
 
 def diffuse_kernel(halo, halves, mine, theirs, top_mine, top_theirs, bottom_mine, bottom_theirs,
-                   other_source, own_source, *refs):
-    outs, (rows, cond, gain, push, inv, u0, u1, res) = refs[:8], refs[8:]
-    sources = (other_source, own_source)
-    levels, tiles, pitch = own_source.shape[:3]
+                   source, *refs):
+    *kept, sent, rows, cond, gain, push, inv, u0, u1, res = refs
+    _, levels, tiles, pitch = source.shape[:4]
     pairs, height = mine.shape[1], mine.shape[2]
     final = height // 2
     core = lax.axis_index("lon")
@@ -215,8 +221,8 @@
             q = c * r
             inv[g, t, k] = r
             gain[g, t, k] = q * c
-            for i, source in enumerate(sources):
-                s = source[block * some + g, t, k]
+            for i in range(2):
+                s = source[i, block * some + g, t, k]
                 push[i * some + g, t, k] = q * s
                 u0[i * some + g, t, k] = c * s
 
@@ -231,7 +237,7 @@
 
         def finish(g, t, k, value, total):
             i, g = divmod(g, some)
-            c, s = cond[g, t, k], sources[i][block * some + g, t, k]
+            c, s = cond[g, t, k], source[i, block * some + g, t, k]
             value = jnp.where(c != 0.0, (s + c * total) * inv[g, t, k], 0.0)
             res[i * some + g, t, pl.ds(k, SUB, stride=pitch), :] = value
 
@@ -239,14 +245,15 @@
         left = on_left((height, LANES))
         first = group == 0
         for i in range(2):
-            near, far, near_send, far_send = outs[4 * i : 4 * i + 4]
             for g in range(some):
                 l = block * some + g
                 for v in range(pairs):
                     a = res[i * some + g, v, pl.ds(halo, height), :]
                     b = pltpu.roll(res[i * some + g, v + pairs, pl.ds(halo, height), :], HALF, 1)
                     keep, send = jnp.where(left, a, b), jnp.where(left, b, a)
-                    for value, close, away in ((keep, near, far), (send, near_send, far_send)):
+                    for value, close, away in (
+                        (keep, kept[2 * i], kept[2 * i + 1]), (send, sent.at[2 * i], sent.at[2 * i + 1]),
+                    ):
                         upper, lower = value[:final], value[final:]
                         close[l, v] = jnp.where(first, upper, lower)
                         away[l, v] = jnp.where(first, lower, upper)
@@ -254,7 +261,7 @@
 
 def diffuse(halo, halves, *operands):
     levels, pairs, height, _ = operands[0].shape
-    tiles, pitch = operands[-1].shape[1:3]
+    tiles, pitch = operands[-1].shape[2:4]
     some = math.gcd(levels, SOME)
     tile = VMEM((some, tiles, pitch, SUB, LANES), jnp.float32)
     both = VMEM((2 * some, tiles, pitch, SUB, LANES), jnp.float32)
@@ -262,15 +269,16 @@
     result = jax.ShapeDtypeStruct((levels, pairs, height // 2, LANES), jnp.float32)
     return pl.pallas_call(
         functools.partial(diffuse_kernel, halo, halves),
-        out_shape=(result,) * 8,
+        out_shape=(result,) * 4 + (jax.ShapeDtypeStruct((4, *result.shape), jnp.float32),),
         in_specs=[whole()] * len(operands),
-        out_specs=(whole(),) * 8,
+        out_specs=(whole(),) * 5,
         scratch_shapes=[line, tile, tile, both, tile, both, both, line],
+        compiler_params=budget(18),
     )(*operands)
 
 
 def unpack(pieces, matrix, out, start):
-    for piece in pieces:
+    for piece in (p.at[i] for p in pieces for i in range(2)):
         levels, tiles, height, _ = piece.shape
         values = jnp.concatenate(
             [piece[:, t].reshape(levels * height, LANES) for t in range(tiles)], axis=1
@@ -283,17 +291,18 @@
 
 def unpack_kernel(*refs):
     *pieces, out = refs
-    tiles = pieces[0].shape[1]
+    tiles = pieces[0].shape[2]
     unpack(pieces, packing(tiles * LANES, 2 * tiles, lax.axis_index("lon"), 0), out, 0)
 
 
 def unpacked(pieces):
-    levels, tiles, height, _ = pieces[0].shape
+    _, levels, tiles, height, _ = pieces[0].shape
     return pl.pallas_call(
         unpack_kernel,
-        out_shape=jax.ShapeDtypeStruct((sum(p.shape[0] for p in pieces), tiles, height, LANES), jnp.float32),
+        out_shape=jax.ShapeDtypeStruct((2 * len(pieces) * levels, tiles, height, LANES), jnp.float32),
         in_specs=[whole()] * len(pieces),
         out_specs=whole(),
+        compiler_params=budget(8),
     )(*pieces)
 
 
@@ -332,7 +341,7 @@
             VMEM((count, tiles, height, LANES), jnp.float32),
             VMEM((total * tiles * height, LANES), jnp.float32),
         ],
-        compiler_params=pltpu.CompilerParams(vmem_limit_bytes=48 << 20),
+        compiler_params=budget(12),
     )(weights, near, *pieces)
 
 
@@ -356,7 +365,7 @@
 
 def gathered(kept, came, weights_of):
     core, member, groups = (lax.axis_index("lon"), lax.axis_index("member"), lax.axis_size("lev"))
-    halves = [jnp.concatenate(half, axis=2) for half in (kept[2:], came[2:], kept[:2], came[:2])]
+    halves = [jnp.concatenate([*half], axis=2) for half in (kept[2:], came[2:], kept[:2], came[:2])]
     rows = jnp.concatenate([jnp.stack(halves[:2]), crossed(jnp.stack(halves[2:]), "member")])
     pieces = lax.all_to_all(rows, "lev", split_axis=3, concat_axis=0, tiled=True)
     count, share, tiles, height, _ = pieces.shape
@@ -381,32 +390,33 @@
     if spare:
         land_mask, diffusivity = (jnp.pad(v, ((0, spare), (0, 0), (0, 0))) for v in (land_mask, diffusivity))
     mine, send, top, top_cross, bottom, bottom_cross = packed_conduct(halo, share, land_mask, diffusivity)
+    ids = jnp.concatenate([counter_key, member_id])
+    other_ids = crossed(ids, "member")
+    top, other_ids = lax.optimization_barrier((top, other_ids))
     top, bottom = shifted(top, 1, False), shifted(bottom, -1, False)
     top_cross, bottom_cross = shifted(top_cross, 1, True), shifted(bottom_cross, -1, True)
     theirs = crossed(send, "lon")
     tiles = breadth * cores // LANES
     sizes = (levels, halo, (share, tiles, pitch, SUB, LANES), height * strips, breadth * cores)
-    own = noise(counter_key, member_id, *sizes)
-    other = noise(crossed(counter_key, "member"), crossed(member_id, "member"), *sizes)
-    outs = diffuse(halo, groups == 2, mine, theirs, top, top_cross, bottom, bottom_cross, other, own)
+    source = noise(other_ids, ids, *sizes)
+    *kept, sent = diffuse(halo, groups == 2, mine, theirs, top, top_cross, bottom, bottom_cross, source)
 
     def weights_of(order):
         padded = jnp.pad(balance.reshape(-1, groups, levels), ((0, 0), (0, 0), (0, spare)))
         padded = padded.reshape(-1, groups * 4 * share)
         return jnp.concatenate([part(padded, g * 4 + m * 2 + c, share, 1) for g, m, c in order], axis=1)
 
-    other_near, other_far, other_near_send, other_far_send, near, far, near_send, far_send = outs
-    came = [crossed(v, "lon") for v in (other_near_send, other_far_send, near_send, far_send)]
+    came = crossed(sent, "lon")
     if groups != 2:
-        return gathered((other_near, other_far, near, far), came, weights_of)
-    here = (near, came[2])
-    along_x = [crossed(v, "lev") for v in (far, came[3])]
-    along_y = [crossed(v, "member") for v in (other_near, came[0])]
-    diagonal = [crossed(v, "member", "lev") for v in (other_far, came[1])]
+        return gathered(kept, came, weights_of)
+    other_near, other_far, near, far = (jnp.stack([a, b]) for a, b in zip(kept, came))
+    diagonal = crossed(other_far, "member", "lev")
+    along_x = crossed(far, "lev")
+    along_y = crossed(other_near, "member")
     places = [(group, member), (group, 1 - member), (1 - group, 1 - member), (1 - group, member)]
     weights = weights_of([(g, m, c) for g, m in places for c in (core, 1 - core)])
-    near = unpacked((*here, *along_y))
-    return balanced(weights, near, (*diagonal, *along_x))
+    near = unpacked((near, along_y))
+    return balanced(weights, near, (diagonal, along_x))
 
 
 def solution(mesh):

time: 81.7 us -> 63.9 us (0.78); the launches traced: 80.2 us -> 63.6 us
  Pallas kernels: 32.1 us -> 20.2 us
  starting transfers between devices: 24 us -> 17.9 us
  waiting for transfers between devices: 19.6 us -> 20.6 us
    ppermute x13 -> x6, starting transfers between devices: 13.6 us -> 6.8 us  [crossed(): return lax.ppermute(block, axes, [(i, count - 1 - i) for i in range(count)])]
    pallas_call x1, Pallas kernels: 14.2 us -> 10.6 us  [diffuse(): pl.pallas_call(functools.partial(diffuse_kernel, halo, halves), out_shape...]
    pallas_call x2 -> x1, Pallas kernels: 7.39 us -> 4.17 us  [noise(): pl.pallas_call(functools.partial(noise_kernel, levels_here, halo, total_r...]
    pallas_call x1, Pallas kernels: 4.02 us -> 1.14 us  [packed_conduct(): pl.pallas_call(functools.partial(conduct_kernel, halo), out_shape=(rows,)...]
    pallas_call x1, Pallas kernels: 2.94 us -> 0.77 us  [unpacked(): pl.pallas_call(unpack_kernel, out_shape=jax.ShapeDtypeStruct((2 * len(pie...]
    ppermute x13 -> x6, waiting for transfers between devices: 19.6 us -> 20.6 us  [crossed(): return lax.ppermute(block, axes, [(i, count - 1 - i) for i in range(count)])]
    unnamed x20 -> x6, local copies, waits for them, and re-layouts: 2.77 us -> 2.96 us
  transfers between devices with their start and end apart: 17 -> 10, of which waited for: 6 -> 4; matrix products, arithmetic and copies ran while one was open for 0% -> 1% of each run, Pallas kernels for 13% -> 8%
where the time goes in v4:
time: 63.9 us; the launch traced here: 63.6 us
  waiting for transfers between devices  20.6 us (32%)
  Pallas kernels  20.2 us (32%)
  starting transfers between devices  17.9 us (28%)
  local copies, waits for them, and re-layouts  3.31 us (5%)
  between operations  1.46 us (2%)
    ppermute x6, waiting for transfers between devices, crossed(): return lax.ppermute(block, axes, [(i, count - 1 - i) for i in range(count)])  20.6 us
    ppermute x4, starting transfers between devices, shifted(): return lax.ppermute(block, ('lat', 'lon'), route)  11.1 us
    pallas_call x1, Pallas kernels, diffuse(): pl.pallas_call(functools.partial(diffuse_kernel, halo, halves), out_shape...  10.6 us
    ppermute x6, starting transfers between devices, crossed(): return lax.ppermute(block, axes, [(i, count - 1 - i) for i in range(count)])  6.8 us
    pallas_call x1, Pallas kernels, noise(): pl.pallas_call(functools.partial(noise_kernel, levels_here, halo, total_r...  4.17 us
    pallas_call x1, Pallas kernels, balanced(): pl.pallas_call(balance_kernel, out_shape=jax.ShapeDtypeStruct((total, hei...  3.57 us
    unnamed x6, local copies, waits for them, and re-layouts  2.96 us
  transfers between devices with their start and end apart: 10, of which 4 were waited for; matrix products, arithmetic and copies ran while one was open for 1% of the time, Pallas kernels for 8%

profile of v4, /device:TPU:0, one launch (start us, length us, event | category | flops | bytes accessed | tf_op | source)
XLA Modules:
  0.0 63.6 jit_solution(8993281156639452210)
XLA Ops:
  0.0 1.5 %copy-done = s32[36,32,384]{2,1,0:T(8,128)S(1)} copy-done((s32[36,32,384]{2,1,0:T(8,128)S(1)}, s32[36,32,384]{2,1,0:T(8,128)}, u32[]{:S(2)}) %copy-start) | copy-done | bytes 1769496
  1.5 1.5 %copy-done.1 = f32[36,32,384]{2,1,0:T(8,128)S(1)} copy-done((f32[36,32,384]{2,1,0:T(8,128)S(1)}, f32[36,32,384]{2,1,0:T(8,128)}, u32[]{:S(2)}) %copy-start.1) | copy-done | bytes 1769496
  3.0 1.1 %shard_map.55 = (f32[9,3,32,128]{3,2,1,0:T(8,128)S(1)}, f32[9,3,32,128]{3,2,1,0:T(8,128)S(1)}, f32[3,112,128]{2,1,0:T(8,128)S(1)}, f32[3,112,128]{2,1,0:T(8,128)...) custom-call(s32[36,32,384]{2,1,0:T(8,128)S(1)} %copy-done, f32[36,32,384]{2,1,0:T(8,128)S(1)} %copy-done.1, ...), custom_call_target="tpu_custom_call" | custom-call | tf_op jit(solution)/shard_map/pallas_call | solution.py:114
  4.1 0.5 collective-permute-start
  5.9 0.1 pad_add_fusion.own
  6.0 2.5 %collective-permute-start.1 = (s32[2]{0:T(128)S(1)}, s32[2]{0:T(128)S(1)}, u32[]{:S(2)}, u32[]{:S(2)}) collective-permute-start(s32[2]{0:T(128)S(1)} %pad_add_fusion.own), channel_id=1, source_target_pairs={{0,16},{16,0},{1,17},{17,1},{2,18},{18,2},{3,19},{19,3},{4,20},{20... | collective-permute-start | bytes 32 | tf_op jit(solution)/shard_map/ppermute | solution.py:350
  8.5 3.3 %collective-permute-start.3 = (f32[3,112,128]{2,1,0:T(8,128)S(1)}, f32[3,112,128]{2,1,0:T(8,128)S(1)}, u32[]{:S(2)}, u32[]{:S(2)}) collective-permute-start(f32[3,112,128]{2,1,0:T(8,128)S(1)} %get-tuple-element.22), channel_id=1, source_target_pairs={{0,5},{1,4},{4,9},{5,8},{8,13},{9,12},{2,7},{3,6},{6,11},{7,10},{1... | collective-permute-start | bytes 516104 | tf_op jit(solution)/shard_map/ppermute | solution.py:359
  11.8 1.3 %collective-permute-start.4 = (f32[3,112,128]{2,1,0:T(8,128)S(1)}, f32[3,112,128]{2,1,0:T(8,128)S(1)}, u32[]{:S(2)}, u32[]{:S(2)}) collective-permute-start(f32[3,112,128]{2,1,0:T(8,128)S(1)} %get-tuple-element.23), channel_id=1, source_target_pairs={{4,0},{5,1},{8,4},{9,5},{12,8},{13,9},{6,2},{7,3},{10,6},{11,7},{1... | collective-permute-start | bytes 516104 | tf_op jit(solution)/shard_map/ppermute | solution.py:359
  13.1 1.3 %collective-permute-start.5 = (f32[3,112,128]{2,1,0:T(8,128)S(1)}, f32[3,112,128]{2,1,0:T(8,128)S(1)}, u32[]{:S(2)}, u32[]{:S(2)}) collective-permute-start(f32[3,112,128]{2,1,0:T(8,128)S(1)} %get-tuple-element.24), channel_id=1, source_target_pairs={{4,1},{5,0},{8,5},{9,4},{12,9},{13,8},{6,3},{7,2},{10,7},{11,6},{1... | collective-permute-start | bytes 516104 | tf_op jit(solution)/shard_map/ppermute | solution.py:359
  14.4 5.2 %collective-permute-start.2 = (f32[3,112,128]{2,1,0:T(8,128)S(1)}, f32[3,112,128]{2,1,0:T(8,128)S(1)}, u32[]{:S(2)}, u32[]{:S(2)}) collective-permute-start(f32[3,112,128]{2,1,0:T(8,128)S(1)} %get-tuple-element.21), channel_id=1, source_target_pairs={{0,4},{1,5},{4,8},{5,9},{8,12},{9,13},{2,6},{3,7},{6,10},{7,11},{1... | collective-permute-start | bytes 516104 | tf_op jit(solution)/shard_map/ppermute | solution.py:359
  19.6 4.2 %shard_map.56.source = f32[2,9,6,7,8,128]{5,4,3,2,1,0:T(8,128)S(1)} custom-call(s32[2]{0:T(128)S(1)} %collective-permute-done.1.other, s32[2]{0:T(128)S(1)} %pad_add_fusion.own), custom_call_target="tpu_custom_call" | custom-call | tf_op jit(solution)/shard_map/pallas_call | solution.py:145
  23.9 10.6 %shard_map.57 = (f32[9,3,16,128]{3,2,1,0:T(8,128)S(1)}, f32[9,3,16,128]{3,2,1,0:T(8,128)S(1)}, f32[9,3,16,128]{3,2,1,0:T(8,128)S(1)}, f32[9,3,16,128]{3,2,1,0:T(8,128)S(1)}, f32[4,9,3,16,128]{4,3,2,1,0:T(8,128)S(1)}) custom-call(f32[9,3,32,128]{3,2,1,0:T(8,128)S(1)} %get-tuple-element.18.mine, f32[9,3,32,128]{3,2,1,0:T(8,128)S(1)} %collective-permute-done.theirs, ...), custom_call_target="tpu_custom_call" | custom-call | tf_op jit(solution)/shard_map/pallas_call | solution.py:270
  34.4 0.1 collective-permute-start.6
  34.5 2.4 %collective-permute-done.6 = f32[4,9,3,16,128]{4,3,2,1,0:T(8,128)S(1)} collective-permute-done((f32[4,9,3,16,128]{4,3,2,1,0:T(8,128)S(1)}, f32[4,9,3,16,128]{4,3,2,1,0:T(8,128)S(1)}, u32[]{:S(2)}, u32[]{:S(2)}) %collective-permute-start.6) | collective-permute-done | bytes 884768 | tf_op jit(solution)/shard_map/ppermute | solution.py:350
  37.0 0.6 collective-permute-start.7
  37.6 1.6 %collective-permute-start.9 = (f32[2,9,3,16,128]{4,3,2,1,0:T(8,128)S(1)}, f32[2,9,3,16,128]{4,3,2,1,0:T(8,128)S(1)}, u32[]{:S(2)}, u32[]{:S(2)}) collective-permute-start(f32[2,9,3,16,128]{4,3,2,1,0:T(8,128)S(1)} %pad_maximum_fusion.3), channel_id=1, source_target_pairs={{0,2},{2,0},{1,3},{3,1},{4,6},{6,4},{5,7},{7,5},{8,10},{10,8},{9,1... | collective-permute-start | bytes 1327112 | tf_op jit(solution)/shard_map/ppermute | solution.py:350
  39.2 1.6 %collective-permute-start.8 = (f32[2,9,3,16,128]{4,3,2,1,0:T(8,128)S(1)}, f32[2,9,3,16,128]{4,3,2,1,0:T(8,128)S(1)}, u32[]{:S(2)}, u32[]{:S(2)}) collective-permute-start(f32[2,9,3,16,128]{4,3,2,1,0:T(8,128)S(1)} %pad_maximum_fusion.2), channel_id=1, source_target_pairs={{0,18},{2,16},{16,2},{18,0},{1,19},{3,17},{17,3},{19,1},{4,22},{6,... | collective-permute-start | bytes 1327112 | tf_op jit(solution)/shard_map/ppermute | solution.py:350
  40.8 0.1 constant_dynamic-slice_fusion
  40.9 0.1 concatenate.6.weights
  41.1 8.2 %collective-permute-done.7.refs_1_ = f32[2,9,3,16,128]{4,3,2,1,0:T(8,128)S(1)} collective-permute-done((f32[2,9,3,16,128]{4,3,2,1,0:T(8,128)S(1)}, f32[2,9,3,16,128]{4,3,2,1,0:T(8,128)S(1)}, u32[]{:S(2)}, u32[]{:S(2)}) %collective-permute-start.7) | collective-permute-done | bytes 442400 | tf_op jit(solution)/shard_map/ppermute | solution.py:350
  49.3 0.8 %shard_map.58.near = f32[36,3,16,128]{3,2,1,0:T(8,128)S(1)} custom-call(f32[2,9,3,16,128]{4,3,2,1,0:T(8,128)S(1)} %pad_maximum_fusion.refs_0_, f32[2,9,3,16,128]{4,3,2,1,0:T(8,128)S(1)} %collective-permute-done.7.refs_1_), custom_call_target="tpu_custom_call" | custom-call | tf_op jit(solution)/shard_map/pallas_call | solution.py:300
  50.1 0.7 %collective-permute-done.9.refs_1_ = f32[2,9,3,16,128]{4,3,2,1,0:T(8,128)S(1)} collective-permute-done((f32[2,9,3,16,128]{4,3,2,1,0:T(8,128)S(1)}, f32[2,9,3,16,128]{4,3,2,1,0:T(8,128)S(1)}, u32[]{:S(2)}, u32[]{:S(2)}) %collective-permute-start.9) | collective-permute-done | bytes 442400 | tf_op jit(solution)/shard_map/ppermute | solution.py:350
  50.7 9.3 %collective-permute-done.8.refs_0_ = f32[2,9,3,16,128]{4,3,2,1,0:T(8,128)S(1)} collective-permute-done((f32[2,9,3,16,128]{4,3,2,1,0:T(8,128)S(1)}, f32[2,9,3,16,128]{4,3,2,1,0:T(8,128)S(1)}, u32[]{:S(2)}, u32[]{:S(2)}) %collective-permute-start.8) | collective-permute-done | bytes 442400 | tf_op jit(solution)/shard_map/ppermute | solution.py:350
  60.1 3.6 %shard_map.59 = f32[72,16,384]{2,1,0:T(8,128)} custom-call(f32[72,72]{1,0:T(8,128)S(1)} %concatenate.6.weights, f32[36,3,16,128]{3,2,1,0:T(8,128)S(1)} %shard_map.58.near, f32[2,9,3,16,128]{4,3,2,1,0:T(8,128)S(1)} %collective-permute-done.8.refs_0_, f32[2,9,3,16,128]{4,3,2,1,0:T(8,128)S(1)} %collective-permute-done.9.refs_1_), custom_call_target="tpu_custom_call" | custom-call | tf_op jit(solution)/shard_map/pallas_call | solution.py:335
  (15 shorter events, 0.2 us)
Async XLA Ops:
  0.0 1.5 %copy-start = (s32[36,32,384]{2,1,0:T(8,128)S(1)}, s32[36,32,384]{2,1,0:T(8,128)}, u32[]{:S(2)}) copy-start(s32[36,32,384]{2,1,0:T(8,128)} %mask_send.1) | copy-start | bytes 5308420
  1.5 1.5 %copy-start.1 = (f32[36,32,384]{2,1,0:T(8,128)S(1)}, f32[36,32,384]{2,1,0:T(8,128)}, u32[]{:S(2)}) copy-start(f32[36,32,384]{2,1,0:T(8,128)} %send_in.1) | copy-start | bytes 5308420
  4.1 19.7 %collective-permute-start = (f32[9,3,32,128]{3,2,1,0:T(8,128)S(1)}, f32[9,3,32,128]{3,2,1,0:T(8,128)S(1)}, u32[]{:S(2)}, u32[]{:S(2)}) collective-permute-start(f32[9,3,32,128]{3,2,1,0:T(8,128)S(1)} %get-tuple-element.19), channel_id=1, source_target_pairs={{0,1},{1,0},{2,3},{3,2},{4,5},{5,4},{6,7},{7,6},{8,9},{9,8},{10,11... | collective-permute-start | bytes 1327112 | tf_op jit(solution)/shard_map/ppermute | solution.py:350
  6.0 8.4 %collective-permute-start.1 = (s32[2]{0:T(128)S(1)}, s32[2]{0:T(128)S(1)}, u32[]{:S(2)}, u32[]{:S(2)}) collective-permute-start(s32[2]{0:T(128)S(1)} %pad_add_fusion.own), channel_id=1, source_target_pairs={{0,16},{16,0},{1,17},{17,1},{2,18},{18,2},{3,19},{19,3},{4,20},{20... | collective-permute-start | bytes 32 | tf_op jit(solution)/shard_map/ppermute | solution.py:350
  8.5 15.3 %collective-permute-start.3 = (f32[3,112,128]{2,1,0:T(8,128)S(1)}, f32[3,112,128]{2,1,0:T(8,128)S(1)}, u32[]{:S(2)}, u32[]{:S(2)}) collective-permute-start(f32[3,112,128]{2,1,0:T(8,128)S(1)} %get-tuple-element.22), channel_id=1, source_target_pairs={{0,5},{1,4},{4,9},{5,8},{8,13},{9,12},{2,7},{3,6},{6,11},{7,10},{1... | collective-permute-start | bytes 516104 | tf_op jit(solution)/shard_map/ppermute | solution.py:359
  11.8 12.0 %collective-permute-start.4 = (f32[3,112,128]{2,1,0:T(8,128)S(1)}, f32[3,112,128]{2,1,0:T(8,128)S(1)}, u32[]{:S(2)}, u32[]{:S(2)}) collective-permute-start(f32[3,112,128]{2,1,0:T(8,128)S(1)} %get-tuple-element.23), channel_id=1, source_target_pairs={{4,0},{5,1},{8,4},{9,5},{12,8},{13,9},{6,2},{7,3},{10,6},{11,7},{1... | collective-permute-start | bytes 516104 | tf_op jit(solution)/shard_map/ppermute | solution.py:359
  13.1 10.7 %collective-permute-start.5 = (f32[3,112,128]{2,1,0:T(8,128)S(1)}, f32[3,112,128]{2,1,0:T(8,128)S(1)}, u32[]{:S(2)}, u32[]{:S(2)}) collective-permute-start(f32[3,112,128]{2,1,0:T(8,128)S(1)} %get-tuple-element.24), channel_id=1, source_target_pairs={{4,1},{5,0},{8,5},{9,4},{12,9},{13,8},{6,3},{7,2},{10,7},{11,6},{1... | collective-permute-start | bytes 516104 | tf_op jit(solution)/shard_map/ppermute | solution.py:359
  14.4 9.4 %collective-permute-start.2 = (f32[3,112,128]{2,1,0:T(8,128)S(1)}, f32[3,112,128]{2,1,0:T(8,128)S(1)}, u32[]{:S(2)}, u32[]{:S(2)}) collective-permute-start(f32[3,112,128]{2,1,0:T(8,128)S(1)} %get-tuple-element.21), channel_id=1, source_target_pairs={{0,4},{1,5},{4,8},{5,9},{8,12},{9,13},{2,6},{3,7},{6,10},{7,11},{1... | collective-permute-start | bytes 516104 | tf_op jit(solution)/shard_map/ppermute | solution.py:359
  34.4 2.5 %collective-permute-start.6 = (f32[4,9,3,16,128]{4,3,2,1,0:T(8,128)S(1)}, f32[4,9,3,16,128]{4,3,2,1,0:T(8,128)S(1)}, u32[]{:S(2)}, u32[]{:S(2)}) collective-permute-start(f32[4,9,3,16,128]{4,3,2,1,0:T(8,128)S(1)} %get-tuple-element.27), channel_id=1, source_target_pairs={{0,1},{1,0},{2,3},{3,2},{4,5},{5,4},{6,7},{7,6},{8,9},{9,8},{10,11... | collective-permute-start | bytes 2654216 | tf_op jit(solution)/shard_map/ppermute | solution.py:350
  37.0 3.8 %copy-start.2 = (f32[72,72]{1,0:T(8,128)S(1)}, f32[72,72]{1,0:T(8,128)}, u32[]{:S(2)}) copy-start(f32[72,72]{1,0:T(8,128)} %param.7) | copy-start | bytes 62212
  37.0 12.3 %collective-permute-start.7 = (f32[2,9,3,16,128]{4,3,2,1,0:T(8,128)S(1)}, f32[2,9,3,16,128]{4,3,2,1,0:T(8,128)S(1)}, u32[]{:S(2)}, u32[]{:S(2)}) collective-permute-start(f32[2,9,3,16,128]{4,3,2,1,0:T(8,128)S(1)} %pad_maximum_fusion.1), channel_id=1, source_target_pairs={{0,16},{16,0},{1,17},{17,1},{2,18},{18,2},{3,19},{19,3},{4,20},{20... | collective-permute-start | bytes 1327112 | tf_op jit(solution)/shard_map/ppermute | solution.py:350
  37.6 13.1 %collective-permute-start.9 = (f32[2,9,3,16,128]{4,3,2,1,0:T(8,128)S(1)}, f32[2,9,3,16,128]{4,3,2,1,0:T(8,128)S(1)}, u32[]{:S(2)}, u32[]{:S(2)}) collective-permute-start(f32[2,9,3,16,128]{4,3,2,1,0:T(8,128)S(1)} %pad_maximum_fusion.3), channel_id=1, source_target_pairs={{0,2},{2,0},{1,3},{3,1},{4,6},{6,4},{5,7},{7,5},{8,10},{10,8},{9,1... | collective-permute-start | bytes 1327112 | tf_op jit(solution)/shard_map/ppermute | solution.py:350
  39.2 20.8 %collective-permute-start.8 = (f32[2,9,3,16,128]{4,3,2,1,0:T(8,128)S(1)}, f32[2,9,3,16,128]{4,3,2,1,0:T(8,128)S(1)}, u32[]{:S(2)}, u32[]{:S(2)}) collective-permute-start(f32[2,9,3,16,128]{4,3,2,1,0:T(8,128)S(1)} %pad_maximum_fusion.2), channel_id=1, source_target_pairs={{0,18},{2,16},{16,2},{18,0},{1,19},{3,17},{17,3},{19,1},{4,22},{6,... | collective-permute-start | bytes 1327112 | tf_op jit(solution)/shard_map/ppermute | solution.py:350

commit v5 on v4

--- a/solution.py
+++ b/solution.py
@@ -67,70 +67,49 @@
     return both[:rows] + both[rows:]
 
 
-def quarter(keep):
-    core = lax.axis_index("lon")
-    return lax.axis_index("member") * 2 + (core if keep else 1 - core)
-
-
 def edge_rows(some, pairs, halo):
     return -(-some * pairs * halo // SUB) * SUB
 
 
-def conduct_kernel(halo, mask_mine, mine_in, mask_send, send_in, *refs):
-    *outs, matrix = refs
-    levels, height, width = mask_mine.shape
+def conduct_kernel(halo, some, kept, other, mine, send, mine_edges, send_edges, matrix):
+    levels, height, width = kept.shape
     pairs = width // LANES
-
-    @pl.when(pl.program_id(0) == 0)
-    def _():
-        matrix[...] = packing(width, 2 * pairs, lax.axis_index("lon"), 1)
-
-    both = [d[...] * m[...].astype(jnp.float32) for m, d in ((mask_mine, mine_in), (mask_send, send_in))]
-    values = jnp.concatenate([v.reshape(levels * height, width) for v in both], axis=0)
-    moved = permuted(values, matrix[...])
-    for i in range(2):
-        rows, top, bottom = outs[i], outs[2 + i], outs[4 + i]
-        for g in range(levels):
+    matrix[...] = packing(width, 2 * pairs, lax.axis_index("lon"), 1)
+    for source, rows, edges in ((other, send, send_edges), (kept, mine, mine_edges)):
+        moved = permuted(source[...].reshape(levels * height, width), matrix[...])
+        for l in range(levels):
             for v in range(pairs):
-                start = (i * levels + g) * height
-                value = moved[start : start + height, v * LANES : (v + 1) * LANES]
-                rows[g, v] = value
-                here = pl.ds((g * pairs + v) * halo, halo)
-                top[0, here, :] = value[height - halo :]
-                bottom[0, here, :] = value[:halo]
-
-
-def packed_conduct(halo, share, mask, diffusivity):
-    _, height, width = mask.shape
+                value = moved[l * height : (l + 1) * height, v * LANES : (v + 1) * LANES]
+                rows[l, v] = value
+                edge = pl.ds((l % some * pairs + v) * halo, halo)
+                edges[0, l // some, edge, :] = value[height - halo :]
+                edges[1, l // some, edge, :] = value[:halo]
+
+
+def packed_conduct(halo, kept, other):
+    share, height, width = kept.shape
     some, pairs = math.gcd(share, SOME), width // LANES
-    steps = share // some
-    extent = edge_rows(some, pairs, halo)
-    ins = [
-        pl.BlockSpec((some, height, width), lambda l, keep=keep: (quarter(keep) * steps + l, 0, 0))
-        for keep in (True, True, False, False)
-    ]
     rows = jax.ShapeDtypeStruct((share, pairs, height, LANES), jnp.float32)
-    edge = jax.ShapeDtypeStruct((steps, extent, LANES), jnp.float32)
+    edge = jax.ShapeDtypeStruct((2, share // some, edge_rows(some, pairs, halo), LANES), jnp.float32)
     return pl.pallas_call(
-        functools.partial(conduct_kernel, halo),
-        out_shape=(rows,) * 2 + (edge,) * 4,
-        grid=(steps,),
-        in_specs=ins,
-        out_specs=[pl.BlockSpec((some, pairs, height, LANES), lambda l: (l, 0, 0, 0))] * 2
-        + [pl.BlockSpec((1, extent, LANES), lambda l: (l, 0, 0))] * 4,
+        functools.partial(conduct_kernel, halo, some),
+        out_shape=(rows, rows, edge, edge),
+        in_specs=[whole()] * 2,
+        out_specs=(whole(),) * 4,
         scratch_shapes=[VMEM((width, width), jnp.bfloat16)],
-        compiler_params=budget(12),
-    )(mask, diffusivity, mask, diffusivity)
+        compiler_params=budget(8),
+    )(kept, other)
 
 
 def noise_kernel(levels_here, halo, total_rows, total_cols, other, own, out):
     _, levels, tiles, pitch = out.shape[:4]
-    level0 = lax.axis_index("lev") * levels_here + quarter(True) * levels
+    quarter = lax.axis_index("member") * 2 + lax.axis_index("lon")
+    level0 = lax.axis_index("lev") * levels_here + quarter * levels
     row0 = lax.axis_index("lat") * (total_rows // lax.axis_size("lat")) - halo
     sub = lax.broadcasted_iota(jnp.int32, (SUB, LANES), 0)
     lane = lax.broadcasted_iota(jnp.int32, (SUB, LANES), 1)
     within = sub * (pitch * total_cols) + lane * tiles
-    bases = [ids[0] * 69069 + ids[1] * 362437 for ids in (other, own)]
+    bases = [other[...], own[...]]
 
     @pl.loop(0, levels)
     def _(l):
@@ -145,7 +124,7 @@
     return pl.pallas_call(
         functools.partial(noise_kernel, levels_here, halo, total_rows, total_cols),
         out_shape=jax.ShapeDtypeStruct((2, *shape), jnp.float32),
-        in_specs=[scalars()] * 2,
+        in_specs=[whole()] * 2,
         out_specs=whole(),
         compiler_params=budget(8),
     )(other, own)
@@ -177,8 +156,7 @@
     return [*range(1, tiles - 1), 0, tiles - 1]
 
 
-def diffuse_kernel(halo, halves, mine, theirs, top_mine, top_theirs, bottom_mine, bottom_theirs,
-                   source, *refs):
+def diffuse_kernel(halo, halves, mine, theirs, top, bottom, source, *refs):
     *kept, sent, rows, cond, gain, push, inv, u0, u1, res = refs
     _, levels, tiles, pitch = source.shape[:4]
     pairs, height = mine.shape[1], mine.shape[2]
@@ -204,9 +182,9 @@
             for v in range(pairs):
                 edge = pl.ds((g * pairs + v) * halo, halo)
                 for p, q, start in (
-                    (top_mine[block, edge, :], top_theirs[block, edge, :], 0),
+                    (top[0, block, edge, :], top[1, block, edge, :], 0),
                     (mine[l, v], theirs[l, v], halo),
-                    (bottom_mine[block, edge, :], bottom_theirs[block, edge, :], halo + height),
+                    (bottom[0, block, edge, :], bottom[1, block, edge, :], halo + height),
                 ):
                     count = p.shape[0]
                     left = on_left(p.shape)
@@ -350,13 +328,9 @@
     return lax.ppermute(block, axes, [(i, count - 1 - i) for i in range(count)])
 
 
-def shifted(block, step, cross):
+def shifted(block, step):
     strips = lax.axis_size("lat")
-    route = [
-        (2 * i + c, 2 * (i + step) + (1 - c if cross else c))
-        for i in range(strips) if 0 <= i + step < strips for c in range(2)
-    ]
-    return lax.ppermute(block, ("lat", "lon"), route)
+    return lax.ppermute(block, "lat", [(i, i + step) for i in range(strips) if 0 <= i + step < strips])
 
 
 def part(block, index, size, axis):
@@ -389,17 +363,20 @@
     spare = share * 4 - levels
     if spare:
         land_mask, diffusivity = (jnp.pad(v, ((0, spare), (0, 0), (0, 0))) for v in (land_mask, diffusivity))
-    mine, send, top, top_cross, bottom, bottom_cross = packed_conduct(halo, share, land_mask, diffusivity)
-    ids = jnp.concatenate([counter_key, member_id])
-    other_ids = crossed(ids, "member")
-    top, other_ids = lax.optimization_barrier((top, other_ids))
-    top, bottom = shifted(top, 1, False), shifted(bottom, -1, False)
-    top_cross, bottom_cross = shifted(top_cross, 1, True), shifted(bottom_cross, -1, True)
+    kept, other = (
+        part(diffusivity, member * 2 + c, share, 0) * part(land_mask, member * 2 + c, share, 0).astype(jnp.float32)
+        for c in (core, 1 - core)
+    )
+    mine, send, mine_edges, send_edges = packed_conduct(halo, kept, other)
+    edges = jnp.stack([mine_edges, crossed(send_edges, "lon")], axis=1)
     theirs = crossed(send, "lon")
+    top, bottom = shifted(edges[0], 1), shifted(edges[1], -1)
+    base = jnp.broadcast_to(counter_key[0] * 69069 + member_id[0] * 362437, (SUB, LANES))
+    other_base = crossed(base, "member")
     tiles = breadth * cores // LANES
     sizes = (levels, halo, (share, tiles, pitch, SUB, LANES), height * strips, breadth * cores)
-    source = noise(other_ids, ids, *sizes)
-    *kept, sent = diffuse(halo, groups == 2, mine, theirs, top, top_cross, bottom, bottom_cross, source)
+    source = noise(other_base, base, *sizes)
+    *kept, sent = diffuse(halo, groups == 2, mine, theirs, top, bottom, source)
 
     def weights_of(order):
         padded = jnp.pad(balance.reshape(-1, groups, levels), ((0, 0), (0, 0), (0, spare)))

time: 63.9 us -> 61.5 us (0.962)
  waiting for transfers between devices: 20.6 us -> 26.5 us
  starting transfers between devices: 17.9 us -> 12.1 us
  local copies, waits for them, and re-layouts: 3.31 us -> 0.36 us
  other arithmetic: 0.2 us -> 1.73 us
  Pallas kernels: 20.2 us -> 19.2 us
    ppermute x4 -> x2, starting transfers between devices: 11.1 us -> 6.16 us  [shifted(): lax.ppermute(block, 'lat', [(i, i + step) for i in range(strips) if 0 <=...]
    ppermute x6 -> x7, waiting for transfers between devices: 20.6 us -> 24.7 us  [crossed(): return lax.ppermute(block, axes, [(i, count - 1 - i) for i in range(count)])]
    unnamed x6 -> x2, local copies, waits for them, and re-layouts: 2.96 us -> 0.01 us
    ppermute x4 -> x2, waiting for transfers between devices: 0.01 us -> 1.8 us  [shifted(): lax.ppermute(block, 'lat', [(i, i + step) for i in range(strips) if 0 <=...]
    mul x0 -> x1, other arithmetic: none -> 1.54 us  [per_device(): part(diffusivity, member * 2 + c, share, 0)]
    ppermute x6 -> x7, starting transfers between devices: 6.8 us -> 5.92 us  [crossed(): return lax.ppermute(block, axes, [(i, count - 1 - i) for i in range(count)])]
  transfers between devices with their start and end apart: 10 -> 9, of which waited for: 4 -> 5; matrix products, arithmetic and copies ran while one was open for 1% -> 1% of each run, Pallas kernels for 8% -> 7%
where the time goes in v5:
time: 61.5 us; the launch traced here: 61.3 us
  waiting for transfers between devices  26.5 us (43%)
  Pallas kernels  19.2 us (31%)
  starting transfers between devices  12.1 us (20%)
  other arithmetic  1.73 us (3%)
  between operations  1.44 us (2%)
    ppermute x7, waiting for transfers between devices, crossed(): return lax.ppermute(block, axes, [(i, count - 1 - i) for i in range(count)])  24.7 us
    pallas_call x1, Pallas kernels, diffuse(): pl.pallas_call(functools.partial(diffuse_kernel, halo, halves), out_shape...  10.5 us
    ppermute x2, starting transfers between devices, shifted(): lax.ppermute(block, 'lat', [(i, i + step) for i in range(strips) if 0 <=...  6.16 us
    ppermute x7, starting transfers between devices, crossed(): return lax.ppermute(block, axes, [(i, count - 1 - i) for i in range(count)])  5.92 us
    pallas_call x1, Pallas kernels, noise(): pl.pallas_call(functools.partial(noise_kernel, levels_here, halo, total_r...  3.61 us
    pallas_call x1, Pallas kernels, balanced(): pl.pallas_call(balance_kernel, out_shape=jax.ShapeDtypeStruct((total, hei...  3.57 us
    ppermute x2, waiting for transfers between devices, shifted(): lax.ppermute(block, 'lat', [(i, i + step) for i in range(strips) if 0 <=...  1.8 us
    mul x1, other arithmetic, per_device(): part(diffusivity, member * 2 + c, share, 0)  1.54 us
  transfers between devices with their start and end apart: 9, of which 5 were waited for; matrix products, arithmetic and copies ran while one was open for 1% of the time, Pallas kernels for 7%

profile of v5, /device:TPU:0, one launch (start us, length us, event | category | flops | bytes accessed | tf_op | source)
XLA Modules:
  0.0 61.3 jit_solution(5774509121770654616)
XLA Ops:
  0.0 1.5 %convert_multiply_fusion = (f32[9,32,384]{2,1,0:T(8,128)S(1)}, f32[9,32,384]{2,1,0:T(8,128)S(1)}) fusion(s32[36,32,384]{2,1,0:T(8,128)} %param.5, s32[]{:T(128)S(6)} %select_n.41, f32[36,32,384]{2,1,0:T(8,128)} %param.6, s32[]{:T(128)S(6)} %select_n.40), kind=kLoop, calls=%fused_computation.6 | loop fusion | flops 442368 | bytes 2654216 | tf_op jit(solution)/shard_map/mul | solution.py:367
  1.5 0.7 %shard_map.55 = (f32[9,3,32,128]{3,2,1,0:T(8,128)S(1)}, f32[9,3,32,128]{3,2,1,0:T(8,128)S(1)}, f32[2,3,112,128]{3,2,1,0:T(8,128)S(1)}, f32[2,3,112,128]{3,2,1,0:T(8,128)S(1)}) custom-call(f32[9,32,384]{2,1,0:T(8,128)S(1)} %get-tuple-element.24.kept, f32[9,32,384]{2,1,0:T(8,128)S(1)} %get-tuple-element.23.other), custom_call_target="tpu_custom_call" | custom-call | tf_op jit(solution)/shard_map/pallas_call | solution.py:94
  2.3 0.5 collective-permute-start.1
  2.8 0.1 collective-permute-start
  2.9 1.2 %collective-permute-done.1 = f32[2,3,112,128]{3,2,1,0:T(8,128)S(1)} collective-permute-done((f32[2,3,112,128]{3,2,1,0:T(8,128)S(1)}, f32[2,3,112,128]{3,2,1,0:T(8,128)S(1)}, u32[]{:S(2)}, u32[]{:S(2)}) %collective-permute-start.1) | collective-permute-done | bytes 344096 | tf_op jit(solution)/shard_map/ppermute | solution.py:328
  4.1 4.9 %collective-permute-start.2 = (f32[2,3,112,128]{3,2,1,0:T(8,128)S(1)}, f32[2,3,112,128]{3,2,1,0:T(8,128)S(1)}, u32[]{:S(2)}, u32[]{:S(2)}) collective-permute-start(f32[2,3,112,128]{3,2,1,0:T(8,128)S(1)} %get-tuple-element.30), channel_id=1, source_target_pairs={{0,4},{4,8},{8,12},{1,5},{5,9},{9,13},{2,6},{6,10},{10,14},{3,7},{... | collective-permute-start | bytes 1032200 | tf_op jit(solution)/shard_map/ppermute | solution.py:333
  9.0 1.3 %collective-permute-start.3 = (f32[2,3,112,128]{3,2,1,0:T(8,128)S(1)}, f32[2,3,112,128]{3,2,1,0:T(8,128)S(1)}, u32[]{:S(2)}, u32[]{:S(2)}) collective-permute-start(f32[2,3,112,128]{3,2,1,0:T(8,128)S(1)} %get-tuple-element.29), channel_id=1, source_target_pairs={{4,0},{8,4},{12,8},{5,1},{9,5},{13,9},{6,2},{10,6},{14,10},{7,3},{... | collective-permute-start | bytes 1032200 | tf_op jit(solution)/shard_map/ppermute | solution.py:333
  11.6 1.6 %collective-permute-start.4 = (s32[8,128]{1,0:T(8,128)S(1)}, s32[8,128]{1,0:T(8,128)S(1)}, u32[]{:S(2)}, u32[]{:S(2)}) collective-permute-start(s32[8,128]{1,0:T(8,128)S(1)} %broadcast_in_dim.3.own), channel_id=1, source_target_pairs={{0,16},{16,0},{1,17},{17,1},{2,18},{18,2},{3,19},{19,3},{4,20},{20... | collective-permute-start | bytes 12296 | tf_op jit(solution)/shard_map/ppermute | solution.py:328
  13.2 2.1 %collective-permute-done.4.other = s32[8,128]{1,0:T(8,128)S(1)} collective-permute-done((s32[8,128]{1,0:T(8,128)S(1)}, s32[8,128]{1,0:T(8,128)S(1)}, u32[]{:S(2)}, u32[]{:S(2)}) %collective-permute-start.4) | collective-permute-done | bytes 4128 | tf_op jit(solution)/shard_map/ppermute | solution.py:328
  15.3 3.6 %shard_map.56.source = f32[2,9,6,7,8,128]{5,4,3,2,1,0:T(8,128)S(1)} custom-call(s32[8,128]{1,0:T(8,128)S(1)} %collective-permute-done.4.other, s32[8,128]{1,0:T(8,128)S(1)} %broadcast_in_dim.3.own), custom_call_target="tpu_custom_call" | custom-call | tf_op jit(solution)/shard_map/pallas_call | solution.py:124
  18.9 1.8 %collective-permute-done.3.bottom = f32[2,3,112,128]{3,2,1,0:T(8,128)S(1)} collective-permute-done((f32[2,3,112,128]{3,2,1,0:T(8,128)S(1)}, f32[2,3,112,128]{3,2,1,0:T(8,128)S(1)}, u32[]{:S(2)}, u32[]{:S(2)}) %collective-permute-start.3) | collective-permute-done | bytes 344096 | tf_op jit(solution)/shard_map/ppermute | solution.py:333
  20.7 10.5 %shard_map.57 = (f32[9,3,16,128]{3,2,1,0:T(8,128)S(1)}, f32[9,3,16,128]{3,2,1,0:T(8,128)S(1)}, f32[9,3,16,128]{3,2,1,0:T(8,128)S(1)}, f32[9,3,16,128]{3,2,1,0:T(8,128)S(1)}, f32[4,9,3,16,128]{4,3,2,1,0:T(8,128)S(1)}) custom-call(f32[9,3,32,128]{3,2,1,0:T(8,128)S(1)} %get-tuple-element.14.mine, f32[9,3,32,128]{3,2,1,0:T(8,128)S(1)} %collective-permute-done.theirs, ...), custom_call_target="tpu_custom_call" | custom-call | tf_op jit(solution)/shard_map/pallas_call | solution.py:248
  31.3 0.1 collective-permute-start.5
  31.3 2.4 %collective-permute-done.5 = f32[4,9,3,16,128]{4,3,2,1,0:T(8,128)S(1)} collective-permute-done((f32[4,9,3,16,128]{4,3,2,1,0:T(8,128)S(1)}, f32[4,9,3,16,128]{4,3,2,1,0:T(8,128)S(1)}, u32[]{:S(2)}, u32[]{:S(2)}) %collective-permute-start.5) | collective-permute-done | bytes 884768 | tf_op jit(solution)/shard_map/ppermute | solution.py:328
  33.8 0.1 fusion.3
  33.8 0.0 copy-start
  33.9 1.6 %collective-permute-start.8 = (f32[2,9,3,16,128]{4,3,2,1,0:T(8,128)S(1)}, f32[2,9,3,16,128]{4,3,2,1,0:T(8,128)S(1)}, u32[]{:S(2)}, u32[]{:S(2)}) collective-permute-start(f32[2,9,3,16,128]{4,3,2,1,0:T(8,128)S(1)} %pad_maximum_fusion.3), channel_id=1, source_target_pairs={{0,2},{2,0},{1,3},{3,1},{4,6},{6,4},{5,7},{7,5},{8,10},{10,8},{9,1... | collective-permute-start | bytes 1327112 | tf_op jit(solution)/shard_map/ppermute | solution.py:328
  35.5 1.6 %collective-permute-start.6 = (f32[2,9,3,16,128]{4,3,2,1,0:T(8,128)S(1)}, f32[2,9,3,16,128]{4,3,2,1,0:T(8,128)S(1)}, u32[]{:S(2)}, u32[]{:S(2)}) collective-permute-start(f32[2,9,3,16,128]{4,3,2,1,0:T(8,128)S(1)} %pad_maximum_fusion.1), channel_id=1, source_target_pairs={{0,16},{16,0},{1,17},{17,1},{2,18},{18,2},{3,19},{19,3},{4,20},{20... | collective-permute-start | bytes 1327112 | tf_op jit(solution)/shard_map/ppermute | solution.py:328
  37.1 0.5 collective-permute-start.7
  37.6 0.1 constant_dynamic-slice_fusion
  37.8 0.1 concatenate.3.weights
  38.0 19.0 %collective-permute-done.6.refs_1_ = f32[2,9,3,16,128]{4,3,2,1,0:T(8,128)S(1)} collective-permute-done((f32[2,9,3,16,128]{4,3,2,1,0:T(8,128)S(1)}, f32[2,9,3,16,128]{4,3,2,1,0:T(8,128)S(1)}, u32[]{:S(2)}, u32[]{:S(2)}) %collective-permute-start.6) | collective-permute-done | bytes 442400 | tf_op jit(solution)/shard_map/ppermute | solution.py:328
  56.9 0.8 %shard_map.58.near = f32[36,3,16,128]{3,2,1,0:T(8,128)S(1)} custom-call(f32[2,9,3,16,128]{4,3,2,1,0:T(8,128)S(1)} %pad_maximum_fusion.refs_0_, f32[2,9,3,16,128]{4,3,2,1,0:T(8,128)S(1)} %collective-permute-done.6.refs_1_), custom_call_target="tpu_custom_call" | custom-call | tf_op jit(solution)/shard_map/pallas_call | solution.py:278
  57.7 3.6 %shard_map.59 = f32[72,16,384]{2,1,0:T(8,128)} custom-call(f32[72,72]{1,0:T(8,128)S(1)} %concatenate.3.weights, f32[36,3,16,128]{3,2,1,0:T(8,128)S(1)} %shard_map.58.near, f32[2,9,3,16,128]{4,3,2,1,0:T(8,128)S(1)} %collective-permute-done.7.refs_0_, f32[2,9,3,16,128]{4,3,2,1,0:T(8,128)S(1)} %collective-permute-done.8.refs_1_), custom_call_target="tpu_custom_call" | custom-call | tf_op jit(solution)/shard_map/pallas_call | solution.py:313
  (11 shorter events, 0.2 us)
Async XLA Ops:
  2.3 1.8 %collective-permute-start.1 = (f32[2,3,112,128]{3,2,1,0:T(8,128)S(1)}, f32[2,3,112,128]{3,2,1,0:T(8,128)S(1)}, u32[]{:S(2)}, u32[]{:S(2)}) collective-permute-start(f32[2,3,112,128]{3,2,1,0:T(8,128)S(1)} %get-tuple-element.17), channel_id=1, source_target_pairs={{0,1},{1,0},{2,3},{3,2},{4,5},{5,4},{6,7},{7,6},{8,9},{9,8},{10,11... | collective-permute-start | bytes 1032200 | tf_op jit(solution)/shard_map/ppermute | solution.py:328
  2.8 16.1 %collective-permute-start = (f32[9,3,32,128]{3,2,1,0:T(8,128)S(1)}, f32[9,3,32,128]{3,2,1,0:T(8,128)S(1)}, u32[]{:S(2)}, u32[]{:S(2)}) collective-permute-start(f32[9,3,32,128]{3,2,1,0:T(8,128)S(1)} %get-tuple-element.15), channel_id=1, source_target_pairs={{0,1},{1,0},{2,3},{3,2},{4,5},{5,4},{6,7},{7,6},{8,9},{9,8},{10,11... | collective-permute-start | bytes 1327112 | tf_op jit(solution)/shard_map/ppermute | solution.py:328
  4.1 14.8 %collective-permute-start.2 = (f32[2,3,112,128]{3,2,1,0:T(8,128)S(1)}, f32[2,3,112,128]{3,2,1,0:T(8,128)S(1)}, u32[]{:S(2)}, u32[]{:S(2)}) collective-permute-start(f32[2,3,112,128]{3,2,1,0:T(8,128)S(1)} %get-tuple-element.30), channel_id=1, source_target_pairs={{0,4},{4,8},{8,12},{1,5},{5,9},{9,13},{2,6},{6,10},{10,14},{3,7},{... | collective-permute-start | bytes 1032200 | tf_op jit(solution)/shard_map/ppermute | solution.py:333
  9.0 11.7 %collective-permute-start.3 = (f32[2,3,112,128]{3,2,1,0:T(8,128)S(1)}, f32[2,3,112,128]{3,2,1,0:T(8,128)S(1)}, u32[]{:S(2)}, u32[]{:S(2)}) collective-permute-start(f32[2,3,112,128]{3,2,1,0:T(8,128)S(1)} %get-tuple-element.29), channel_id=1, source_target_pairs={{4,0},{8,4},{12,8},{5,1},{9,5},{13,9},{6,2},{10,6},{14,10},{7,3},{... | collective-permute-start | bytes 1032200 | tf_op jit(solution)/shard_map/ppermute | solution.py:333
  11.6 3.7 %collective-permute-start.4 = (s32[8,128]{1,0:T(8,128)S(1)}, s32[8,128]{1,0:T(8,128)S(1)}, u32[]{:S(2)}, u32[]{:S(2)}) collective-permute-start(s32[8,128]{1,0:T(8,128)S(1)} %broadcast_in_dim.3.own), channel_id=1, source_target_pairs={{0,16},{16,0},{1,17},{17,1},{2,18},{18,2},{3,19},{19,3},{4,20},{20... | collective-permute-start | bytes 12296 | tf_op jit(solution)/shard_map/ppermute | solution.py:328
  31.3 2.5 %collective-permute-start.5 = (f32[4,9,3,16,128]{4,3,2,1,0:T(8,128)S(1)}, f32[4,9,3,16,128]{4,3,2,1,0:T(8,128)S(1)}, u32[]{:S(2)}, u32[]{:S(2)}) collective-permute-start(f32[4,9,3,16,128]{4,3,2,1,0:T(8,128)S(1)} %get-tuple-element.19), channel_id=1, source_target_pairs={{0,1},{1,0},{2,3},{3,2},{4,5},{5,4},{6,7},{7,6},{8,9},{9,8},{10,11... | collective-permute-start | bytes 2654216 | tf_op jit(solution)/shard_map/ppermute | solution.py:328
  33.8 3.8 %copy-start = (f32[72,72]{1,0:T(8,128)S(1)}, f32[72,72]{1,0:T(8,128)}, u32[]{:S(2)}) copy-start(f32[72,72]{1,0:T(8,128)} %param.7) | copy-start | bytes 62212
  33.9 23.8 %collective-permute-start.8 = (f32[2,9,3,16,128]{4,3,2,1,0:T(8,128)S(1)}, f32[2,9,3,16,128]{4,3,2,1,0:T(8,128)S(1)}, u32[]{:S(2)}, u32[]{:S(2)}) collective-permute-start(f32[2,9,3,16,128]{4,3,2,1,0:T(8,128)S(1)} %pad_maximum_fusion.3), channel_id=1, source_target_pairs={{0,2},{2,0},{1,3},{3,1},{4,6},{6,4},{5,7},{7,5},{8,10},{10,8},{9,1... | collective-permute-start | bytes 1327112 | tf_op jit(solution)/shard_map/ppermute | solution.py:328
  35.5 21.5 %collective-permute-start.6 = (f32[2,9,3,16,128]{4,3,2,1,0:T(8,128)S(1)}, f32[2,9,3,16,128]{4,3,2,1,0:T(8,128)S(1)}, u32[]{:S(2)}, u32[]{:S(2)}) collective-permute-start(f32[2,9,3,16,128]{4,3,2,1,0:T(8,128)S(1)} %pad_maximum_fusion.1), channel_id=1, source_target_pairs={{0,16},{16,0},{1,17},{17,1},{2,18},{18,2},{3,19},{19,3},{4,20},{20... | collective-permute-start | bytes 1327112 | tf_op jit(solution)/shard_map/ppermute | solution.py:328
  37.1 20.6 %collective-permute-start.7 = (f32[2,9,3,16,128]{4,3,2,1,0:T(8,128)S(1)}, f32[2,9,3,16,128]{4,3,2,1,0:T(8,128)S(1)}, u32[]{:S(2)}, u32[]{:S(2)}) collective-permute-start(f32[2,9,3,16,128]{4,3,2,1,0:T(8,128)S(1)} %pad_maximum_fusion.2), channel_id=1, source_target_pairs={{0,18},{2,16},{16,2},{18,0},{1,19},{3,17},{17,3},{19,1},{4,22},{6,... | collective-permute-start | bytes 1327112 | tf_op jit(solution)/shard_map/ppermute | solution.py:328

commit v6 on v5

--- a/solution.py
+++ b/solution.py
@@ -101,33 +101,32 @@
     )(kept, other)
 
 
-def noise_kernel(levels_here, halo, total_rows, total_cols, other, own, out):
-    _, levels, tiles, pitch = out.shape[:4]
+def noise_kernel(levels_here, halo, total_rows, total_cols, base, out):
+    levels, tiles, pitch = out.shape[:3]
     quarter = lax.axis_index("member") * 2 + lax.axis_index("lon")
     level0 = lax.axis_index("lev") * levels_here + quarter * levels
     row0 = lax.axis_index("lat") * (total_rows // lax.axis_size("lat")) - halo
     sub = lax.broadcasted_iota(jnp.int32, (SUB, LANES), 0)
     lane = lax.broadcasted_iota(jnp.int32, (SUB, LANES), 1)
     within = sub * (pitch * total_cols) + lane * tiles
-    bases = [other[...], own[...]]
+    stream = base[...]
 
     @pl.loop(0, levels)
     def _(l):
         start = ((level0 + l) * total_rows + row0) * total_cols
-        for i, base in enumerate(bases):
-            for t in range(tiles):
-                for k in range(pitch):
-                    out[i, l, t, k] = draw(within + (start + k * total_cols + t), base)
-
-
-def noise(other, own, levels_here, halo, shape, total_rows, total_cols):
+        for t in range(tiles):
+            for k in range(pitch):
+                out[l, t, k] = draw(within + (start + k * total_cols + t), stream)
+
+
+def noise(base, levels_here, halo, shape, total_rows, total_cols):
     return pl.pallas_call(
         functools.partial(noise_kernel, levels_here, halo, total_rows, total_cols),
-        out_shape=jax.ShapeDtypeStruct((2, *shape), jnp.float32),
-        in_specs=[whole()] * 2,
+        out_shape=jax.ShapeDtypeStruct(shape, jnp.float32),
+        in_specs=[whole()],
         out_specs=whole(),
         compiler_params=budget(8),
-    )(other, own)
+    )(base)
 
 
 def neighbour_sums(old, tiles, pitch, emit):
@@ -156,9 +155,10 @@
     return [*range(1, tiles - 1), 0, tiles - 1]
 
 
-def diffuse_kernel(halo, halves, mine, theirs, top, bottom, source, *refs):
+def diffuse_kernel(halo, halves, start_block, mine, theirs, top, bottom, other_source, own_source, *refs):
     *kept, sent, rows, cond, gain, push, inv, u0, u1, res = refs
-    _, levels, tiles, pitch = source.shape[:4]
+    sources = (other_source, own_source)
+    tiles, pitch = own_source.shape[1:3]
     pairs, height = mine.shape[1], mine.shape[2]
     final = height // 2
     core = lax.axis_index("lon")
@@ -175,7 +175,7 @@
 
         neighbour_sums(old, tiles, pitch, step)
 
-    @pl.loop(0, levels // some)
+    @pl.loop(start_block, start_block + kept[0].shape[0] // some)
     def _(block):
         for g in range(some):
             l = block * some + g
@@ -200,7 +200,7 @@
             inv[g, t, k] = r
             gain[g, t, k] = q * c
             for i in range(2):
-                s = source[i, block * some + g, t, k]
+                s = sources[i][block * some + g, t, k]
                 push[i * some + g, t, k] = q * s
                 u0[i * some + g, t, k] = c * s
 
@@ -215,7 +215,7 @@
 
         def finish(g, t, k, value, total):
             i, g = divmod(g, some)
-            c, s = cond[g, t, k], source[i, block * some + g, t, k]
+            c, s = cond[g, t, k], sources[i][block * some + g, t, k]
             value = jnp.where(c != 0.0, (s + c * total) * inv[g, t, k], 0.0)
             res[i * some + g, t, pl.ds(k, SUB, stride=pitch), :] = value
 
@@ -224,7 +224,7 @@
         first = group == 0
         for i in range(2):
             for g in range(some):
-                l = block * some + g
+                l = (block - start_block) * some + g
                 for v in range(pairs):
                     a = res[i * some + g, v, pl.ds(halo, height), :]
                     b = pltpu.roll(res[i * some + g, v + pairs, pl.ds(halo, height), :], HALF, 1)
@@ -237,16 +237,16 @@
                         away[l, v] = jnp.where(first, lower, upper)
 
 
-def diffuse(halo, halves, *operands):
+def diffuse(halo, halves, blocks, *operands):
     levels, pairs, height, _ = operands[0].shape
-    tiles, pitch = operands[-1].shape[2:4]
+    tiles, pitch = operands[-1].shape[1:3]
     some = math.gcd(levels, SOME)
     tile = VMEM((some, tiles, pitch, SUB, LANES), jnp.float32)
     both = VMEM((2 * some, tiles, pitch, SUB, LANES), jnp.float32)
     line = VMEM((2 * some, tiles, pitch * SUB, LANES), jnp.float32)
-    result = jax.ShapeDtypeStruct((levels, pairs, height // 2, LANES), jnp.float32)
+    result = jax.ShapeDtypeStruct((len(blocks) * some, pairs, height // 2, LANES), jnp.float32)
     return pl.pallas_call(
-        functools.partial(diffuse_kernel, halo, halves),
+        functools.partial(diffuse_kernel, halo, halves, blocks[0]),
         out_shape=(result,) * 4 + (jax.ShapeDtypeStruct((4, *result.shape), jnp.float32),),
         in_specs=[whole()] * len(operands),
         out_specs=(whole(),) * 5,
@@ -255,7 +255,8 @@
     )(*operands)
 
 
-def unpack(pieces, matrix, out, start):
+def unpack(pieces, matrix, out):
+    start = 0
     for piece in (p.at[i] for p in pieces for i in range(2)):
         levels, tiles, height, _ = piece.shape
         values = jnp.concatenate(
@@ -267,60 +268,94 @@
         start += levels
 
 
-def unpack_kernel(*refs):
-    *pieces, out = refs
-    tiles = pieces[0].shape[2]
-    unpack(pieces, packing(tiles * LANES, 2 * tiles, lax.axis_index("lon"), 0), out, 0)
-
-
-def unpacked(pieces):
-    _, levels, tiles, height, _ = pieces[0].shape
-    return pl.pallas_call(
-        unpack_kernel,
-        out_shape=jax.ShapeDtypeStruct((2 * len(pieces) * levels, tiles, height, LANES), jnp.float32),
-        in_specs=[whole()] * len(pieces),
-        out_specs=whole(),
-        compiler_params=budget(8),
-    )(*pieces)
-
-
-def balance_kernel(weights, near, *refs):
-    *pieces, out, columns, result = refs
-    total = weights.shape[0]
+def chosen(balance, places, width):
+    total = balance.shape[1]
+    core, member, group = (lax.axis_index(a) for a in ("lon", "member", "lev"))
+    column = lax.broadcasted_iota(jnp.int32, (total, width), 1)
+    level, offset = jnp.full((total, width), -1, jnp.int32), 0
+    share = total // 8
+    for across, swapped, start, size in places:
+        for c in (core, 1 - core):
+            g = 1 - group if across else group
+            m = 1 - member if swapped else member
+            first = (g * 4 + m * 2 + c) * share + start - offset
+            level = jnp.where((column >= offset) & (column < offset + size), column + first, level)
+            offset += size
+    select = jnp.where(lax.broadcasted_iota(jnp.int32, (total, width), 0) == level, 1.0, 0.0).astype(jnp.bfloat16)
+    high, low = (
+        jnp.dot(v, select, preferred_element_type=jnp.float32).astype(jnp.bfloat16) for v in split(balance[...])
+    )
+    return jnp.concatenate([high, high, low], axis=1)
+
+
+def weighted(balance, places, pieces, columns, emit):
+    total = balance.shape[0]
     count, tiles, height, _ = columns.shape
     pitch = tiles * height
-    columns[: near.shape[0]] = near[...]
-    unpack(pieces, packing(tiles * LANES, 2 * tiles, lax.axis_index("lon"), 0), columns, near.shape[0])
+    unpack(pieces, packing(tiles * LANES, 2 * tiles, lax.axis_index("lon"), 0), columns)
     flat = columns.reshape(count * pitch, LANES)
-    high, low = split(weights[...])
-    stacked = jnp.concatenate([high, high, low], axis=1)
-    for r in range(height):
-        for t in range(tiles):
+    stacked = chosen(balance, places, count)
+    for t in range(tiles):
+        for r in range(height):
             top, rest = split(flat[pl.ds(t * height + r, count, stride=pitch), :])
             right = jnp.concatenate([top, rest, top], axis=0)
-            result[pl.ds(t * height + r, total, stride=pitch), :] = jnp.dot(
-                stacked, right, preferred_element_type=jnp.float32
+            value = jnp.dot(stacked, right, preferred_element_type=jnp.float32)
+            emit(t, r, pl.ds(t * height + r, total, stride=pitch), value)
+
+
+def early_kernel(places, weights, *refs):
+    *pieces, out, columns = refs
+
+    def store(t, r, rows, value):
+        out[rows, :] = value
+
+    weighted(weights, places, pieces, columns, store)
+
+
+def late_kernel(places, weights, early, *refs):
+    *pieces, out, columns, result, sent = refs
+    total = weights.shape[0]
+    tiles, height = columns.shape[1:3]
+    copies = []
+
+    def store(t, r, rows, value):
+        result[rows, :] = early[rows, :] + value
+        if r == height - 1:
+            copy = pltpu.make_async_copy(
+                result.reshape(total, tiles, height, LANES).at[:, t],
+                out.at[:, :, pl.ds(t * LANES, LANES)],
+                sent.at[t],
             )
-    for t in range(tiles):
-        for l in range(total):
-            start = l * pitch + t * height
-            out[l, :, t * LANES : (t + 1) * LANES] = result[start : start + height, :]
-
-
-def balanced(weights, near, pieces):
-    _, tiles, height, _ = near.shape
-    total, count = weights.shape
+            copy.start()
+            copies.append(copy)
+
+    weighted(weights, places, pieces, columns, store)
+    for copy in copies:
+        copy.wait()
+
+
+def balanced(weights, places, pieces, early=None):
+    total, count = weights.shape[0], sum(2 * p.shape[1] for p in pieces)
+    tiles, height = pieces[0].shape[2:4]
+    flat = (total * tiles * height, LANES)
+    columns = VMEM((count, tiles, height, LANES), jnp.float32)
+    if early is None:
+        return pl.pallas_call(
+            functools.partial(early_kernel, places),
+            out_shape=jax.ShapeDtypeStruct(flat, jnp.float32),
+            in_specs=[whole()] * (1 + len(pieces)),
+            out_specs=whole(),
+            scratch_shapes=[columns],
+            compiler_params=budget(10),
+        )(weights, *pieces)
     return pl.pallas_call(
-        balance_kernel,
+        functools.partial(late_kernel, places),
         out_shape=jax.ShapeDtypeStruct((total, height, tiles * LANES), jnp.float32),
         in_specs=[whole()] * (2 + len(pieces)),
-        out_specs=whole(),
-        scratch_shapes=[
-            VMEM((count, tiles, height, LANES), jnp.float32),
-            VMEM((total * tiles * height, LANES), jnp.float32),
-        ],
-        compiler_params=budget(12),
-    )(weights, near, *pieces)
+        out_specs=pl.BlockSpec(memory_space=pl.ANY),
+        scratch_shapes=[columns, VMEM(flat, jnp.float32), pltpu.SemaphoreType.DMA((tiles,))],
+        compiler_params=budget(10),
+    )(weights, early, *pieces)
 
 
 def crossed(block, *axes):
@@ -337,7 +372,7 @@
     return lax.dynamic_slice_in_dim(block, index * size, size, axis=axis)
 
 
-def gathered(kept, came, weights_of):
+def gathered(kept, came, balance, levels):
     core, member, groups = (lax.axis_index("lon"), lax.axis_index("member"), lax.axis_size("lev"))
     halves = [jnp.concatenate([*half], axis=2) for half in (kept[2:], came[2:], kept[:2], came[:2])]
     rows = jnp.concatenate([jnp.stack(halves[:2]), crossed(jnp.stack(halves[2:]), "member")])
@@ -346,9 +381,11 @@
     values = pieces.transpose(0, 1, 3, 2, 4).reshape(count * share, height, tiles * LANES)
     matrix = packing(tiles * LANES, 2 * tiles, core, 0).astype(jnp.float32)
     values = jnp.einsum("mrp,pc->mrc", values, matrix, precision=lax.Precision.HIGHEST)
-    weights = weights_of(
-        [(g, m, c) for g in range(groups) for m in (member, 1 - member) for c in (core, 1 - core)]
-    )
+    spare = 4 * share - levels
+    padded = jnp.pad(balance.reshape(-1, groups, levels), ((0, 0), (0, 0), (0, spare)))
+    padded = padded.reshape(-1, groups * 4 * share)
+    order = [(g, m, c) for g in range(groups) for m in (member, 1 - member) for c in (core, 1 - core)]
+    weights = jnp.concatenate([part(padded, g * 4 + m * 2 + c, share, 1) for g, m, c in order], axis=1)
     return jnp.einsum("lm,mrc->lrc", weights, values, precision=lax.Precision.HIGHEST)
 
 
@@ -375,25 +412,32 @@
     other_base = crossed(base, "member")
     tiles = breadth * cores // LANES
     sizes = (levels, halo, (share, tiles, pitch, SUB, LANES), height * strips, breadth * cores)
-    source = noise(other_base, base, *sizes)
-    *kept, sent = diffuse(halo, groups == 2, mine, theirs, top, bottom, source)
-
-    def weights_of(order):
-        padded = jnp.pad(balance.reshape(-1, groups, levels), ((0, 0), (0, 0), (0, spare)))
-        padded = padded.reshape(-1, groups * 4 * share)
-        return jnp.concatenate([part(padded, g * 4 + m * 2 + c, share, 1) for g, m, c in order], axis=1)
-
-    came = crossed(sent, "lon")
+    own_source = noise(base, *sizes)
+    other_source = noise(other_base, *sizes)
+    blocks = range(share // math.gcd(share, SOME))
+    operands = (mine, theirs, top, bottom, other_source, own_source)
+
     if groups != 2:
-        return gathered(kept, came, weights_of)
-    other_near, other_far, near, far = (jnp.stack([a, b]) for a, b in zip(kept, came))
-    diagonal = crossed(other_far, "member", "lev")
-    along_x = crossed(far, "lev")
-    along_y = crossed(other_near, "member")
-    places = [(group, member), (group, 1 - member), (1 - group, 1 - member), (1 - group, member)]
-    weights = weights_of([(g, m, c) for g, m in places for c in (core, 1 - core)])
-    near = unpacked((near, along_y))
-    return balanced(weights, near, (diagonal, along_x))
+        *kept, sent = diffuse(halo, False, blocks, *operands)
+        return gathered(kept, crossed(sent, "lon"), balance, levels)
+    cut = max(1, len(blocks) * 3 // 3)
+    parts, start = {}, 0
+    for i, some_blocks in enumerate(filter(len, (blocks[:cut], blocks[cut:]))):
+        *kept, sent = diffuse(halo, True, some_blocks, *operands)
+        came = crossed(sent, "lon")
+        other_near, other_far, near, far = (jnp.stack([a, b]) for a, b in zip(kept, came))
+        size = near.shape[1]
+        parts["near", i] = near, (False, False, start, size)
+        parts["diagonal", i] = crossed(other_far, "member", "lev"), (True, True, start, size)
+        parts["x", i] = crossed(far, "lev"), (True, False, start, size)
+        parts["y", i] = crossed(other_near, "member"), (False, True, start, size)
+        start += size
+    late = [parts[name, max(i for _, i in parts)] for name in ("x", "y")]
+    soon = [p for p in parts.values() if all(p is not q for q in late)]
+    pieces, places = zip(*soon)
+    early = balanced(balance, places, pieces)
+    pieces, places = zip(*late)
+    return balanced(balance, places, pieces, early)
 
 
 def solution(mesh):

time: 61.5 us -> 58.1 us (0.945)
  waiting for transfers between devices: 26.5 us -> 21.2 us
  Pallas kernels: 19.2 us -> 20.3 us
  starting transfers between devices: 12.1 us -> 13.2 us
    ppermute x7, waiting for transfers between devices: 24.7 us -> 20.8 us  [crossed(): return lax.ppermute(block, axes, [(i, count - 1 - i) for i in range(count)])]
    ppermute x2, waiting for transfers between devices: 1.8 us -> 0.38 us  [shifted(): lax.ppermute(block, 'lat', [(i, i + step) for i in range(strips) if 0 <=...]
    pallas_call x3, Pallas kernels: 14.9 us -> 15.7 us  [the longest x1 10.6 us: diffuse(): pl.pallas_call(functools.partial(diffuse_kernel, halo, halves, blocks[0])...]
    ppermute x2, starting transfers between devices: 6.16 us -> 6.79 us  [shifted(): lax.ppermute(block, 'lat', [(i, i + step) for i in range(strips) if 0 <=...]
    pallas_call x1 -> x2, Pallas kernels: 3.61 us -> 3.83 us  [noise(): pl.pallas_call(functools.partial(noise_kernel, levels_here, halo, total_r...]
  transfers between devices with their start and end apart: 9 -> 9, of which waited for: 5 -> 5; matrix products, arithmetic and copies ran while one was open for 1% -> 0% of each run, Pallas kernels for 7% -> 10%
where the time goes in v6:
time: 58.1 us; the launch traced here: 57.9 us
  waiting for transfers between devices  21.2 us (36%)
  Pallas kernels  20.3 us (35%)
  starting transfers between devices  13.2 us (23%)
  other arithmetic  1.73 us (3%)
  between operations  1.43 us (2%)
    ppermute x7, waiting for transfers between devices, crossed(): return lax.ppermute(block, axes, [(i, count - 1 - i) for i in range(count)])  20.8 us
    pallas_call x1, Pallas kernels, diffuse(): pl.pallas_call(functools.partial(diffuse_kernel, halo, halves, blocks[0])...  10.6 us
    ppermute x2, starting transfers between devices, shifted(): lax.ppermute(block, 'lat', [(i, i + step) for i in range(strips) if 0 <=...  6.79 us
    ppermute x7, starting transfers between devices, crossed(): return lax.ppermute(block, axes, [(i, count - 1 - i) for i in range(count)])  6.37 us
    pallas_call x2, Pallas kernels, noise(): pl.pallas_call(functools.partial(noise_kernel, levels_here, halo, total_r...  3.83 us
    pallas_call x1, Pallas kernels, balanced(): pl.pallas_call(functools.partial(late_kernel, places), out_shape=jax.Shap...  3.22 us
    pallas_call x1, Pallas kernels, balanced(): pl.pallas_call(functools.partial(early_kernel, places), out_shape=jax.Sha...  1.95 us
    mul x1, other arithmetic, per_device(): part(diffusivity, member * 2 + c, share, 0)  1.54 us
  transfers between devices with their start and end apart: 9, of which 5 were waited for; matrix products, arithmetic and copies ran while one was open for 0% of the time, Pallas kernels for 10%

profile of v6, /device:TPU:0, one launch (start us, length us, event | category | flops | bytes accessed | tf_op | source)
XLA Modules:
  0.0 57.9 jit_solution(4888483759961113980)
XLA Ops:
  0.0 1.5 %convert_multiply_fusion = (f32[9,32,384]{2,1,0:T(8,128)S(1)}, f32[9,32,384]{2,1,0:T(8,128)S(1)}) fusion(s32[36,32,384]{2,1,0:T(8,128)} %param.5, s32[]{:T(128)S(6)} %select_n.9, f32[36,32,384]{2,1,0:T(8,128)} %param.6, s32[]{:T(128)S(6)} %select_n.8), kind=kLoop, calls=%fused_computation.6 | loop fusion | flops 442368 | bytes 2654216 | tf_op jit(solution)/shard_map/mul | solution.py:404
  1.5 0.7 %shard_map.55 = (f32[9,3,32,128]{3,2,1,0:T(8,128)S(1)}, f32[9,3,32,128]{3,2,1,0:T(8,128)S(1)}, f32[2,3,112,128]{3,2,1,0:T(8,128)S(1)}, f32[2,3,112,128]{3,2,1,0:T(8,128)S(1)}) custom-call(f32[9,32,384]{2,1,0:T(8,128)S(1)} %get-tuple-element.24.kept, f32[9,32,384]{2,1,0:T(8,128)S(1)} %get-tuple-element.23.other), custom_call_target="tpu_custom_call" | custom-call | tf_op jit(solution)/shard_map/pallas_call | solution.py:94
  2.3 0.5 collective-permute-start.1
  2.8 0.1 collective-permute-start
  2.9 1.2 %collective-permute-done.1 = f32[2,3,112,128]{3,2,1,0:T(8,128)S(1)} collective-permute-done((f32[2,3,112,128]{3,2,1,0:T(8,128)S(1)}, f32[2,3,112,128]{3,2,1,0:T(8,128)S(1)}, u32[]{:S(2)}, u32[]{:S(2)}) %collective-permute-start.1) | collective-permute-done | bytes 344096 | tf_op jit(solution)/shard_map/ppermute | solution.py:363
  4.1 1.3 %collective-permute-start.3 = (f32[2,3,112,128]{3,2,1,0:T(8,128)S(1)}, f32[2,3,112,128]{3,2,1,0:T(8,128)S(1)}, u32[]{:S(2)}, u32[]{:S(2)}) collective-permute-start(f32[2,3,112,128]{3,2,1,0:T(8,128)S(1)} %get-tuple-element.29), channel_id=1, source_target_pairs={{4,0},{8,4},{12,8},{5,1},{9,5},{13,9},{6,2},{10,6},{14,10},{7,3},{... | collective-permute-start | bytes 1032200 | tf_op jit(solution)/shard_map/ppermute | solution.py:368
  5.4 5.5 %collective-permute-start.2 = (f32[2,3,112,128]{3,2,1,0:T(8,128)S(1)}, f32[2,3,112,128]{3,2,1,0:T(8,128)S(1)}, u32[]{:S(2)}, u32[]{:S(2)}) collective-permute-start(f32[2,3,112,128]{3,2,1,0:T(8,128)S(1)} %get-tuple-element.30), channel_id=1, source_target_pairs={{0,4},{4,8},{8,12},{1,5},{5,9},{9,13},{2,6},{6,10},{10,14},{3,7},{... | collective-permute-start | bytes 1032200 | tf_op jit(solution)/shard_map/ppermute | solution.py:368
  12.3 2.0 %collective-permute-start.4 = (s32[8,128]{1,0:T(8,128)S(1)}, s32[8,128]{1,0:T(8,128)S(1)}, u32[]{:S(2)}, u32[]{:S(2)}) collective-permute-start(s32[8,128]{1,0:T(8,128)S(1)} %broadcast_in_dim.3.base), channel_id=1, source_target_pairs={{0,16},{16,0},{1,17},{17,1},{2,18},{18,2},{3,19},{19,3},{4,20},{20... | collective-permute-start | bytes 12296 | tf_op jit(solution)/shard_map/ppermute | solution.py:363
  14.3 1.9 %shard_map.57.own_source = f32[9,6,7,8,128]{4,3,2,1,0:T(8,128)S(1)} custom-call(s32[8,128]{1,0:T(8,128)S(1)} %broadcast_in_dim.3.base), custom_call_target="tpu_custom_call" | custom-call | tf_op jit(solution)/shard_map/pallas_call | solution.py:123
  16.2 0.0 collective-permute-done.4.base
  16.2 1.9 %shard_map.56.other_source = f32[9,6,7,8,128]{4,3,2,1,0:T(8,128)S(1)} custom-call(s32[8,128]{1,0:T(8,128)S(1)} %collective-permute-done.4.base), custom_call_target="tpu_custom_call" | custom-call | tf_op jit(solution)/shard_map/pallas_call | solution.py:123
  18.1 0.4 collective-permute-done.2.top
  18.5 10.6 %shard_map.58 = (f32[9,3,16,128]{3,2,1,0:T(8,128)S(1)}, f32[9,3,16,128]{3,2,1,0:T(8,128)S(1)}, f32[9,3,16,128]{3,2,1,0:T(8,128)S(1)}, f32[9,3,16,128]{3,2,1,0:T(8,128)S(1)}, f32[4,9,3,16,128]{4,3,2,1,0:T(8,128)S(1)}) custom-call(f32[9,3,32,128]{3,2,1,0:T(8,128)S(1)} %get-tuple-element.14.mine, f32[9,3,32,128]{3,2,1,0:T(8,128)S(1)} %collective-permute-done.theirs, ...), custom_call_target="tpu_custom_call" | custom-call | tf_op jit(solution)/shard_map/pallas_call | solution.py:248
  29.1 0.1 collective-permute-start.5
  29.2 2.4 %collective-permute-done.5 = f32[4,9,3,16,128]{4,3,2,1,0:T(8,128)S(1)} collective-permute-done((f32[4,9,3,16,128]{4,3,2,1,0:T(8,128)S(1)}, f32[4,9,3,16,128]{4,3,2,1,0:T(8,128)S(1)}, u32[]{:S(2)}, u32[]{:S(2)}) %collective-permute-start.5) | collective-permute-done | bytes 884768 | tf_op jit(solution)/shard_map/ppermute | solution.py:363
  31.6 0.1 fusion.3
  31.7 0.0 copy-start
  31.7 2.7 %collective-permute-start.6 = (f32[2,9,3,16,128]{4,3,2,1,0:T(8,128)S(1)}, f32[2,9,3,16,128]{4,3,2,1,0:T(8,128)S(1)}, u32[]{:S(2)}, u32[]{:S(2)}) collective-permute-start(f32[2,9,3,16,128]{4,3,2,1,0:T(8,128)S(1)} %pad_maximum_fusion.1), channel_id=1, source_target_pairs={{0,18},{2,16},{16,2},{18,0},{1,19},{3,17},{17,3},{19,1},{4,22},{6,... | collective-permute-start | bytes 1327112 | tf_op jit(solution)/shard_map/ppermute | solution.py:363
  34.4 0.6 %collective-permute-start.7 = (f32[2,9,3,16,128]{4,3,2,1,0:T(8,128)S(1)}, f32[2,9,3,16,128]{4,3,2,1,0:T(8,128)S(1)}, u32[]{:S(2)}, u32[]{:S(2)}) collective-permute-start(f32[2,9,3,16,128]{4,3,2,1,0:T(8,128)S(1)} %pad_maximum_fusion.2), channel_id=1, source_target_pairs={{0,2},{2,0},{1,3},{3,1},{4,6},{6,4},{5,7},{7,5},{8,10},{10,8},{9,1... | collective-permute-start | bytes 1327112 | tf_op jit(solution)/shard_map/ppermute | solution.py:363
  35.1 0.4 collective-permute-start.8
  35.5 10.2 %collective-permute-done.6.refs_1_ = f32[2,9,3,16,128]{4,3,2,1,0:T(8,128)S(1)} collective-permute-done((f32[2,9,3,16,128]{4,3,2,1,0:T(8,128)S(1)}, f32[2,9,3,16,128]{4,3,2,1,0:T(8,128)S(1)}, u32[]{:S(2)}, u32[]{:S(2)}) %collective-permute-start.6) | collective-permute-done | bytes 442400 | tf_op jit(solution)/shard_map/ppermute | solution.py:363
  45.7 2.0 %shard_map.59.early = f32[3456,128]{1,0:T(8,128)S(1)} custom-call(f32[72,72]{1,0:T(8,128)S(1)} %copy-done, f32[2,9,3,16,128]{4,3,2,1,0:T(8,128)S(1)} %pad_maximum_fusion.refs_0_, f32[2,9,3,16,128]{4,3,2,1,0:T(8,128)S(1)} %collective-permute-done.6.refs_1_), custom_call_target="tpu_custom_call" | custom-call | tf_op jit(solution)/shard_map/pallas_call | solution.py:343
  47.7 6.9 %collective-permute-done.7.refs_0_ = f32[2,9,3,16,128]{4,3,2,1,0:T(8,128)S(1)} collective-permute-done((f32[2,9,3,16,128]{4,3,2,1,0:T(8,128)S(1)}, f32[2,9,3,16,128]{4,3,2,1,0:T(8,128)S(1)}, u32[]{:S(2)}, u32[]{:S(2)}) %collective-permute-start.7) | collective-permute-done | bytes 442400 | tf_op jit(solution)/shard_map/ppermute | solution.py:363
  54.6 3.2 %shard_map.60 = f32[72,16,384]{2,1,0:T(8,128)} custom-call(f32[72,72]{1,0:T(8,128)S(1)} %copy-done, f32[3456,128]{1,0:T(8,128)S(1)} %shard_map.59.early, f32[2,9,3,16,128]{4,3,2,1,0:T(8,128)S(1)} %collective-permute-done.7.refs_0_, f32[2,9,3,16,128]{4,3,2,1,0:T(8,128)S(1)} %collective-permute-done.8.refs_1_), custom_call_target="tpu_custom_call" | custom-call | tf_op jit(solution)/shard_map/pallas_call | solution.py:351
  (10 shorter events, 0.2 us)
Async XLA Ops:
  2.3 1.8 %collective-permute-start.1 = (f32[2,3,112,128]{3,2,1,0:T(8,128)S(1)}, f32[2,3,112,128]{3,2,1,0:T(8,128)S(1)}, u32[]{:S(2)}, u32[]{:S(2)}) collective-permute-start(f32[2,3,112,128]{3,2,1,0:T(8,128)S(1)} %get-tuple-element.17), channel_id=1, source_target_pairs={{0,1},{1,0},{2,3},{3,2},{4,5},{5,4},{6,7},{7,6},{8,9},{9,8},{10,11... | collective-permute-start | bytes 1032200 | tf_op jit(solution)/shard_map/ppermute | solution.py:363
  2.8 15.3 %collective-permute-start = (f32[9,3,32,128]{3,2,1,0:T(8,128)S(1)}, f32[9,3,32,128]{3,2,1,0:T(8,128)S(1)}, u32[]{:S(2)}, u32[]{:S(2)}) collective-permute-start(f32[9,3,32,128]{3,2,1,0:T(8,128)S(1)} %get-tuple-element.15), channel_id=1, source_target_pairs={{0,1},{1,0},{2,3},{3,2},{4,5},{5,4},{6,7},{7,6},{8,9},{9,8},{10,11... | collective-permute-start | bytes 1327112 | tf_op jit(solution)/shard_map/ppermute | solution.py:363
  4.1 14.0 %collective-permute-start.3 = (f32[2,3,112,128]{3,2,1,0:T(8,128)S(1)}, f32[2,3,112,128]{3,2,1,0:T(8,128)S(1)}, u32[]{:S(2)}, u32[]{:S(2)}) collective-permute-start(f32[2,3,112,128]{3,2,1,0:T(8,128)S(1)} %get-tuple-element.29), channel_id=1, source_target_pairs={{4,0},{8,4},{12,8},{5,1},{9,5},{13,9},{6,2},{10,6},{14,10},{7,3},{... | collective-permute-start | bytes 1032200 | tf_op jit(solution)/shard_map/ppermute | solution.py:368
  5.4 13.1 %collective-permute-start.2 = (f32[2,3,112,128]{3,2,1,0:T(8,128)S(1)}, f32[2,3,112,128]{3,2,1,0:T(8,128)S(1)}, u32[]{:S(2)}, u32[]{:S(2)}) collective-permute-start(f32[2,3,112,128]{3,2,1,0:T(8,128)S(1)} %get-tuple-element.30), channel_id=1, source_target_pairs={{0,4},{4,8},{8,12},{1,5},{5,9},{9,13},{2,6},{6,10},{10,14},{3,7},{... | collective-permute-start | bytes 1032200 | tf_op jit(solution)/shard_map/ppermute | solution.py:368
  12.3 3.9 %collective-permute-start.4 = (s32[8,128]{1,0:T(8,128)S(1)}, s32[8,128]{1,0:T(8,128)S(1)}, u32[]{:S(2)}, u32[]{:S(2)}) collective-permute-start(s32[8,128]{1,0:T(8,128)S(1)} %broadcast_in_dim.3.base), channel_id=1, source_target_pairs={{0,16},{16,0},{1,17},{17,1},{2,18},{18,2},{3,19},{19,3},{4,20},{20... | collective-permute-start | bytes 12296 | tf_op jit(solution)/shard_map/ppermute | solution.py:363
  29.1 2.5 %collective-permute-start.5 = (f32[4,9,3,16,128]{4,3,2,1,0:T(8,128)S(1)}, f32[4,9,3,16,128]{4,3,2,1,0:T(8,128)S(1)}, u32[]{:S(2)}, u32[]{:S(2)}) collective-permute-start(f32[4,9,3,16,128]{4,3,2,1,0:T(8,128)S(1)} %get-tuple-element.19), channel_id=1, source_target_pairs={{0,1},{1,0},{2,3},{3,2},{4,5},{5,4},{6,7},{7,6},{8,9},{9,8},{10,11... | collective-permute-start | bytes 2654216 | tf_op jit(solution)/shard_map/ppermute | solution.py:363
  31.7 14.1 %copy-start = (f32[72,72]{1,0:T(8,128)S(1)}, f32[72,72]{1,0:T(8,128)}, u32[]{:S(2)}) copy-start(f32[72,72]{1,0:T(8,128)} %weights.3) | copy-start | bytes 62212
  31.7 14.0 %collective-permute-start.6 = (f32[2,9,3,16,128]{4,3,2,1,0:T(8,128)S(1)}, f32[2,9,3,16,128]{4,3,2,1,0:T(8,128)S(1)}, u32[]{:S(2)}, u32[]{:S(2)}) collective-permute-start(f32[2,9,3,16,128]{4,3,2,1,0:T(8,128)S(1)} %pad_maximum_fusion.1), channel_id=1, source_target_pairs={{0,18},{2,16},{16,2},{18,0},{1,19},{3,17},{17,3},{19,1},{4,22},{6,... | collective-permute-start | bytes 1327112 | tf_op jit(solution)/shard_map/ppermute | solution.py:363
  34.4 20.2 %collective-permute-start.7 = (f32[2,9,3,16,128]{4,3,2,1,0:T(8,128)S(1)}, f32[2,9,3,16,128]{4,3,2,1,0:T(8,128)S(1)}, u32[]{:S(2)}, u32[]{:S(2)}) collective-permute-start(f32[2,9,3,16,128]{4,3,2,1,0:T(8,128)S(1)} %pad_maximum_fusion.2), channel_id=1, source_target_pairs={{0,2},{2,0},{1,3},{3,1},{4,6},{6,4},{5,7},{7,5},{8,10},{10,8},{9,1... | collective-permute-start | bytes 1327112 | tf_op jit(solution)/shard_map/ppermute | solution.py:363
  35.1 19.6 %collective-permute-start.8 = (f32[2,9,3,16,128]{4,3,2,1,0:T(8,128)S(1)}, f32[2,9,3,16,128]{4,3,2,1,0:T(8,128)S(1)}, u32[]{:S(2)}, u32[]{:S(2)}) collective-permute-start(f32[2,9,3,16,128]{4,3,2,1,0:T(8,128)S(1)} %pad_maximum_fusion.3), channel_id=1, source_target_pairs={{0,16},{16,0},{1,17},{17,1},{2,18},{18,2},{3,19},{19,3},{4,20},{20... | collective-permute-start | bytes 1327112 | tf_op jit(solution)/shard_map/ppermute | solution.py:363

commit v7 on v6

--- a/solution.py
+++ b/solution.py
@@ -131,28 +131,27 @@
 
 def neighbour_sums(old, tiles, pitch, emit):
     some = range(old.shape[0])
-    first = [[old[g, t, 0] for t in range(tiles)] for g in some]
-    last = [[old[g, t, pitch - 1] for t in range(tiles)] for g in some]
-    above = [[pltpu.roll(v, 1, 0) for v in last[g]] for g in some]
+
+    def row(g, k):
+        values = [old[g, t, k] for t in range(tiles)]
+        return [pltpu.roll(values[-1], 1, 1), *values, pltpu.roll(values[0], LANES - 1, 1)]
+
+    first = [row(g, 0) for g in some]
+    above = [[pltpu.roll(old[g, t, pitch - 1], 1, 0) for t in range(tiles)] for g in some]
+    pairs = [[above[g][t] + first[g][t] for t in range(tiles)] for g in some]
     here = first
     for k in range(pitch):
         if k == pitch - 1:
-            below = [[pltpu.roll(v, SUB - 1, 0) for v in first[g]] for g in some]
-        elif k == pitch - 2:
-            below = last
+            below = [[None, *(pltpu.roll(v, SUB - 1, 0) for v in first[g][1:-1]), None] for g in some]
         else:
-            below = [[old[g, t, k + 1] for t in range(tiles)] for g in some]
+            below = [row(g, k + 1) for g in some]
         for g in some:
-            row = here[g]
-            west = [pltpu.roll(row[-1], 1, 1)] + row[:-1]
-            east = row[1:] + [pltpu.roll(row[0], LANES - 1, 1)]
-            for t in ORDER(tiles):
-                emit(g, t, k, row[t], (west[t] + east[t]) + (above[g][t] + below[g][t]))
-        above, here = here, below
-
-
-def ORDER(tiles):
-    return [*range(1, tiles - 1), 0, tiles - 1]
+            now, later = here[g], below[g]
+            fresh = [None if t == 0 and later[0] is None else now[t + 1] + later[t] for t in range(tiles + 1)]
+            for t in range(tiles):
+                emit(g, t, k, now[t + 1], fresh[t + 1] + pairs[g][t])
+            pairs[g] = fresh
+        here = below
 
 
 def diffuse_kernel(halo, halves, start_block, mine, theirs, top, bottom, other_source, own_source, *refs):
@@ -206,12 +205,8 @@
 
         neighbour_sums(cond, tiles, pitch, prepare)
 
-        @pl.loop(0, (SWEEPS - 2) // 2)
-        def _(i):
-            sweep(u0, u1)
-            sweep(u1, u0)
-
-        sweep(u0, u1)
+        for i in range(SWEEPS - 1):
+            sweep(*((u0, u1) if i % 2 == 0 else (u1, u0)))
 
         def finish(g, t, k, value, total):
             i, g = divmod(g, some)

time: 58.1 us -> 56.3 us (0.969)
  Pallas kernels: 20.3 us -> 18.5 us
    pallas_call x1, Pallas kernels: 10.6 us -> 8.79 us  [diffuse(): pl.pallas_call(functools.partial(diffuse_kernel, halo, halves, blocks[0])...]
where the time goes in v7:
time: 56.3 us; the launch traced here: 56.1 us
  waiting for transfers between devices  21.2 us (38%)
  Pallas kernels  18.5 us (33%)
  starting transfers between devices  13.2 us (23%)
  other arithmetic  1.73 us (3%)
  between operations  1.43 us (3%)
    ppermute x7, waiting for transfers between devices, crossed(): return lax.ppermute(block, axes, [(i, count - 1 - i) for i in range(count)])  20.8 us
    pallas_call x1, Pallas kernels, diffuse(): pl.pallas_call(functools.partial(diffuse_kernel, halo, halves, blocks[0])...  8.79 us
    ppermute x2, starting transfers between devices, shifted(): lax.ppermute(block, 'lat', [(i, i + step) for i in range(strips) if 0 <=...  6.79 us
    ppermute x7, starting transfers between devices, crossed(): return lax.ppermute(block, axes, [(i, count - 1 - i) for i in range(count)])  6.37 us
    pallas_call x2, Pallas kernels, noise(): pl.pallas_call(functools.partial(noise_kernel, levels_here, halo, total_r...  3.83 us
    pallas_call x1, Pallas kernels, balanced(): pl.pallas_call(functools.partial(late_kernel, places), out_shape=jax.Shap...  3.22 us
    pallas_call x1, Pallas kernels, balanced(): pl.pallas_call(functools.partial(early_kernel, places), out_shape=jax.Sha...  1.96 us
    mul x1, other arithmetic, per_device(): part(diffusivity, member * 2 + c, share, 0)  1.54 us
  transfers between devices with their start and end apart: 9, of which 5 were waited for; matrix products, arithmetic and copies ran while one was open for 0% of the time, Pallas kernels for 10%

profile of v7, /device:TPU:0, one launch (start us, length us, event | category | flops | bytes accessed | tf_op | source)
XLA Modules:
  0.0 56.1 jit_solution(6467193743742692697)
XLA Ops:
  0.0 1.5 %convert_multiply_fusion = (f32[9,32,384]{2,1,0:T(8,128)S(1)}, f32[9,32,384]{2,1,0:T(8,128)S(1)}) fusion(s32[36,32,384]{2,1,0:T(8,128)} %param.5, s32[]{:T(128)S(6)} %select_n.9, f32[36,32,384]{2,1,0:T(8,128)} %param.6, s32[]{:T(128)S(6)} %select_n.8), kind=kLoop, calls=%fused_computation.6 | loop fusion | flops 442368 | bytes 2654216 | tf_op jit(solution)/shard_map/mul | solution.py:399
  1.5 0.7 %shard_map.55 = (f32[9,3,32,128]{3,2,1,0:T(8,128)S(1)}, f32[9,3,32,128]{3,2,1,0:T(8,128)S(1)}, f32[2,3,112,128]{3,2,1,0:T(8,128)S(1)}, f32[2,3,112,128]{3,2,1,0:T(8,128)S(1)}) custom-call(f32[9,32,384]{2,1,0:T(8,128)S(1)} %get-tuple-element.24.kept, f32[9,32,384]{2,1,0:T(8,128)S(1)} %get-tuple-element.23.other), custom_call_target="tpu_custom_call" | custom-call | tf_op jit(solution)/shard_map/pallas_call | solution.py:94
  2.3 0.5 collective-permute-start.1
  2.8 0.1 collective-permute-start
  2.9 1.2 %collective-permute-done.1 = f32[2,3,112,128]{3,2,1,0:T(8,128)S(1)} collective-permute-done((f32[2,3,112,128]{3,2,1,0:T(8,128)S(1)}, f32[2,3,112,128]{3,2,1,0:T(8,128)S(1)}, u32[]{:S(2)}, u32[]{:S(2)}) %collective-permute-start.1) | collective-permute-done | bytes 344096 | tf_op jit(solution)/shard_map/ppermute | solution.py:358
  4.1 1.3 %collective-permute-start.3 = (f32[2,3,112,128]{3,2,1,0:T(8,128)S(1)}, f32[2,3,112,128]{3,2,1,0:T(8,128)S(1)}, u32[]{:S(2)}, u32[]{:S(2)}) collective-permute-start(f32[2,3,112,128]{3,2,1,0:T(8,128)S(1)} %get-tuple-element.29), channel_id=1, source_target_pairs={{4,0},{8,4},{12,8},{5,1},{9,5},{13,9},{6,2},{10,6},{14,10},{7,3},{... | collective-permute-start | bytes 1032200 | tf_op jit(solution)/shard_map/ppermute | solution.py:363
  5.4 5.5 %collective-permute-start.2 = (f32[2,3,112,128]{3,2,1,0:T(8,128)S(1)}, f32[2,3,112,128]{3,2,1,0:T(8,128)S(1)}, u32[]{:S(2)}, u32[]{:S(2)}) collective-permute-start(f32[2,3,112,128]{3,2,1,0:T(8,128)S(1)} %get-tuple-element.30), channel_id=1, source_target_pairs={{0,4},{4,8},{8,12},{1,5},{5,9},{9,13},{2,6},{6,10},{10,14},{3,7},{... | collective-permute-start | bytes 1032200 | tf_op jit(solution)/shard_map/ppermute | solution.py:363
  12.3 2.0 %collective-permute-start.4 = (s32[8,128]{1,0:T(8,128)S(1)}, s32[8,128]{1,0:T(8,128)S(1)}, u32[]{:S(2)}, u32[]{:S(2)}) collective-permute-start(s32[8,128]{1,0:T(8,128)S(1)} %broadcast_in_dim.3.base), channel_id=1, source_target_pairs={{0,16},{16,0},{1,17},{17,1},{2,18},{18,2},{3,19},{19,3},{4,20},{20... | collective-permute-start | bytes 12296 | tf_op jit(solution)/shard_map/ppermute | solution.py:358
  14.3 1.9 %shard_map.57.own_source = f32[9,6,7,8,128]{4,3,2,1,0:T(8,128)S(1)} custom-call(s32[8,128]{1,0:T(8,128)S(1)} %broadcast_in_dim.3.base), custom_call_target="tpu_custom_call" | custom-call | tf_op jit(solution)/shard_map/pallas_call | solution.py:123
  16.2 0.0 collective-permute-done.4.base
  16.2 1.9 %shard_map.56.other_source = f32[9,6,7,8,128]{4,3,2,1,0:T(8,128)S(1)} custom-call(s32[8,128]{1,0:T(8,128)S(1)} %collective-permute-done.4.base), custom_call_target="tpu_custom_call" | custom-call | tf_op jit(solution)/shard_map/pallas_call | solution.py:123
  18.1 0.4 collective-permute-done.2.top
  18.5 8.8 %shard_map.58 = (f32[9,3,16,128]{3,2,1,0:T(8,128)S(1)}, f32[9,3,16,128]{3,2,1,0:T(8,128)S(1)}, f32[9,3,16,128]{3,2,1,0:T(8,128)S(1)}, f32[9,3,16,128]{3,2,1,0:T(8,128)S(1)}, f32[4,9,3,16,128]{4,3,2,1,0:T(8,128)S(1)}) custom-call(f32[9,3,32,128]{3,2,1,0:T(8,128)S(1)} %get-tuple-element.14.mine, f32[9,3,32,128]{3,2,1,0:T(8,128)S(1)} %collective-permute-done.theirs, ...), custom_call_target="tpu_custom_call" | custom-call | tf_op jit(solution)/shard_map/pallas_call | solution.py:243
  27.3 0.1 collective-permute-start.5
  27.4 2.4 %collective-permute-done.5 = f32[4,9,3,16,128]{4,3,2,1,0:T(8,128)S(1)} collective-permute-done((f32[4,9,3,16,128]{4,3,2,1,0:T(8,128)S(1)}, f32[4,9,3,16,128]{4,3,2,1,0:T(8,128)S(1)}, u32[]{:S(2)}, u32[]{:S(2)}) %collective-permute-start.5) | collective-permute-done | bytes 884768 | tf_op jit(solution)/shard_map/ppermute | solution.py:358
  29.8 0.1 fusion.3
  29.9 0.0 copy-start
  29.9 2.7 %collective-permute-start.6 = (f32[2,9,3,16,128]{4,3,2,1,0:T(8,128)S(1)}, f32[2,9,3,16,128]{4,3,2,1,0:T(8,128)S(1)}, u32[]{:S(2)}, u32[]{:S(2)}) collective-permute-start(f32[2,9,3,16,128]{4,3,2,1,0:T(8,128)S(1)} %pad_maximum_fusion.1), channel_id=1, source_target_pairs={{0,18},{2,16},{16,2},{18,0},{1,19},{3,17},{17,3},{19,1},{4,22},{6,... | collective-permute-start | bytes 1327112 | tf_op jit(solution)/shard_map/ppermute | solution.py:358
  32.7 0.6 %collective-permute-start.7 = (f32[2,9,3,16,128]{4,3,2,1,0:T(8,128)S(1)}, f32[2,9,3,16,128]{4,3,2,1,0:T(8,128)S(1)}, u32[]{:S(2)}, u32[]{:S(2)}) collective-permute-start(f32[2,9,3,16,128]{4,3,2,1,0:T(8,128)S(1)} %pad_maximum_fusion.2), channel_id=1, source_target_pairs={{0,2},{2,0},{1,3},{3,1},{4,6},{6,4},{5,7},{7,5},{8,10},{10,8},{9,1... | collective-permute-start | bytes 1327112 | tf_op jit(solution)/shard_map/ppermute | solution.py:358
  33.3 0.4 collective-permute-start.8
  33.7 10.2 %collective-permute-done.6.refs_1_ = f32[2,9,3,16,128]{4,3,2,1,0:T(8,128)S(1)} collective-permute-done((f32[2,9,3,16,128]{4,3,2,1,0:T(8,128)S(1)}, f32[2,9,3,16,128]{4,3,2,1,0:T(8,128)S(1)}, u32[]{:S(2)}, u32[]{:S(2)}) %collective-permute-start.6) | collective-permute-done | bytes 442400 | tf_op jit(solution)/shard_map/ppermute | solution.py:358
  44.0 2.0 %shard_map.59.early = f32[3456,128]{1,0:T(8,128)S(1)} custom-call(f32[72,72]{1,0:T(8,128)S(1)} %copy-done, f32[2,9,3,16,128]{4,3,2,1,0:T(8,128)S(1)} %pad_maximum_fusion.refs_0_, f32[2,9,3,16,128]{4,3,2,1,0:T(8,128)S(1)} %collective-permute-done.6.refs_1_), custom_call_target="tpu_custom_call" | custom-call | tf_op jit(solution)/shard_map/pallas_call | solution.py:338
  45.9 6.9 %collective-permute-done.7.refs_0_ = f32[2,9,3,16,128]{4,3,2,1,0:T(8,128)S(1)} collective-permute-done((f32[2,9,3,16,128]{4,3,2,1,0:T(8,128)S(1)}, f32[2,9,3,16,128]{4,3,2,1,0:T(8,128)S(1)}, u32[]{:S(2)}, u32[]{:S(2)}) %collective-permute-start.7) | collective-permute-done | bytes 442400 | tf_op jit(solution)/shard_map/ppermute | solution.py:358
  52.9 3.2 %shard_map.60 = f32[72,16,384]{2,1,0:T(8,128)} custom-call(f32[72,72]{1,0:T(8,128)S(1)} %copy-done, f32[3456,128]{1,0:T(8,128)S(1)} %shard_map.59.early, f32[2,9,3,16,128]{4,3,2,1,0:T(8,128)S(1)} %collective-permute-done.7.refs_0_, f32[2,9,3,16,128]{4,3,2,1,0:T(8,128)S(1)} %collective-permute-done.8.refs_1_), custom_call_target="tpu_custom_call" | custom-call | tf_op jit(solution)/shard_map/pallas_call | solution.py:346
  (10 shorter events, 0.2 us)
Async XLA Ops:
  2.3 1.8 %collective-permute-start.1 = (f32[2,3,112,128]{3,2,1,0:T(8,128)S(1)}, f32[2,3,112,128]{3,2,1,0:T(8,128)S(1)}, u32[]{:S(2)}, u32[]{:S(2)}) collective-permute-start(f32[2,3,112,128]{3,2,1,0:T(8,128)S(1)} %get-tuple-element.17), channel_id=1, source_target_pairs={{0,1},{1,0},{2,3},{3,2},{4,5},{5,4},{6,7},{7,6},{8,9},{9,8},{10,11... | collective-permute-start | bytes 1032200 | tf_op jit(solution)/shard_map/ppermute | solution.py:358
  2.8 15.3 %collective-permute-start = (f32[9,3,32,128]{3,2,1,0:T(8,128)S(1)}, f32[9,3,32,128]{3,2,1,0:T(8,128)S(1)}, u32[]{:S(2)}, u32[]{:S(2)}) collective-permute-start(f32[9,3,32,128]{3,2,1,0:T(8,128)S(1)} %get-tuple-element.15), channel_id=1, source_target_pairs={{0,1},{1,0},{2,3},{3,2},{4,5},{5,4},{6,7},{7,6},{8,9},{9,8},{10,11... | collective-permute-start | bytes 1327112 | tf_op jit(solution)/shard_map/ppermute | solution.py:358
  4.1 14.0 %collective-permute-start.3 = (f32[2,3,112,128]{3,2,1,0:T(8,128)S(1)}, f32[2,3,112,128]{3,2,1,0:T(8,128)S(1)}, u32[]{:S(2)}, u32[]{:S(2)}) collective-permute-start(f32[2,3,112,128]{3,2,1,0:T(8,128)S(1)} %get-tuple-element.29), channel_id=1, source_target_pairs={{4,0},{8,4},{12,8},{5,1},{9,5},{13,9},{6,2},{10,6},{14,10},{7,3},{... | collective-permute-start | bytes 1032200 | tf_op jit(solution)/shard_map/ppermute | solution.py:363
  5.4 13.1 %collective-permute-start.2 = (f32[2,3,112,128]{3,2,1,0:T(8,128)S(1)}, f32[2,3,112,128]{3,2,1,0:T(8,128)S(1)}, u32[]{:S(2)}, u32[]{:S(2)}) collective-permute-start(f32[2,3,112,128]{3,2,1,0:T(8,128)S(1)} %get-tuple-element.30), channel_id=1, source_target_pairs={{0,4},{4,8},{8,12},{1,5},{5,9},{9,13},{2,6},{6,10},{10,14},{3,7},{... | collective-permute-start | bytes 1032200 | tf_op jit(solution)/shard_map/ppermute | solution.py:363
  12.3 3.9 %collective-permute-start.4 = (s32[8,128]{1,0:T(8,128)S(1)}, s32[8,128]{1,0:T(8,128)S(1)}, u32[]{:S(2)}, u32[]{:S(2)}) collective-permute-start(s32[8,128]{1,0:T(8,128)S(1)} %broadcast_in_dim.3.base), channel_id=1, source_target_pairs={{0,16},{16,0},{1,17},{17,1},{2,18},{18,2},{3,19},{19,3},{4,20},{20... | collective-permute-start | bytes 12296 | tf_op jit(solution)/shard_map/ppermute | solution.py:358
  27.3 2.5 %collective-permute-start.5 = (f32[4,9,3,16,128]{4,3,2,1,0:T(8,128)S(1)}, f32[4,9,3,16,128]{4,3,2,1,0:T(8,128)S(1)}, u32[]{:S(2)}, u32[]{:S(2)}) collective-permute-start(f32[4,9,3,16,128]{4,3,2,1,0:T(8,128)S(1)} %get-tuple-element.19), channel_id=1, source_target_pairs={{0,1},{1,0},{2,3},{3,2},{4,5},{5,4},{6,7},{7,6},{8,9},{9,8},{10,11... | collective-permute-start | bytes 2654216 | tf_op jit(solution)/shard_map/ppermute | solution.py:358
  29.9 14.1 %copy-start = (f32[72,72]{1,0:T(8,128)S(1)}, f32[72,72]{1,0:T(8,128)}, u32[]{:S(2)}) copy-start(f32[72,72]{1,0:T(8,128)} %weights.3) | copy-start | bytes 62212
  29.9 14.0 %collective-permute-start.6 = (f32[2,9,3,16,128]{4,3,2,1,0:T(8,128)S(1)}, f32[2,9,3,16,128]{4,3,2,1,0:T(8,128)S(1)}, u32[]{:S(2)}, u32[]{:S(2)}) collective-permute-start(f32[2,9,3,16,128]{4,3,2,1,0:T(8,128)S(1)} %pad_maximum_fusion.1), channel_id=1, source_target_pairs={{0,18},{2,16},{16,2},{18,0},{1,19},{3,17},{17,3},{19,1},{4,22},{6,... | collective-permute-start | bytes 1327112 | tf_op jit(solution)/shard_map/ppermute | solution.py:358
  32.7 20.2 %collective-permute-start.7 = (f32[2,9,3,16,128]{4,3,2,1,0:T(8,128)S(1)}, f32[2,9,3,16,128]{4,3,2,1,0:T(8,128)S(1)}, u32[]{:S(2)}, u32[]{:S(2)}) collective-permute-start(f32[2,9,3,16,128]{4,3,2,1,0:T(8,128)S(1)} %pad_maximum_fusion.2), channel_id=1, source_target_pairs={{0,2},{2,0},{1,3},{3,1},{4,6},{6,4},{5,7},{7,5},{8,10},{10,8},{9,1... | collective-permute-start | bytes 1327112 | tf_op jit(solution)/shard_map/ppermute | solution.py:358
  33.3 19.6 %collective-permute-start.8 = (f32[2,9,3,16,128]{4,3,2,1,0:T(8,128)S(1)}, f32[2,9,3,16,128]{4,3,2,1,0:T(8,128)S(1)}, u32[]{:S(2)}, u32[]{:S(2)}) collective-permute-start(f32[2,9,3,16,128]{4,3,2,1,0:T(8,128)S(1)} %pad_maximum_fusion.3), channel_id=1, source_target_pairs={{0,16},{16,0},{1,17},{17,1},{2,18},{18,2},{3,19},{19,3},{4,20},{20... | collective-permute-start | bytes 1327112 | tf_op jit(solution)/shard_map/ppermute | solution.py:358

commit v8 on v7

--- a/solution.py
+++ b/solution.py
@@ -155,7 +155,8 @@
 
 
 def diffuse_kernel(halo, halves, start_block, mine, theirs, top, bottom, other_source, own_source, *refs):
-    *kept, sent, rows, cond, gain, push, inv, u0, u1, res = refs
+    kept, sent = refs[:4], refs[4:8]
+    rows, cond, gain, push, inv, u0, u1, res = refs[8:]
     sources = (other_source, own_source)
     tiles, pitch = own_source.shape[1:3]
     pairs, height = mine.shape[1], mine.shape[2]
@@ -225,7 +226,7 @@
                     b = pltpu.roll(res[i * some + g, v + pairs, pl.ds(halo, height), :], HALF, 1)
                     keep, send = jnp.where(left, a, b), jnp.where(left, b, a)
                     for value, close, away in (
-                        (keep, kept[2 * i], kept[2 * i + 1]), (send, sent.at[2 * i], sent.at[2 * i + 1]),
+                        (keep, kept[2 * i], kept[2 * i + 1]), (send, sent[2 * i], sent[2 * i + 1]),
                     ):
                         upper, lower = value[:final], value[final:]
                         close[l, v] = jnp.where(first, upper, lower)
@@ -242,9 +243,9 @@
     result = jax.ShapeDtypeStruct((len(blocks) * some, pairs, height // 2, LANES), jnp.float32)
     return pl.pallas_call(
         functools.partial(diffuse_kernel, halo, halves, blocks[0]),
-        out_shape=(result,) * 4 + (jax.ShapeDtypeStruct((4, *result.shape), jnp.float32),),
+        out_shape=(result,) * 8,
         in_specs=[whole()] * len(operands),
-        out_specs=(whole(),) * 5,
+        out_specs=(whole(),) * 8,
         scratch_shapes=[line, tile, tile, both, tile, both, both, line],
         compiler_params=budget(18),
     )(*operands)
@@ -252,7 +253,7 @@
 
 def unpack(pieces, matrix, out):
     start = 0
-    for piece in (p.at[i] for p in pieces for i in range(2)):
+    for piece in pieces:
         levels, tiles, height, _ = piece.shape
         values = jnp.concatenate(
             [piece[:, t].reshape(levels * height, LANES) for t in range(tiles)], axis=1
@@ -269,13 +270,12 @@
     column = lax.broadcasted_iota(jnp.int32, (total, width), 1)
     level, offset = jnp.full((total, width), -1, jnp.int32), 0
     share = total // 8
-    for across, swapped, start, size in places:
-        for c in (core, 1 - core):
-            g = 1 - group if across else group
-            m = 1 - member if swapped else member
-            first = (g * 4 + m * 2 + c) * share + start - offset
-            level = jnp.where((column >= offset) & (column < offset + size), column + first, level)
-            offset += size
+    for across, swapped, other in places:
+        g = 1 - group if across else group
+        m = 1 - member if swapped else member
+        first = (g * 4 + m * 2 + (1 - core if other else core)) * share - offset
+        level = jnp.where((column >= offset) & (column < offset + share), column + first, level)
+        offset += share
     select = jnp.where(lax.broadcasted_iota(jnp.int32, (total, width), 0) == level, 1.0, 0.0).astype(jnp.bfloat16)
     high, low = (
         jnp.dot(v, select, preferred_element_type=jnp.float32).astype(jnp.bfloat16) for v in split(balance[...])
@@ -330,8 +330,8 @@
 
 
 def balanced(weights, places, pieces, early=None):
-    total, count = weights.shape[0], sum(2 * p.shape[1] for p in pieces)
-    tiles, height = pieces[0].shape[2:4]
+    total, count = weights.shape[0], sum(p.shape[0] for p in pieces)
+    tiles, height = pieces[0].shape[1:3]
     flat = (total * tiles * height, LANES)
     columns = VMEM((count, tiles, height, LANES), jnp.float32)
     if early is None:
@@ -413,26 +413,20 @@
     operands = (mine, theirs, top, bottom, other_source, own_source)
 
     if groups != 2:
-        *kept, sent = diffuse(halo, False, blocks, *operands)
-        return gathered(kept, crossed(sent, "lon"), balance, levels)
-    cut = max(1, len(blocks) * 3 // 3)
-    parts, start = {}, 0
-    for i, some_blocks in enumerate(filter(len, (blocks[:cut], blocks[cut:]))):
-        *kept, sent = diffuse(halo, True, some_blocks, *operands)
-        came = crossed(sent, "lon")
-        other_near, other_far, near, far = (jnp.stack([a, b]) for a, b in zip(kept, came))
-        size = near.shape[1]
-        parts["near", i] = near, (False, False, start, size)
-        parts["diagonal", i] = crossed(other_far, "member", "lev"), (True, True, start, size)
-        parts["x", i] = crossed(far, "lev"), (True, False, start, size)
-        parts["y", i] = crossed(other_near, "member"), (False, True, start, size)
-        start += size
-    late = [parts[name, max(i for _, i in parts)] for name in ("x", "y")]
-    soon = [p for p in parts.values() if all(p is not q for q in late)]
-    pieces, places = zip(*soon)
-    early = balanced(balance, places, pieces)
-    pieces, places = zip(*late)
-    return balanced(balance, places, pieces, early)
+        outs = diffuse(halo, False, blocks, *operands)
+        return gathered(outs[:4], crossed(jnp.stack(outs[4:]), "lon"), balance, levels)
+    outs = diffuse(halo, True, blocks, *operands)
+    other_near, other_far, near, far, other_near_send, other_far_send, near_send, far_send = outs
+    diagonal = [crossed(other_far, "member", "lev"), crossed(other_far_send, "member", "lev", "lon")]
+    along_x = [crossed(far, "lev"), crossed(far_send, "lev", "lon")]
+    along_y = [crossed(other_near, "member"), crossed(other_near_send, "member", "lon")]
+    here = [near, crossed(near_send, "lon")]
+
+    def places(across, swapped):
+        return [(across, swapped, other) for other in (False, True)]
+
+    early = balanced(balance, places(False, False) + places(True, True), (*here, *diagonal))
+    return balanced(balance, places(True, False) + places(False, True), (*along_x, *along_y), early)
 
 
 def solution(mesh):

time: 56.3 us -> 53.7 us (0.954)
  waiting for transfers between devices: 21.2 us -> 16 us
  starting transfers between devices: 13.2 us -> 16 us
    ppermute x7 -> x10, waiting for transfers between devices: 20.8 us -> 15.6 us  [crossed(): return lax.ppermute(block, axes, [(i, count - 1 - i) for i in range(count)])]
    ppermute x7 -> x10, starting transfers between devices: 6.37 us -> 9.22 us  [crossed(): return lax.ppermute(block, axes, [(i, count - 1 - i) for i in range(count)])]
  transfers between devices with their start and end apart: 9 -> 12, of which waited for: 5 -> 7; matrix products, arithmetic and copies ran while one was open for 0% -> 0% of each run, Pallas kernels for 10% -> 11%
where the time goes in v8:
time: 53.7 us; the launch traced here: 53.5 us
  Pallas kernels  18.5 us (34%)
  starting transfers between devices  16 us (30%)
  waiting for transfers between devices  16 us (30%)
  other arithmetic  1.58 us (3%)
  between operations  1.41 us (3%)
    ppermute x10, waiting for transfers between devices, crossed(): return lax.ppermute(block, axes, [(i, count - 1 - i) for i in range(count)])  15.6 us
    ppermute x10, starting transfers between devices, crossed(): return lax.ppermute(block, axes, [(i, count - 1 - i) for i in range(count)])  9.22 us
    pallas_call x1, Pallas kernels, diffuse(): pl.pallas_call(functools.partial(diffuse_kernel, halo, halves, blocks[0])...  8.79 us
    ppermute x2, starting transfers between devices, shifted(): lax.ppermute(block, 'lat', [(i, i + step) for i in range(strips) if 0 <=...  6.79 us
    pallas_call x2, Pallas kernels, noise(): pl.pallas_call(functools.partial(noise_kernel, levels_here, halo, total_r...  3.83 us
    pallas_call x1, Pallas kernels, balanced(): pl.pallas_call(functools.partial(late_kernel, places), out_shape=jax.Shap...  3.22 us
    pallas_call x1, Pallas kernels, balanced(): pl.pallas_call(functools.partial(early_kernel, places), out_shape=jax.Sha...  1.95 us
    mul x1, other arithmetic, per_device(): part(diffusivity, member * 2 + c, share, 0)  1.54 us
  transfers between devices with their start and end apart: 12, of which 7 were waited for; matrix products, arithmetic and copies ran while one was open for 0% of the time, Pallas kernels for 11%

profile of v8, /device:TPU:0, one launch (start us, length us, event | category | flops | bytes accessed | tf_op | source)
XLA Modules:
  0.0 53.5 jit_solution(10805754999523441271)
XLA Ops:
  0.0 1.5 %convert_multiply_fusion = (f32[9,32,384]{2,1,0:T(8,128)S(1)}, f32[9,32,384]{2,1,0:T(8,128)S(1)}) fusion(s32[36,32,384]{2,1,0:T(8,128)} %param.5, s32[]{:T(128)S(6)} %select_n.9, f32[36,32,384]{2,1,0:T(8,128)} %param.6, s32[]{:T(128)S(6)} %select_n.8), kind=kLoop, calls=%fused_computation.2 | loop fusion | flops 442368 | bytes 2654216 | tf_op jit(solution)/shard_map/mul | solution.py:399
  1.5 0.7 %shard_map.55 = (f32[9,3,32,128]{3,2,1,0:T(8,128)S(1)}, f32[9,3,32,128]{3,2,1,0:T(8,128)S(1)}, f32[2,3,112,128]{3,2,1,0:T(8,128)S(1)}, f32[2,3,112,128]{3,2,1,0:T(8,128)S(1)}) custom-call(f32[9,32,384]{2,1,0:T(8,128)S(1)} %get-tuple-element.30.kept, f32[9,32,384]{2,1,0:T(8,128)S(1)} %get-tuple-element.29.other), custom_call_target="tpu_custom_call" | custom-call | tf_op jit(solution)/shard_map/pallas_call | solution.py:94
  2.3 0.5 collective-permute-start.1
  2.8 0.1 collective-permute-start
  2.9 1.2 %collective-permute-done.1 = f32[2,3,112,128]{3,2,1,0:T(8,128)S(1)} collective-permute-done((f32[2,3,112,128]{3,2,1,0:T(8,128)S(1)}, f32[2,3,112,128]{3,2,1,0:T(8,128)S(1)}, u32[]{:S(2)}, u32[]{:S(2)}) %collective-permute-start.1) | collective-permute-done | bytes 344096 | tf_op jit(solution)/shard_map/ppermute | solution.py:358
  4.1 1.3 %collective-permute-start.3 = (f32[2,3,112,128]{3,2,1,0:T(8,128)S(1)}, f32[2,3,112,128]{3,2,1,0:T(8,128)S(1)}, u32[]{:S(2)}, u32[]{:S(2)}) collective-permute-start(f32[2,3,112,128]{3,2,1,0:T(8,128)S(1)} %get-tuple-element.31), channel_id=1, source_target_pairs={{4,0},{8,4},{12,8},{5,1},{9,5},{13,9},{6,2},{10,6},{14,10},{7,3},{... | collective-permute-start | bytes 1032200 | tf_op jit(solution)/shard_map/ppermute | solution.py:363
  5.4 5.5 %collective-permute-start.2 = (f32[2,3,112,128]{3,2,1,0:T(8,128)S(1)}, f32[2,3,112,128]{3,2,1,0:T(8,128)S(1)}, u32[]{:S(2)}, u32[]{:S(2)}) collective-permute-start(f32[2,3,112,128]{3,2,1,0:T(8,128)S(1)} %get-tuple-element.32), channel_id=1, source_target_pairs={{0,4},{4,8},{8,12},{1,5},{5,9},{9,13},{2,6},{6,10},{10,14},{3,7},{... | collective-permute-start | bytes 1032200 | tf_op jit(solution)/shard_map/ppermute | solution.py:363
  12.3 2.0 %collective-permute-start.4 = (s32[8,128]{1,0:T(8,128)S(1)}, s32[8,128]{1,0:T(8,128)S(1)}, u32[]{:S(2)}, u32[]{:S(2)}) collective-permute-start(s32[8,128]{1,0:T(8,128)S(1)} %broadcast_in_dim.3.base), channel_id=1, source_target_pairs={{0,16},{16,0},{1,17},{17,1},{2,18},{18,2},{3,19},{19,3},{4,20},{20... | collective-permute-start | bytes 12296 | tf_op jit(solution)/shard_map/ppermute | solution.py:358
  14.3 1.9 %shard_map.57.own_source = f32[9,6,7,8,128]{4,3,2,1,0:T(8,128)S(1)} custom-call(s32[8,128]{1,0:T(8,128)S(1)} %broadcast_in_dim.3.base), custom_call_target="tpu_custom_call" | custom-call | tf_op jit(solution)/shard_map/pallas_call | solution.py:123
  16.2 1.9 %shard_map.56.other_source = f32[9,6,7,8,128]{4,3,2,1,0:T(8,128)S(1)} custom-call(s32[8,128]{1,0:T(8,128)S(1)} %collective-permute-done.4.base), custom_call_target="tpu_custom_call" | custom-call | tf_op jit(solution)/shard_map/pallas_call | solution.py:123
  18.1 0.4 collective-permute-done.2.top
  18.5 8.8 %shard_map.58 = (f32[9,3,16,128]{3,2,1,0:T(8,128)S(1)}, f32[9,3,16,128]{3,2,1,0:T(8,128)S(1)}, f32[9,3,16,128]{3,2,1,0:T(8,128)S(1)}, f32[9,3,16,128]{3,2,1,0:T(...) custom-call(f32[9,3,32,128]{3,2,1,0:T(8,128)S(1)} %get-tuple-element, ...), custom_call_target="tpu_custom_call" | custom-call | tf_op jit(solution)/shard_map/pallas_call | solution.py:244
  27.4 2.7 %collective-permute-start.6 = (f32[9,3,16,128]{3,2,1,0:T(8,128)S(1)}, f32[9,3,16,128]{3,2,1,0:T(8,128)S(1)}, u32[]{:S(2)}, u32[]{:S(2)}) collective-permute-start(f32[9,3,16,128]{3,2,1,0:T(8,128)S(1)} %get-tuple-element.23), channel_id=1, source_target_pairs={{0,18},{2,16},{16,2},{18,0},{1,19},{3,17},{17,3},{19,1},{4,22},{6,... | collective-permute-start | bytes 663560 | tf_op jit(solution)/shard_map/ppermute | solution.py:358
  30.1 0.1 collective-permute-start.7
  30.2 1.6 %collective-permute-start.8 = (f32[9,3,16,128]{3,2,1,0:T(8,128)S(1)}, f32[9,3,16,128]{3,2,1,0:T(8,128)S(1)}, u32[]{:S(2)}, u32[]{:S(2)}) collective-permute-start(f32[9,3,16,128]{3,2,1,0:T(8,128)S(1)} %get-tuple-element.25), channel_id=1, source_target_pairs={{0,2},{2,0},{1,3},{3,1},{4,6},{6,4},{5,7},{7,5},{8,10},{10,8},{9,1... | collective-permute-start | bytes 663560 | tf_op jit(solution)/shard_map/ppermute | solution.py:358
  31.9 1.7 %collective-permute-start.10 = (f32[9,3,16,128]{3,2,1,0:T(8,128)S(1)}, f32[9,3,16,128]{3,2,1,0:T(8,128)S(1)}, u32[]{:S(2)}, u32[]{:S(2)}) collective-permute-start(f32[9,3,16,128]{3,2,1,0:T(8,128)S(1)} %get-tuple-element.27), channel_id=1, source_target_pairs={{0,16},{16,0},{1,17},{17,1},{2,18},{18,2},{3,19},{19,3},{4,20},{20... | collective-permute-start | bytes 663560 | tf_op jit(solution)/shard_map/ppermute | solution.py:358
  33.5 3.2 %collective-permute-done.6.refs_2_ = f32[9,3,16,128]{3,2,1,0:T(8,128)S(1)} collective-permute-done((f32[9,3,16,128]{3,2,1,0:T(8,128)S(1)}, f32[9,3,16,128]{3,2,1,0:T(8,128)S(1)}, u32[]{:S(2)}, u32[]{:S(2)}) %collective-permute-start.6) | collective-permute-done | bytes 221216 | tf_op jit(solution)/shard_map/ppermute | solution.py:358
  36.7 0.4 collective-permute-start.11
  37.1 3.5 %collective-permute-done.7.refs_3_ = f32[9,3,16,128]{3,2,1,0:T(8,128)S(1)} collective-permute-done((f32[9,3,16,128]{3,2,1,0:T(8,128)S(1)}, f32[9,3,16,128]{3,2,1,0:T(8,128)S(1)}, u32[]{:S(2)}, u32[]{:S(2)}) %collective-permute-start.7) | collective-permute-done | bytes 221216 | tf_op jit(solution)/shard_map/ppermute | solution.py:358
  40.6 2.0 %shard_map.59.early = f32[3456,128]{1,0:T(8,128)S(1)} custom-call(f32[72,72]{1,0:T(8,128)S(1)} %copy-done, f32[9,3,16,128]{3,2,1,0:T(8,128)S(1)} %get-tuple-element.21.refs_0_, f32[9,3,16,128]{3,2,1,0:T(8,128)S(1)} %collective-permute-done.5.refs_1_, f32[9,3,16,128]{3,2,1,0:T(8,128)S(1)} %collective-permute-done.6.refs_2_, ...), custom_call_target="tpu_custom_call" | custom-call | tf_op jit(solution)/shard_map/pallas_call | solution.py:338
  42.6 3.8 %collective-permute-done.8.refs_0_ = f32[9,3,16,128]{3,2,1,0:T(8,128)S(1)} collective-permute-done((f32[9,3,16,128]{3,2,1,0:T(8,128)S(1)}, f32[9,3,16,128]{3,2,1,0:T(8,128)S(1)}, u32[]{:S(2)}, u32[]{:S(2)}) %collective-permute-start.8) | collective-permute-done | bytes 221216 | tf_op jit(solution)/shard_map/ppermute | solution.py:358
  46.3 3.8 %collective-permute-done.9.refs_1_ = f32[9,3,16,128]{3,2,1,0:T(8,128)S(1)} collective-permute-done((f32[9,3,16,128]{3,2,1,0:T(8,128)S(1)}, f32[9,3,16,128]{3,2,1,0:T(8,128)S(1)}, u32[]{:S(2)}, u32[]{:S(2)}) %collective-permute-start.9) | collective-permute-done | bytes 221216 | tf_op jit(solution)/shard_map/ppermute | solution.py:358
  50.2 0.1 collective-permute-done.11.refs_3_
  50.3 3.2 %shard_map.60 = f32[72,16,384]{2,1,0:T(8,128)} custom-call(f32[72,72]{1,0:T(8,128)S(1)} %copy-done, f32[3456,128]{1,0:T(8,128)S(1)} %shard_map.59.early, f32[9,3,16,128]{3,2,1,0:T(8,128)S(1)} %collective-permute-done.8.refs_0_, f32[9,3,16,128]{3,2,1,0:T(8,128)S(1)} %collective-permute-done.9.refs_1_, f32[9,3,16,128]{3,2,1,0:T(8,128)S(1)} %collective-permute-done.10.refs_2_, ...), custom_call_target="tpu_custom_call" | custom-call | tf_op jit(solution)/shard_map/pallas_call | solution.py:346
  (11 shorter events, 0.2 us)
Async XLA Ops:
  2.3 1.8 %collective-permute-start.1 = (f32[2,3,112,128]{3,2,1,0:T(8,128)S(1)}, f32[2,3,112,128]{3,2,1,0:T(8,128)S(1)}, u32[]{:S(2)}, u32[]{:S(2)}) collective-permute-start(f32[2,3,112,128]{3,2,1,0:T(8,128)S(1)} %get-tuple-element.20), channel_id=1, source_target_pairs={{0,1},{1,0},{2,3},{3,2},{4,5},{5,4},{6,7},{7,6},{8,9},{9,8},{10,11... | collective-permute-start | bytes 1032200 | tf_op jit(solution)/shard_map/ppermute | solution.py:358
  2.8 15.3 %collective-permute-start = (f32[9,3,32,128]{3,2,1,0:T(8,128)S(1)}, f32[9,3,32,128]{3,2,1,0:T(8,128)S(1)}, u32[]{:S(2)}, u32[]{:S(2)}) collective-permute-start(f32[9,3,32,128]{3,2,1,0:T(8,128)S(1)} %get-tuple-element.18), channel_id=1, source_target_pairs={{0,1},{1,0},{2,3},{3,2},{4,5},{5,4},{6,7},{7,6},{8,9},{9,8},{10,11... | collective-permute-start | bytes 1327112 | tf_op jit(solution)/shard_map/ppermute | solution.py:358
  4.1 14.0 %collective-permute-start.3 = (f32[2,3,112,128]{3,2,1,0:T(8,128)S(1)}, f32[2,3,112,128]{3,2,1,0:T(8,128)S(1)}, u32[]{:S(2)}, u32[]{:S(2)}) collective-permute-start(f32[2,3,112,128]{3,2,1,0:T(8,128)S(1)} %get-tuple-element.31), channel_id=1, source_target_pairs={{4,0},{8,4},{12,8},{5,1},{9,5},{13,9},{6,2},{10,6},{14,10},{7,3},{... | collective-permute-start | bytes 1032200 | tf_op jit(solution)/shard_map/ppermute | solution.py:363
  5.4 13.1 %collective-permute-start.2 = (f32[2,3,112,128]{3,2,1,0:T(8,128)S(1)}, f32[2,3,112,128]{3,2,1,0:T(8,128)S(1)}, u32[]{:S(2)}, u32[]{:S(2)}) collective-permute-start(f32[2,3,112,128]{3,2,1,0:T(8,128)S(1)} %get-tuple-element.32), channel_id=1, source_target_pairs={{0,4},{4,8},{8,12},{1,5},{5,9},{9,13},{2,6},{6,10},{10,14},{3,7},{... | collective-permute-start | bytes 1032200 | tf_op jit(solution)/shard_map/ppermute | solution.py:363
  12.3 3.9 %collective-permute-start.4 = (s32[8,128]{1,0:T(8,128)S(1)}, s32[8,128]{1,0:T(8,128)S(1)}, u32[]{:S(2)}, u32[]{:S(2)}) collective-permute-start(s32[8,128]{1,0:T(8,128)S(1)} %broadcast_in_dim.3.base), channel_id=1, source_target_pairs={{0,16},{16,0},{1,17},{17,1},{2,18},{18,2},{3,19},{19,3},{4,20},{20... | collective-permute-start | bytes 12296 | tf_op jit(solution)/shard_map/ppermute | solution.py:358
  18.5 22.1 %copy-start = (f32[72,72]{1,0:T(8,128)S(1)}, f32[72,72]{1,0:T(8,128)}, u32[]{:S(2)}) copy-start(f32[72,72]{1,0:T(8,128)} %weights.3) | copy-start | bytes 62212
  27.3 4.5 %collective-permute-start.5 = (f32[9,3,16,128]{3,2,1,0:T(8,128)S(1)}, f32[9,3,16,128]{3,2,1,0:T(8,128)S(1)}, u32[]{:S(2)}, u32[]{:S(2)}) collective-permute-start(f32[9,3,16,128]{3,2,1,0:T(8,128)S(1)} %get-tuple-element.22), channel_id=1, source_target_pairs={{0,1},{1,0},{2,3},{3,2},{4,5},{5,4},{6,7},{7,6},{8,9},{9,8},{10,11... | collective-permute-start | bytes 663560 | tf_op jit(solution)/shard_map/ppermute | solution.py:358
  27.4 9.3 %collective-permute-start.6 = (f32[9,3,16,128]{3,2,1,0:T(8,128)S(1)}, f32[9,3,16,128]{3,2,1,0:T(8,128)S(1)}, u32[]{:S(2)}, u32[]{:S(2)}) collective-permute-start(f32[9,3,16,128]{3,2,1,0:T(8,128)S(1)} %get-tuple-element.23), channel_id=1, source_target_pairs={{0,18},{2,16},{16,2},{18,0},{1,19},{3,17},{17,3},{19,1},{4,22},{6,... | collective-permute-start | bytes 663560 | tf_op jit(solution)/shard_map/ppermute | solution.py:358
  30.1 10.5 %collective-permute-start.7 = (f32[9,3,16,128]{3,2,1,0:T(8,128)S(1)}, f32[9,3,16,128]{3,2,1,0:T(8,128)S(1)}, u32[]{:S(2)}, u32[]{:S(2)}) collective-permute-start(f32[9,3,16,128]{3,2,1,0:T(8,128)S(1)} %get-tuple-element.24), channel_id=1, source_target_pairs={{0,19},{1,18},{2,17},{3,16},{16,3},{17,2},{18,1},{19,0},{4,23},{5,... | collective-permute-start | bytes 663560 | tf_op jit(solution)/shard_map/ppermute | solution.py:358
  30.2 16.2 %collective-permute-start.8 = (f32[9,3,16,128]{3,2,1,0:T(8,128)S(1)}, f32[9,3,16,128]{3,2,1,0:T(8,128)S(1)}, u32[]{:S(2)}, u32[]{:S(2)}) collective-permute-start(f32[9,3,16,128]{3,2,1,0:T(8,128)S(1)} %get-tuple-element.25), channel_id=1, source_target_pairs={{0,2},{2,0},{1,3},{3,1},{4,6},{6,4},{5,7},{7,5},{8,10},{10,8},{9,1... | collective-permute-start | bytes 663560 | tf_op jit(solution)/shard_map/ppermute | solution.py:358
  31.8 18.4 %collective-permute-start.9 = (f32[9,3,16,128]{3,2,1,0:T(8,128)S(1)}, f32[9,3,16,128]{3,2,1,0:T(8,128)S(1)}, u32[]{:S(2)}, u32[]{:S(2)}) collective-permute-start(f32[9,3,16,128]{3,2,1,0:T(8,128)S(1)} %get-tuple-element.26), channel_id=1, source_target_pairs={{0,3},{1,2},{2,1},{3,0},{4,7},{5,6},{6,5},{7,4},{8,11},{9,10},{10,... | collective-permute-start | bytes 663560 | tf_op jit(solution)/shard_map/ppermute | solution.py:358
  31.9 18.3 %collective-permute-start.10 = (f32[9,3,16,128]{3,2,1,0:T(8,128)S(1)}, f32[9,3,16,128]{3,2,1,0:T(8,128)S(1)}, u32[]{:S(2)}, u32[]{:S(2)}) collective-permute-start(f32[9,3,16,128]{3,2,1,0:T(8,128)S(1)} %get-tuple-element.27), channel_id=1, source_target_pairs={{0,16},{16,0},{1,17},{17,1},{2,18},{18,2},{3,19},{19,3},{4,20},{20... | collective-permute-start | bytes 663560 | tf_op jit(solution)/shard_map/ppermute | solution.py:358
  36.7 13.6 %collective-permute-start.11 = (f32[9,3,16,128]{3,2,1,0:T(8,128)S(1)}, f32[9,3,16,128]{3,2,1,0:T(8,128)S(1)}, u32[]{:S(2)}, u32[]{:S(2)}) collective-permute-start(f32[9,3,16,128]{3,2,1,0:T(8,128)S(1)} %get-tuple-element.28), channel_id=1, source_target_pairs={{0,17},{1,16},{16,1},{17,0},{2,19},{3,18},{18,3},{19,2},{4,21},{5,... | collective-permute-start | bytes 663560 | tf_op jit(solution)/shard_map/ppermute | solution.py:358

commit v9 on v8

--- a/solution.py
+++ b/solution.py
@@ -239,7 +239,7 @@
     some = math.gcd(levels, SOME)
     tile = VMEM((some, tiles, pitch, SUB, LANES), jnp.float32)
     both = VMEM((2 * some, tiles, pitch, SUB, LANES), jnp.float32)
-    line = VMEM((2 * some, tiles, pitch * SUB, LANES), jnp.float32)
+    line = VMEM((2 * some, tiles, (pitch + 1) * SUB, LANES), jnp.float32)
     result = jax.ShapeDtypeStruct((len(blocks) * some, pairs, height // 2, LANES), jnp.float32)
     return pl.pallas_call(
         functools.partial(diffuse_kernel, halo, halves, blocks[0]),
@@ -285,10 +285,10 @@
 
 def weighted(balance, places, pieces, columns, emit):
     total = balance.shape[0]
-    count, tiles, height, _ = columns.shape
-    pitch = tiles * height
+    tiles, height = columns.shape[1:3]
+    count, pitch = sum(p.shape[0] for p in pieces), tiles * height
     unpack(pieces, packing(tiles * LANES, 2 * tiles, lax.axis_index("lon"), 0), columns)
-    flat = columns.reshape(count * pitch, LANES)
+    flat = columns.reshape(columns.shape[0] * pitch, LANES)
     stacked = chosen(balance, places, count)
     for t in range(tiles):
         for r in range(height):
@@ -298,28 +298,30 @@
             emit(t, r, pl.ds(t * height + r, total, stride=pitch), value)
 
 
-def early_kernel(places, weights, *refs):
+def share_kernel(places, weights, *refs):
     *pieces, out, columns = refs
+    earlier = pieces.pop(0) if len(pieces) > len(places) else None
 
     def store(t, r, rows, value):
-        out[rows, :] = value
+        out[rows, :] = value if earlier is None else earlier[rows, :] + value
 
     weighted(weights, places, pieces, columns, store)
 
 
-def late_kernel(places, weights, early, *refs):
+def last_kernel(places, weights, earlier, *refs):
     *pieces, out, columns, result, sent = refs
     total = weights.shape[0]
     tiles, height = columns.shape[1:3]
     copies = []
 
     def store(t, r, rows, value):
-        result[rows, :] = early[rows, :] + value
-        if r == height - 1:
+        result[rows, :] = earlier[rows, :] + value
+        if r % SUB == SUB - 1:
+            some = pl.ds(r - SUB + 1, SUB)
             copy = pltpu.make_async_copy(
-                result.reshape(total, tiles, height, LANES).at[:, t],
-                out.at[:, :, pl.ds(t * LANES, LANES)],
-                sent.at[t],
+                result.reshape(total, tiles, height, LANES).at[:, t, some],
+                out.at[:, some, pl.ds(t * LANES, LANES)],
+                sent.at[t, r // SUB],
             )
             copy.start()
             copies.append(copy)
@@ -329,28 +331,29 @@
         copy.wait()
 
 
-def balanced(weights, places, pieces, early=None):
+def balanced(weights, places, pieces, earlier=None, last=False):
     total, count = weights.shape[0], sum(p.shape[0] for p in pieces)
     tiles, height = pieces[0].shape[1:3]
     flat = (total * tiles * height, LANES)
-    columns = VMEM((count, tiles, height, LANES), jnp.float32)
-    if early is None:
+    columns = VMEM((-(-count // SUB) * SUB, tiles, height, LANES), jnp.float32)
+    operands = (weights, *(() if earlier is None else (earlier,)), *pieces)
+    if not last:
         return pl.pallas_call(
-            functools.partial(early_kernel, places),
+            functools.partial(share_kernel, places),
             out_shape=jax.ShapeDtypeStruct(flat, jnp.float32),
-            in_specs=[whole()] * (1 + len(pieces)),
+            in_specs=[whole()] * len(operands),
             out_specs=whole(),
             scratch_shapes=[columns],
             compiler_params=budget(10),
-        )(weights, *pieces)
+        )(*operands)
     return pl.pallas_call(
-        functools.partial(late_kernel, places),
+        functools.partial(last_kernel, places),
         out_shape=jax.ShapeDtypeStruct((total, height, tiles * LANES), jnp.float32),
-        in_specs=[whole()] * (2 + len(pieces)),
+        in_specs=[whole()] * len(operands),
         out_specs=pl.BlockSpec(memory_space=pl.ANY),
-        scratch_shapes=[columns, VMEM(flat, jnp.float32), pltpu.SemaphoreType.DMA((tiles,))],
+        scratch_shapes=[columns, VMEM(flat, jnp.float32), pltpu.SemaphoreType.DMA((tiles, height // SUB))],
         compiler_params=budget(10),
-    )(weights, early, *pieces)
+    )(*operands)
 
 
 def crossed(block, *axes):
@@ -425,8 +428,10 @@
     def places(across, swapped):
         return [(across, swapped, other) for other in (False, True)]
 
-    early = balanced(balance, places(False, False) + places(True, True), (*here, *diagonal))
-    return balanced(balance, places(True, False) + places(False, True), (*along_x, *along_y), early)
+    share_of = balanced(balance, places(False, False) + places(True, True), (*here, *diagonal))
+    x, y = places(True, False), places(False, True)
+    share_of = balanced(balance, [x[0], y[0]], (along_x[0], along_y[0]), share_of)
+    return balanced(balance, [x[1], y[1]], (along_x[1], along_y[1]), share_of, True)
 
 
 def solution(mesh):

time: 53.7 us -> 53.2 us (level)
  waiting for transfers between devices: 16 us -> 14.2 us
  Pallas kernels: 18.5 us -> 20 us
    ppermute x10, waiting for transfers between devices: 15.6 us -> 13.8 us  [crossed(): return lax.ppermute(block, axes, [(i, count - 1 - i) for i in range(count)])]
    pallas_call x2 -> x3, Pallas kernels: 5.17 us -> 6.74 us  [the longest x2 3.96 us: balanced(): pl.pallas_call(functools.partial(share_kernel, places), out_shape=jax.Sha...]
  transfers between devices with their start and end apart: 12 -> 12, of which waited for: 7 -> 7; matrix products, arithmetic and copies ran while one was open for 0% -> 0% of each run, Pallas kernels for 11% -> 15%
where the time goes in v9:
time: 53.2 us; the launch traced here: 53 us
  Pallas kernels  20 us (38%)
  starting transfers between devices  15.8 us (30%)
  waiting for transfers between devices  14.2 us (27%)
  other arithmetic  1.58 us (3%)
  between operations  1.42 us (3%)
    ppermute x10, waiting for transfers between devices, crossed(): return lax.ppermute(block, axes, [(i, count - 1 - i) for i in range(count)])  13.8 us
    ppermute x10, starting transfers between devices, crossed(): return lax.ppermute(block, axes, [(i, count - 1 - i) for i in range(count)])  9.01 us
    pallas_call x1, Pallas kernels, diffuse(): pl.pallas_call(functools.partial(diffuse_kernel, halo, halves, blocks[0])...  8.71 us
    ppermute x2, starting transfers between devices, shifted(): lax.ppermute(block, 'lat', [(i, i + step) for i in range(strips) if 0 <=...  6.79 us
    pallas_call x2, Pallas kernels, balanced(): pl.pallas_call(functools.partial(share_kernel, places), out_shape=jax.Sha...  3.96 us
    pallas_call x2, Pallas kernels, noise(): pl.pallas_call(functools.partial(noise_kernel, levels_here, halo, total_r...  3.83 us
    pallas_call x1, Pallas kernels, balanced(): pl.pallas_call(functools.partial(last_kernel, places), out_shape=jax.Shap...  2.78 us
    mul x1, other arithmetic, per_device(): part(diffusivity, member * 2 + c, share, 0)  1.54 us
  transfers between devices with their start and end apart: 12, of which 7 were waited for; matrix products, arithmetic and copies ran while one was open for 0% of the time, Pallas kernels for 15%

profile of v9, /device:TPU:0, one launch (start us, length us, event | category | flops | bytes accessed | tf_op | source)
XLA Modules:
  0.0 53.0 jit_solution(11147977457917578593)
XLA Ops:
  0.0 1.5 %convert_multiply_fusion = (f32[9,32,384]{2,1,0:T(8,128)S(1)}, f32[9,32,384]{2,1,0:T(8,128)S(1)}) fusion(s32[36,32,384]{2,1,0:T(8,128)} %param.5, s32[]{:T(128)S(6)} %select_n.9, f32[36,32,384]{2,1,0:T(8,128)} %param.6, s32[]{:T(128)S(6)} %select_n.8), kind=kLoop, calls=%fused_computation.2 | loop fusion | flops 442368 | bytes 2654216 | tf_op jit(solution)/shard_map/mul | solution.py:402
  1.5 0.7 %shard_map.55 = (f32[9,3,32,128]{3,2,1,0:T(8,128)S(1)}, f32[9,3,32,128]{3,2,1,0:T(8,128)S(1)}, f32[2,3,112,128]{3,2,1,0:T(8,128)S(1)}, f32[2,3,112,128]{3,2,1,0:T(8,128)S(1)}) custom-call(f32[9,32,384]{2,1,0:T(8,128)S(1)} %get-tuple-element.30.kept, f32[9,32,384]{2,1,0:T(8,128)S(1)} %get-tuple-element.29.other), custom_call_target="tpu_custom_call" | custom-call | tf_op jit(solution)/shard_map/pallas_call | solution.py:94
  2.3 0.5 collective-permute-start.1
  2.9 1.2 %collective-permute-done.1 = f32[2,3,112,128]{3,2,1,0:T(8,128)S(1)} collective-permute-done((f32[2,3,112,128]{3,2,1,0:T(8,128)S(1)}, f32[2,3,112,128]{3,2,1,0:T(8,128)S(1)}, u32[]{:S(2)}, u32[]{:S(2)}) %collective-permute-start.1) | collective-permute-done | bytes 344096 | tf_op jit(solution)/shard_map/ppermute | solution.py:361
  4.1 1.3 %collective-permute-start.3 = (f32[2,3,112,128]{3,2,1,0:T(8,128)S(1)}, f32[2,3,112,128]{3,2,1,0:T(8,128)S(1)}, u32[]{:S(2)}, u32[]{:S(2)}) collective-permute-start(f32[2,3,112,128]{3,2,1,0:T(8,128)S(1)} %get-tuple-element.31), channel_id=1, source_target_pairs={{4,0},{8,4},{12,8},{5,1},{9,5},{13,9},{6,2},{10,6},{14,10},{7,3},{... | collective-permute-start | bytes 1032200 | tf_op jit(solution)/shard_map/ppermute | solution.py:366
  5.4 5.5 %collective-permute-start.2 = (f32[2,3,112,128]{3,2,1,0:T(8,128)S(1)}, f32[2,3,112,128]{3,2,1,0:T(8,128)S(1)}, u32[]{:S(2)}, u32[]{:S(2)}) collective-permute-start(f32[2,3,112,128]{3,2,1,0:T(8,128)S(1)} %get-tuple-element.32), channel_id=1, source_target_pairs={{0,4},{4,8},{8,12},{1,5},{5,9},{9,13},{2,6},{6,10},{10,14},{3,7},{... | collective-permute-start | bytes 1032200 | tf_op jit(solution)/shard_map/ppermute | solution.py:366
  12.3 2.0 %collective-permute-start.4 = (s32[8,128]{1,0:T(8,128)S(1)}, s32[8,128]{1,0:T(8,128)S(1)}, u32[]{:S(2)}, u32[]{:S(2)}) collective-permute-start(s32[8,128]{1,0:T(8,128)S(1)} %broadcast_in_dim.3.base), channel_id=1, source_target_pairs={{0,16},{16,0},{1,17},{17,1},{2,18},{18,2},{3,19},{19,3},{4,20},{20... | collective-permute-start | bytes 12296 | tf_op jit(solution)/shard_map/ppermute | solution.py:361
  14.3 1.9 %shard_map.57.own_source = f32[9,6,7,8,128]{4,3,2,1,0:T(8,128)S(1)} custom-call(s32[8,128]{1,0:T(8,128)S(1)} %broadcast_in_dim.3.base), custom_call_target="tpu_custom_call" | custom-call | tf_op jit(solution)/shard_map/pallas_call | solution.py:123
  16.2 1.9 %shard_map.56.other_source = f32[9,6,7,8,128]{4,3,2,1,0:T(8,128)S(1)} custom-call(s32[8,128]{1,0:T(8,128)S(1)} %collective-permute-done.4.base), custom_call_target="tpu_custom_call" | custom-call | tf_op jit(solution)/shard_map/pallas_call | solution.py:123
  18.1 0.4 collective-permute-done.2.top
  18.5 8.7 %shard_map.58 = (f32[9,3,16,128]{3,2,1,0:T(8,128)S(1)}, f32[9,3,16,128]{3,2,1,0:T(8,128)S(1)}, f32[9,3,16,128]{3,2,1,0:T(8,128)S(1)}, f32[9,3,16,128]{3,2,1,0:T(...) custom-call(f32[9,3,32,128]{3,2,1,0:T(8,128)S(1)} %get-tuple-element, ...), custom_call_target="tpu_custom_call" | custom-call | tf_op jit(solution)/shard_map/pallas_call | solution.py:244
  27.3 2.7 %collective-permute-start.6 = (f32[9,3,16,128]{3,2,1,0:T(8,128)S(1)}, f32[9,3,16,128]{3,2,1,0:T(8,128)S(1)}, u32[]{:S(2)}, u32[]{:S(2)}) collective-permute-start(f32[9,3,16,128]{3,2,1,0:T(8,128)S(1)} %get-tuple-element.23), channel_id=1, source_target_pairs={{0,18},{2,16},{16,2},{18,0},{1,19},{3,17},{17,3},{19,1},{4,22},{6,... | collective-permute-start | bytes 663560 | tf_op jit(solution)/shard_map/ppermute | solution.py:361
  30.0 0.1 collective-permute-start.7
  30.1 1.6 %collective-permute-start.8 = (f32[9,3,16,128]{3,2,1,0:T(8,128)S(1)}, f32[9,3,16,128]{3,2,1,0:T(8,128)S(1)}, u32[]{:S(2)}, u32[]{:S(2)}) collective-permute-start(f32[9,3,16,128]{3,2,1,0:T(8,128)S(1)} %get-tuple-element.25), channel_id=1, source_target_pairs={{0,2},{2,0},{1,3},{3,1},{4,6},{6,4},{5,7},{7,5},{8,10},{10,8},{9,1... | collective-permute-start | bytes 663560 | tf_op jit(solution)/shard_map/ppermute | solution.py:361
  31.7 1.5 %collective-permute-start.9 = (f32[9,3,16,128]{3,2,1,0:T(8,128)S(1)}, f32[9,3,16,128]{3,2,1,0:T(8,128)S(1)}, u32[]{:S(2)}, u32[]{:S(2)}) collective-permute-start(f32[9,3,16,128]{3,2,1,0:T(8,128)S(1)} %get-tuple-element.26), channel_id=1, source_target_pairs={{0,16},{16,0},{1,17},{17,1},{2,18},{18,2},{3,19},{19,3},{4,20},{20... | collective-permute-start | bytes 663560 | tf_op jit(solution)/shard_map/ppermute | solution.py:361
  33.3 3.4 %collective-permute-done.6.refs_2_ = f32[9,3,16,128]{3,2,1,0:T(8,128)S(1)} collective-permute-done((f32[9,3,16,128]{3,2,1,0:T(8,128)S(1)}, f32[9,3,16,128]{3,2,1,0:T(8,128)S(1)}, u32[]{:S(2)}, u32[]{:S(2)}) %collective-permute-start.6) | collective-permute-done | bytes 221216 | tf_op jit(solution)/shard_map/ppermute | solution.py:361
  36.6 0.4 collective-permute-start.11
  37.0 3.5 %collective-permute-done.7.refs_3_ = f32[9,3,16,128]{3,2,1,0:T(8,128)S(1)} collective-permute-done((f32[9,3,16,128]{3,2,1,0:T(8,128)S(1)}, f32[9,3,16,128]{3,2,1,0:T(8,128)S(1)}, u32[]{:S(2)}, u32[]{:S(2)}) %collective-permute-start.7) | collective-permute-done | bytes 221216 | tf_op jit(solution)/shard_map/ppermute | solution.py:361
  40.5 2.0 %shard_map.59.refs_0_ = f32[3456,128]{1,0:T(8,128)S(1)} custom-call(f32[72,72]{1,0:T(8,128)S(1)} %copy-done, f32[9,3,16,128]{3,2,1,0:T(8,128)S(1)} %get-tuple-element.21.refs_0_, f32[9,3,16,128]{3,2,1,0:T(8,128)S(1)} %collective-permute-done.5.refs_1_, f32[9,3,16,128]{3,2,1,0:T(8,128)S(1)} %collective-permute-done.6.refs_2_, ...), custom_call_target="tpu_custom_call" | custom-call | tf_op jit(solution)/shard_map/pallas_call | solution.py:341
  42.5 3.8 %collective-permute-done.8.refs_1_ = f32[9,3,16,128]{3,2,1,0:T(8,128)S(1)} collective-permute-done((f32[9,3,16,128]{3,2,1,0:T(8,128)S(1)}, f32[9,3,16,128]{3,2,1,0:T(8,128)S(1)}, u32[]{:S(2)}, u32[]{:S(2)}) %collective-permute-start.8) | collective-permute-done | bytes 221216 | tf_op jit(solution)/shard_map/ppermute | solution.py:361
  46.3 2.0 %shard_map.60.earlier = f32[3456,128]{1,0:T(8,128)S(1)} custom-call(f32[72,72]{1,0:T(8,128)S(1)} %copy-done, f32[3456,128]{1,0:T(8,128)S(1)} %shard_map.59.refs_0_, f32[9,3,16,128]{3,2,1,0:T(8,128)S(1)} %collective-permute-done.8.refs_1_, f32[9,3,16,128]{3,2,1,0:T(8,128)S(1)} %collective-permute-done.9.refs_2_), custom_call_target="tpu_custom_call" | custom-call | tf_op jit(solution)/shard_map/pallas_call | solution.py:341
  48.3 1.8 %collective-permute-done.10.refs_0_ = f32[9,3,16,128]{3,2,1,0:T(8,128)S(1)} collective-permute-done((f32[9,3,16,128]{3,2,1,0:T(8,128)S(1)}, f32[9,3,16,128]{3,2,1,0:T(8,128)S(1)}, u32[]{:S(2)}, u32[]{:S(2)}) %collective-permute-start.10) | collective-permute-done | bytes 221216 | tf_op jit(solution)/shard_map/ppermute | solution.py:361
  50.1 0.1 collective-permute-done.11.refs_1_
  50.2 2.8 %shard_map.61 = f32[72,16,384]{2,1,0:T(8,128)} custom-call(f32[72,72]{1,0:T(8,128)S(1)} %copy-done, f32[3456,128]{1,0:T(8,128)S(1)} %shard_map.60.earlier, f32[9,3,16,128]{3,2,1,0:T(8,128)S(1)} %collective-permute-done.10.refs_0_, f32[9,3,16,128]{3,2,1,0:T(8,128)S(1)} %collective-permute-done.11.refs_1_), custom_call_target="tpu_custom_call" | custom-call | tf_op jit(solution)/shard_map/pallas_call | solution.py:349
  (12 shorter events, 0.2 us)
Async XLA Ops:
  2.3 1.8 %collective-permute-start.1 = (f32[2,3,112,128]{3,2,1,0:T(8,128)S(1)}, f32[2,3,112,128]{3,2,1,0:T(8,128)S(1)}, u32[]{:S(2)}, u32[]{:S(2)}) collective-permute-start(f32[2,3,112,128]{3,2,1,0:T(8,128)S(1)} %get-tuple-element.20), channel_id=1, source_target_pairs={{0,1},{1,0},{2,3},{3,2},{4,5},{5,4},{6,7},{7,6},{8,9},{9,8},{10,11... | collective-permute-start | bytes 1032200 | tf_op jit(solution)/shard_map/ppermute | solution.py:361
  2.8 15.3 %collective-permute-start = (f32[9,3,32,128]{3,2,1,0:T(8,128)S(1)}, f32[9,3,32,128]{3,2,1,0:T(8,128)S(1)}, u32[]{:S(2)}, u32[]{:S(2)}) collective-permute-start(f32[9,3,32,128]{3,2,1,0:T(8,128)S(1)} %get-tuple-element.18), channel_id=1, source_target_pairs={{0,1},{1,0},{2,3},{3,2},{4,5},{5,4},{6,7},{7,6},{8,9},{9,8},{10,11... | collective-permute-start | bytes 1327112 | tf_op jit(solution)/shard_map/ppermute | solution.py:361
  4.1 14.0 %collective-permute-start.3 = (f32[2,3,112,128]{3,2,1,0:T(8,128)S(1)}, f32[2,3,112,128]{3,2,1,0:T(8,128)S(1)}, u32[]{:S(2)}, u32[]{:S(2)}) collective-permute-start(f32[2,3,112,128]{3,2,1,0:T(8,128)S(1)} %get-tuple-element.31), channel_id=1, source_target_pairs={{4,0},{8,4},{12,8},{5,1},{9,5},{13,9},{6,2},{10,6},{14,10},{7,3},{... | collective-permute-start | bytes 1032200 | tf_op jit(solution)/shard_map/ppermute | solution.py:366
  5.4 13.1 %collective-permute-start.2 = (f32[2,3,112,128]{3,2,1,0:T(8,128)S(1)}, f32[2,3,112,128]{3,2,1,0:T(8,128)S(1)}, u32[]{:S(2)}, u32[]{:S(2)}) collective-permute-start(f32[2,3,112,128]{3,2,1,0:T(8,128)S(1)} %get-tuple-element.32), channel_id=1, source_target_pairs={{0,4},{4,8},{8,12},{1,5},{5,9},{9,13},{2,6},{6,10},{10,14},{3,7},{... | collective-permute-start | bytes 1032200 | tf_op jit(solution)/shard_map/ppermute | solution.py:366
  12.3 3.9 %collective-permute-start.4 = (s32[8,128]{1,0:T(8,128)S(1)}, s32[8,128]{1,0:T(8,128)S(1)}, u32[]{:S(2)}, u32[]{:S(2)}) collective-permute-start(s32[8,128]{1,0:T(8,128)S(1)} %broadcast_in_dim.3.base), channel_id=1, source_target_pairs={{0,16},{16,0},{1,17},{17,1},{2,18},{18,2},{3,19},{19,3},{4,20},{20... | collective-permute-start | bytes 12296 | tf_op jit(solution)/shard_map/ppermute | solution.py:361
  18.5 22.0 %copy-start = (f32[72,72]{1,0:T(8,128)S(1)}, f32[72,72]{1,0:T(8,128)}, u32[]{:S(2)}) copy-start(f32[72,72]{1,0:T(8,128)} %weights.5) | copy-start | bytes 62212
  27.3 6.0 %collective-permute-start.5 = (f32[9,3,16,128]{3,2,1,0:T(8,128)S(1)}, f32[9,3,16,128]{3,2,1,0:T(8,128)S(1)}, u32[]{:S(2)}, u32[]{:S(2)}) collective-permute-start(f32[9,3,16,128]{3,2,1,0:T(8,128)S(1)} %get-tuple-element.22), channel_id=1, source_target_pairs={{0,1},{1,0},{2,3},{3,2},{4,5},{5,4},{6,7},{7,6},{8,9},{9,8},{10,11... | collective-permute-start | bytes 663560 | tf_op jit(solution)/shard_map/ppermute | solution.py:361
  27.3 9.3 %collective-permute-start.6 = (f32[9,3,16,128]{3,2,1,0:T(8,128)S(1)}, f32[9,3,16,128]{3,2,1,0:T(8,128)S(1)}, u32[]{:S(2)}, u32[]{:S(2)}) collective-permute-start(f32[9,3,16,128]{3,2,1,0:T(8,128)S(1)} %get-tuple-element.23), channel_id=1, source_target_pairs={{0,18},{2,16},{16,2},{18,0},{1,19},{3,17},{17,3},{19,1},{4,22},{6,... | collective-permute-start | bytes 663560 | tf_op jit(solution)/shard_map/ppermute | solution.py:361
  30.0 10.5 %collective-permute-start.7 = (f32[9,3,16,128]{3,2,1,0:T(8,128)S(1)}, f32[9,3,16,128]{3,2,1,0:T(8,128)S(1)}, u32[]{:S(2)}, u32[]{:S(2)}) collective-permute-start(f32[9,3,16,128]{3,2,1,0:T(8,128)S(1)} %get-tuple-element.24), channel_id=1, source_target_pairs={{0,19},{1,18},{2,17},{3,16},{16,3},{17,2},{18,1},{19,0},{4,23},{5,... | collective-permute-start | bytes 663560 | tf_op jit(solution)/shard_map/ppermute | solution.py:361
  30.1 16.2 %collective-permute-start.8 = (f32[9,3,16,128]{3,2,1,0:T(8,128)S(1)}, f32[9,3,16,128]{3,2,1,0:T(8,128)S(1)}, u32[]{:S(2)}, u32[]{:S(2)}) collective-permute-start(f32[9,3,16,128]{3,2,1,0:T(8,128)S(1)} %get-tuple-element.25), channel_id=1, source_target_pairs={{0,2},{2,0},{1,3},{3,1},{4,6},{6,4},{5,7},{7,5},{8,10},{10,8},{9,1... | collective-permute-start | bytes 663560 | tf_op jit(solution)/shard_map/ppermute | solution.py:361
  31.7 14.5 %collective-permute-start.9 = (f32[9,3,16,128]{3,2,1,0:T(8,128)S(1)}, f32[9,3,16,128]{3,2,1,0:T(8,128)S(1)}, u32[]{:S(2)}, u32[]{:S(2)}) collective-permute-start(f32[9,3,16,128]{3,2,1,0:T(8,128)S(1)} %get-tuple-element.26), channel_id=1, source_target_pairs={{0,16},{16,0},{1,17},{17,1},{2,18},{18,2},{3,19},{19,3},{4,20},{20... | collective-permute-start | bytes 663560 | tf_op jit(solution)/shard_map/ppermute | solution.py:361
  33.3 16.8 %collective-permute-start.10 = (f32[9,3,16,128]{3,2,1,0:T(8,128)S(1)}, f32[9,3,16,128]{3,2,1,0:T(8,128)S(1)}, u32[]{:S(2)}, u32[]{:S(2)}) collective-permute-start(f32[9,3,16,128]{3,2,1,0:T(8,128)S(1)} %get-tuple-element.27), channel_id=1, source_target_pairs={{0,3},{1,2},{2,1},{3,0},{4,7},{5,6},{6,5},{7,4},{8,11},{9,10},{10,... | collective-permute-start | bytes 663560 | tf_op jit(solution)/shard_map/ppermute | solution.py:361
  36.6 13.6 %collective-permute-start.11 = (f32[9,3,16,128]{3,2,1,0:T(8,128)S(1)}, f32[9,3,16,128]{3,2,1,0:T(8,128)S(1)}, u32[]{:S(2)}, u32[]{:S(2)}) collective-permute-start(f32[9,3,16,128]{3,2,1,0:T(8,128)S(1)} %get-tuple-element.28), channel_id=1, source_target_pairs={{0,17},{1,16},{16,1},{17,0},{2,19},{3,18},{18,3},{19,2},{4,21},{5,... | collective-permute-start | bytes 663560 | tf_op jit(solution)/shard_map/ppermute | solution.py:361

commit v10 on v9

--- a/solution.py
+++ b/solution.py
@@ -283,11 +283,11 @@
     return jnp.concatenate([high, high, low], axis=1)
 
 
-def weighted(balance, places, pieces, columns, emit):
+def weighted(balance, places, pieces, matrix, columns, emit):
     total = balance.shape[0]
     tiles, height = columns.shape[1:3]
     count, pitch = sum(p.shape[0] for p in pieces), tiles * height
-    unpack(pieces, packing(tiles * LANES, 2 * tiles, lax.axis_index("lon"), 0), columns)
+    unpack(pieces, matrix[...], columns)
     flat = columns.reshape(columns.shape[0] * pitch, LANES)
     stacked = chosen(balance, places, count)
     for t in range(tiles):
@@ -299,16 +299,22 @@
 
 
 def share_kernel(places, weights, *refs):
-    *pieces, out, columns = refs
-    earlier = pieces.pop(0) if len(pieces) > len(places) else None
+    *pieces, out, matrix, columns = refs
+    earlier = None
+    if len(pieces) > len(places):
+        earlier, given, *pieces = pieces
+        matrix[...] = given[...]
+    else:
+        tiles = columns.shape[1]
+        matrix[...] = packing(tiles * LANES, 2 * tiles, lax.axis_index("lon"), 0)
 
     def store(t, r, rows, value):
         out[rows, :] = value if earlier is None else earlier[rows, :] + value
 
-    weighted(weights, places, pieces, columns, store)
-
-
-def last_kernel(places, weights, earlier, *refs):
+    weighted(weights, places, pieces, matrix, columns, store)
+
+
+def last_kernel(places, weights, earlier, matrix, *refs):
     *pieces, out, columns, result, sent = refs
     total = weights.shape[0]
     tiles, height = columns.shape[1:3]
@@ -326,7 +332,7 @@
             copy.start()
             copies.append(copy)
 
-    weighted(weights, places, pieces, columns, store)
+    weighted(weights, places, pieces, matrix, columns, store)
     for copy in copies:
         copy.wait()
 
@@ -336,13 +342,14 @@
     tiles, height = pieces[0].shape[1:3]
     flat = (total * tiles * height, LANES)
     columns = VMEM((-(-count // SUB) * SUB, tiles, height, LANES), jnp.float32)
-    operands = (weights, *(() if earlier is None else (earlier,)), *pieces)
+    operands = (weights, *(() if earlier is None else earlier), *pieces)
+    matrix = jax.ShapeDtypeStruct((tiles * LANES, tiles * LANES), jnp.bfloat16)
     if not last:
         return pl.pallas_call(
             functools.partial(share_kernel, places),
-            out_shape=jax.ShapeDtypeStruct(flat, jnp.float32),
+            out_shape=(jax.ShapeDtypeStruct(flat, jnp.float32), matrix),
             in_specs=[whole()] * len(operands),
-            out_specs=whole(),
+            out_specs=(whole(), whole()),
             scratch_shapes=[columns],
             compiler_params=budget(10),
         )(*operands)

time: 53.2 us -> 53.1 us (level)
  no operation moved by 1% of the time
where the time goes in v10:
time: 53.1 us; the launch traced here: 52.9 us
  Pallas kernels  19.9 us (37%)
  starting transfers between devices  15.8 us (30%)
  waiting for transfers between devices  14.2 us (27%)
  other arithmetic  1.58 us (3%)
  between operations  1.42 us (3%)
    ppermute x10, waiting for transfers between devices, crossed(): return lax.ppermute(block, axes, [(i, count - 1 - i) for i in range(count)])  13.8 us
    ppermute x10, starting transfers between devices, crossed(): return lax.ppermute(block, axes, [(i, count - 1 - i) for i in range(count)])  9.01 us
    pallas_call x1, Pallas kernels, diffuse(): pl.pallas_call(functools.partial(diffuse_kernel, halo, halves, blocks[0])...  8.71 us
    ppermute x2, starting transfers between devices, shifted(): lax.ppermute(block, 'lat', [(i, i + step) for i in range(strips) if 0 <=...  6.79 us
    pallas_call x2, Pallas kernels, balanced(): pl.pallas_call(functools.partial(share_kernel, places), out_shape=(jax.Sh...  3.93 us
    pallas_call x2, Pallas kernels, noise(): pl.pallas_call(functools.partial(noise_kernel, levels_here, halo, total_r...  3.83 us
    pallas_call x1, Pallas kernels, balanced(): pl.pallas_call(functools.partial(last_kernel, places), out_shape=jax.Shap...  2.71 us
    mul x1, other arithmetic, per_device(): part(diffusivity, member * 2 + c, share, 0)  1.54 us
  transfers between devices with their start and end apart: 12, of which 7 were waited for; matrix products, arithmetic and copies ran while one was open for 0% of the time, Pallas kernels for 15%

profile of v10, /device:TPU:0, one launch (start us, length us, event | category | flops | bytes accessed | tf_op | source)
XLA Modules:
  0.0 52.9 jit_solution(12998336091628261046)
XLA Ops:
  0.0 1.5 %convert_multiply_fusion = (f32[9,32,384]{2,1,0:T(8,128)S(1)}, f32[9,32,384]{2,1,0:T(8,128)S(1)}) fusion(s32[36,32,384]{2,1,0:T(8,128)} %param.5, s32[]{:T(128)S(6)} %select_n.9, f32[36,32,384]{2,1,0:T(8,128)} %param.6, s32[]{:T(128)S(6)} %select_n.8), kind=kLoop, calls=%fused_computation.2 | loop fusion | flops 442368 | bytes 2654216 | tf_op jit(solution)/shard_map/mul | solution.py:409
  1.5 0.7 %shard_map.55 = (f32[9,3,32,128]{3,2,1,0:T(8,128)S(1)}, f32[9,3,32,128]{3,2,1,0:T(8,128)S(1)}, f32[2,3,112,128]{3,2,1,0:T(8,128)S(1)}, f32[2,3,112,128]{3,2,1,0:T(8,128)S(1)}) custom-call(f32[9,32,384]{2,1,0:T(8,128)S(1)} %get-tuple-element.38.kept, f32[9,32,384]{2,1,0:T(8,128)S(1)} %get-tuple-element.37.other), custom_call_target="tpu_custom_call" | custom-call | tf_op jit(solution)/shard_map/pallas_call | solution.py:94
  2.3 0.5 collective-permute-start.1
  2.9 1.2 %collective-permute-done.1 = f32[2,3,112,128]{3,2,1,0:T(8,128)S(1)} collective-permute-done((f32[2,3,112,128]{3,2,1,0:T(8,128)S(1)}, f32[2,3,112,128]{3,2,1,0:T(8,128)S(1)}, u32[]{:S(2)}, u32[]{:S(2)}) %collective-permute-start.1) | collective-permute-done | bytes 344096 | tf_op jit(solution)/shard_map/ppermute | solution.py:368
  4.1 1.3 %collective-permute-start.3 = (f32[2,3,112,128]{3,2,1,0:T(8,128)S(1)}, f32[2,3,112,128]{3,2,1,0:T(8,128)S(1)}, u32[]{:S(2)}, u32[]{:S(2)}) collective-permute-start(f32[2,3,112,128]{3,2,1,0:T(8,128)S(1)} %get-tuple-element.39), channel_id=1, source_target_pairs={{4,0},{8,4},{12,8},{5,1},{9,5},{13,9},{6,2},{10,6},{14,10},{7,3},{... | collective-permute-start | bytes 1032200 | tf_op jit(solution)/shard_map/ppermute | solution.py:373
  5.4 5.5 %collective-permute-start.2 = (f32[2,3,112,128]{3,2,1,0:T(8,128)S(1)}, f32[2,3,112,128]{3,2,1,0:T(8,128)S(1)}, u32[]{:S(2)}, u32[]{:S(2)}) collective-permute-start(f32[2,3,112,128]{3,2,1,0:T(8,128)S(1)} %get-tuple-element.40), channel_id=1, source_target_pairs={{0,4},{4,8},{8,12},{1,5},{5,9},{9,13},{2,6},{6,10},{10,14},{3,7},{... | collective-permute-start | bytes 1032200 | tf_op jit(solution)/shard_map/ppermute | solution.py:373
  12.3 2.0 %collective-permute-start.4 = (s32[8,128]{1,0:T(8,128)S(1)}, s32[8,128]{1,0:T(8,128)S(1)}, u32[]{:S(2)}, u32[]{:S(2)}) collective-permute-start(s32[8,128]{1,0:T(8,128)S(1)} %broadcast_in_dim.3.base), channel_id=1, source_target_pairs={{0,16},{16,0},{1,17},{17,1},{2,18},{18,2},{3,19},{19,3},{4,20},{20... | collective-permute-start | bytes 12296 | tf_op jit(solution)/shard_map/ppermute | solution.py:368
  14.3 1.9 %shard_map.57.own_source = f32[9,6,7,8,128]{4,3,2,1,0:T(8,128)S(1)} custom-call(s32[8,128]{1,0:T(8,128)S(1)} %broadcast_in_dim.3.base), custom_call_target="tpu_custom_call" | custom-call | tf_op jit(solution)/shard_map/pallas_call | solution.py:123
  16.2 1.9 %shard_map.56.other_source = f32[9,6,7,8,128]{4,3,2,1,0:T(8,128)S(1)} custom-call(s32[8,128]{1,0:T(8,128)S(1)} %collective-permute-done.4.base), custom_call_target="tpu_custom_call" | custom-call | tf_op jit(solution)/shard_map/pallas_call | solution.py:123
  18.1 0.4 collective-permute-done.2.top
  18.5 8.7 %shard_map.58 = (f32[9,3,16,128]{3,2,1,0:T(8,128)S(1)}, f32[9,3,16,128]{3,2,1,0:T(8,128)S(1)}, f32[9,3,16,128]{3,2,1,0:T(8,128)S(1)}, f32[9,3,16,128]{3,2,1,0:T(...) custom-call(f32[9,3,32,128]{3,2,1,0:T(8,128)S(1)} %get-tuple-element, ...), custom_call_target="tpu_custom_call" | custom-call | tf_op jit(solution)/shard_map/pallas_call | solution.py:244
  27.3 2.7 %collective-permute-start.6 = (f32[9,3,16,128]{3,2,1,0:T(8,128)S(1)}, f32[9,3,16,128]{3,2,1,0:T(8,128)S(1)}, u32[]{:S(2)}, u32[]{:S(2)}) collective-permute-start(f32[9,3,16,128]{3,2,1,0:T(8,128)S(1)} %get-tuple-element.27), channel_id=1, source_target_pairs={{0,18},{2,16},{16,2},{18,0},{1,19},{3,17},{17,3},{19,1},{4,22},{6,... | collective-permute-start | bytes 663560 | tf_op jit(solution)/shard_map/ppermute | solution.py:368
  30.0 0.1 collective-permute-start.7
  30.1 1.6 %collective-permute-start.8 = (f32[9,3,16,128]{3,2,1,0:T(8,128)S(1)}, f32[9,3,16,128]{3,2,1,0:T(8,128)S(1)}, u32[]{:S(2)}, u32[]{:S(2)}) collective-permute-start(f32[9,3,16,128]{3,2,1,0:T(8,128)S(1)} %get-tuple-element.31), channel_id=1, source_target_pairs={{0,2},{2,0},{1,3},{3,1},{4,6},{6,4},{5,7},{7,5},{8,10},{10,8},{9,1... | collective-permute-start | bytes 663560 | tf_op jit(solution)/shard_map/ppermute | solution.py:368
  31.7 1.5 %collective-permute-start.9 = (f32[9,3,16,128]{3,2,1,0:T(8,128)S(1)}, f32[9,3,16,128]{3,2,1,0:T(8,128)S(1)}, u32[]{:S(2)}, u32[]{:S(2)}) collective-permute-start(f32[9,3,16,128]{3,2,1,0:T(8,128)S(1)} %get-tuple-element.32), channel_id=1, source_target_pairs={{0,16},{16,0},{1,17},{17,1},{2,18},{18,2},{3,19},{19,3},{4,20},{20... | collective-permute-start | bytes 663560 | tf_op jit(solution)/shard_map/ppermute | solution.py:368
  33.3 3.4 %collective-permute-done.6.refs_2_ = f32[9,3,16,128]{3,2,1,0:T(8,128)S(1)} collective-permute-done((f32[9,3,16,128]{3,2,1,0:T(8,128)S(1)}, f32[9,3,16,128]{3,2,1,0:T(8,128)S(1)}, u32[]{:S(2)}, u32[]{:S(2)}) %collective-permute-start.6) | collective-permute-done | bytes 221216 | tf_op jit(solution)/shard_map/ppermute | solution.py:368
  36.6 0.4 collective-permute-start.11
  37.0 3.5 %collective-permute-done.7.refs_3_ = f32[9,3,16,128]{3,2,1,0:T(8,128)S(1)} collective-permute-done((f32[9,3,16,128]{3,2,1,0:T(8,128)S(1)}, f32[9,3,16,128]{3,2,1,0:T(8,128)S(1)}, u32[]{:S(2)}, u32[]{:S(2)}) %collective-permute-start.7) | collective-permute-done | bytes 221216 | tf_op jit(solution)/shard_map/ppermute | solution.py:368
  40.5 2.0 %shard_map.59 = (f32[3456,128]{1,0:T(8,128)S(1)}, bf16[384,384]{1,0:T(8,128)(2,1)S(1)}) custom-call(f32[72,72]{1,0:T(8,128)S(1)} %copy-done, f32[9,3,16,128]{3,2,1,0:T(8,128)S(1)} %get-tuple-element.25.refs_0_, f32[9,3,16,128]{3,2,1,0:T(8,128)S(1)} %collective-permute-done.5.refs_1_, f32[9,3,16,128]{3,2,1,0:T(8,128)S(1)} %collective-permute-done.6.refs_2_, ...), custom_call_target="tpu_custom_call" | custom-call | tf_op jit(solution)/shard_map/pallas_call | solution.py:348
  42.5 3.7 %collective-permute-done.8.refs_2_ = f32[9,3,16,128]{3,2,1,0:T(8,128)S(1)} collective-permute-done((f32[9,3,16,128]{3,2,1,0:T(8,128)S(1)}, f32[9,3,16,128]{3,2,1,0:T(8,128)S(1)}, u32[]{:S(2)}, u32[]{:S(2)}) %collective-permute-start.8) | collective-permute-done | bytes 221216 | tf_op jit(solution)/shard_map/ppermute | solution.py:368
  46.3 1.9 %shard_map.60 = (f32[3456,128]{1,0:T(8,128)S(1)}, bf16[384,384]{1,0:T(8,128)(2,1)S(1)}) custom-call(f32[72,72]{1,0:T(8,128)S(1)} %copy-done, f32[3456,128]{1,0:T(8,128)S(1)} %get-tuple-element.29.refs_0_, bf16[384,384]{1,0:T(8,128)(2,1)S(1)} %get-tuple-element.30.refs_1_, f32[9,3,16,128]{3,2,1,0:T(8,128)S(1)} %collective-permute-done.8.refs_2_, ...), custom_call_target="tpu_custom_call" | custom-call | tf_op jit(solution)/shard_map/pallas_call | solution.py:348
  48.2 1.9 %collective-permute-done.10.refs_0_ = f32[9,3,16,128]{3,2,1,0:T(8,128)S(1)} collective-permute-done((f32[9,3,16,128]{3,2,1,0:T(8,128)S(1)}, f32[9,3,16,128]{3,2,1,0:T(8,128)S(1)}, u32[]{:S(2)}, u32[]{:S(2)}) %collective-permute-start.10) | collective-permute-done | bytes 221216 | tf_op jit(solution)/shard_map/ppermute | solution.py:368
  50.1 0.1 collective-permute-done.11.refs_1_
  50.2 2.7 %shard_map.61 = f32[72,16,384]{2,1,0:T(8,128)} custom-call(f32[72,72]{1,0:T(8,128)S(1)} %copy-done, f32[3456,128]{1,0:T(8,128)S(1)} %get-tuple-element.33.earlier, bf16[384,384]{1,0:T(8,128)(2,1)S(1)} %get-tuple-element.34.matrix, f32[9,3,16,128]{3,2,1,0:T(8,128)S(1)} %collective-permute-done.10.refs_0_, f32[9,3,16,128]{3,2,1,0:T(8,128)S(1)} %collective-permute-done.11.refs_1_), custom_call_target="tpu_custom_call" | custom-call | tf_op jit(solution)/shard_map/pallas_call | solution.py:356
  (12 shorter events, 0.2 us)
Async XLA Ops:
  2.3 1.8 %collective-permute-start.1 = (f32[2,3,112,128]{3,2,1,0:T(8,128)S(1)}, f32[2,3,112,128]{3,2,1,0:T(8,128)S(1)}, u32[]{:S(2)}, u32[]{:S(2)}) collective-permute-start(f32[2,3,112,128]{3,2,1,0:T(8,128)S(1)} %get-tuple-element.24), channel_id=1, source_target_pairs={{0,1},{1,0},{2,3},{3,2},{4,5},{5,4},{6,7},{7,6},{8,9},{9,8},{10,11... | collective-permute-start | bytes 1032200 | tf_op jit(solution)/shard_map/ppermute | solution.py:368
  2.8 15.3 %collective-permute-start = (f32[9,3,32,128]{3,2,1,0:T(8,128)S(1)}, f32[9,3,32,128]{3,2,1,0:T(8,128)S(1)}, u32[]{:S(2)}, u32[]{:S(2)}) collective-permute-start(f32[9,3,32,128]{3,2,1,0:T(8,128)S(1)} %get-tuple-element.22), channel_id=1, source_target_pairs={{0,1},{1,0},{2,3},{3,2},{4,5},{5,4},{6,7},{7,6},{8,9},{9,8},{10,11... | collective-permute-start | bytes 1327112 | tf_op jit(solution)/shard_map/ppermute | solution.py:368
  4.1 14.0 %collective-permute-start.3 = (f32[2,3,112,128]{3,2,1,0:T(8,128)S(1)}, f32[2,3,112,128]{3,2,1,0:T(8,128)S(1)}, u32[]{:S(2)}, u32[]{:S(2)}) collective-permute-start(f32[2,3,112,128]{3,2,1,0:T(8,128)S(1)} %get-tuple-element.39), channel_id=1, source_target_pairs={{4,0},{8,4},{12,8},{5,1},{9,5},{13,9},{6,2},{10,6},{14,10},{7,3},{... | collective-permute-start | bytes 1032200 | tf_op jit(solution)/shard_map/ppermute | solution.py:373
  5.4 13.1 %collective-permute-start.2 = (f32[2,3,112,128]{3,2,1,0:T(8,128)S(1)}, f32[2,3,112,128]{3,2,1,0:T(8,128)S(1)}, u32[]{:S(2)}, u32[]{:S(2)}) collective-permute-start(f32[2,3,112,128]{3,2,1,0:T(8,128)S(1)} %get-tuple-element.40), channel_id=1, source_target_pairs={{0,4},{4,8},{8,12},{1,5},{5,9},{9,13},{2,6},{6,10},{10,14},{3,7},{... | collective-permute-start | bytes 1032200 | tf_op jit(solution)/shard_map/ppermute | solution.py:373
  12.3 3.9 %collective-permute-start.4 = (s32[8,128]{1,0:T(8,128)S(1)}, s32[8,128]{1,0:T(8,128)S(1)}, u32[]{:S(2)}, u32[]{:S(2)}) collective-permute-start(s32[8,128]{1,0:T(8,128)S(1)} %broadcast_in_dim.3.base), channel_id=1, source_target_pairs={{0,16},{16,0},{1,17},{17,1},{2,18},{18,2},{3,19},{19,3},{4,20},{20... | collective-permute-start | bytes 12296 | tf_op jit(solution)/shard_map/ppermute | solution.py:368
  18.5 22.0 %copy-start = (f32[72,72]{1,0:T(8,128)S(1)}, f32[72,72]{1,0:T(8,128)}, u32[]{:S(2)}) copy-start(f32[72,72]{1,0:T(8,128)} %weights.5) | copy-start | bytes 62212
  27.3 6.0 %collective-permute-start.5 = (f32[9,3,16,128]{3,2,1,0:T(8,128)S(1)}, f32[9,3,16,128]{3,2,1,0:T(8,128)S(1)}, u32[]{:S(2)}, u32[]{:S(2)}) collective-permute-start(f32[9,3,16,128]{3,2,1,0:T(8,128)S(1)} %get-tuple-element.26), channel_id=1, source_target_pairs={{0,1},{1,0},{2,3},{3,2},{4,5},{5,4},{6,7},{7,6},{8,9},{9,8},{10,11... | collective-permute-start | bytes 663560 | tf_op jit(solution)/shard_map/ppermute | solution.py:368
  27.3 9.3 %collective-permute-start.6 = (f32[9,3,16,128]{3,2,1,0:T(8,128)S(1)}, f32[9,3,16,128]{3,2,1,0:T(8,128)S(1)}, u32[]{:S(2)}, u32[]{:S(2)}) collective-permute-start(f32[9,3,16,128]{3,2,1,0:T(8,128)S(1)} %get-tuple-element.27), channel_id=1, source_target_pairs={{0,18},{2,16},{16,2},{18,0},{1,19},{3,17},{17,3},{19,1},{4,22},{6,... | collective-permute-start | bytes 663560 | tf_op jit(solution)/shard_map/ppermute | solution.py:368
  30.0 10.5 %collective-permute-start.7 = (f32[9,3,16,128]{3,2,1,0:T(8,128)S(1)}, f32[9,3,16,128]{3,2,1,0:T(8,128)S(1)}, u32[]{:S(2)}, u32[]{:S(2)}) collective-permute-start(f32[9,3,16,128]{3,2,1,0:T(8,128)S(1)} %get-tuple-element.28), channel_id=1, source_target_pairs={{0,19},{1,18},{2,17},{3,16},{16,3},{17,2},{18,1},{19,0},{4,23},{5,... | collective-permute-start | bytes 663560 | tf_op jit(solution)/shard_map/ppermute | solution.py:368
  30.1 16.2 %collective-permute-start.8 = (f32[9,3,16,128]{3,2,1,0:T(8,128)S(1)}, f32[9,3,16,128]{3,2,1,0:T(8,128)S(1)}, u32[]{:S(2)}, u32[]{:S(2)}) collective-permute-start(f32[9,3,16,128]{3,2,1,0:T(8,128)S(1)} %get-tuple-element.31), channel_id=1, source_target_pairs={{0,2},{2,0},{1,3},{3,1},{4,6},{6,4},{5,7},{7,5},{8,10},{10,8},{9,1... | collective-permute-start | bytes 663560 | tf_op jit(solution)/shard_map/ppermute | solution.py:368
  31.7 14.5 %collective-permute-start.9 = (f32[9,3,16,128]{3,2,1,0:T(8,128)S(1)}, f32[9,3,16,128]{3,2,1,0:T(8,128)S(1)}, u32[]{:S(2)}, u32[]{:S(2)}) collective-permute-start(f32[9,3,16,128]{3,2,1,0:T(8,128)S(1)} %get-tuple-element.32), channel_id=1, source_target_pairs={{0,16},{16,0},{1,17},{17,1},{2,18},{18,2},{3,19},{19,3},{4,20},{20... | collective-permute-start | bytes 663560 | tf_op jit(solution)/shard_map/ppermute | solution.py:368
  33.3 16.8 %collective-permute-start.10 = (f32[9,3,16,128]{3,2,1,0:T(8,128)S(1)}, f32[9,3,16,128]{3,2,1,0:T(8,128)S(1)}, u32[]{:S(2)}, u32[]{:S(2)}) collective-permute-start(f32[9,3,16,128]{3,2,1,0:T(8,128)S(1)} %get-tuple-element.35), channel_id=1, source_target_pairs={{0,3},{1,2},{2,1},{3,0},{4,7},{5,6},{6,5},{7,4},{8,11},{9,10},{10,... | collective-permute-start | bytes 663560 | tf_op jit(solution)/shard_map/ppermute | solution.py:368
  36.6 13.6 %collective-permute-start.11 = (f32[9,3,16,128]{3,2,1,0:T(8,128)S(1)}, f32[9,3,16,128]{3,2,1,0:T(8,128)S(1)}, u32[]{:S(2)}, u32[]{:S(2)}) collective-permute-start(f32[9,3,16,128]{3,2,1,0:T(8,128)S(1)} %get-tuple-element.36), channel_id=1, source_target_pairs={{0,17},{1,16},{16,1},{17,0},{2,19},{3,18},{18,3},{19,2},{4,21},{5,... | collective-permute-start | bytes 663560 | tf_op jit(solution)/shard_map/ppermute | solution.py:368

commit v11 on v10

--- a/solution.py
+++ b/solution.py
@@ -252,16 +252,15 @@
 
 
 def unpack(pieces, matrix, out):
-    start = 0
-    for piece in pieces:
-        levels, tiles, height, _ = piece.shape
-        values = jnp.concatenate(
-            [piece[:, t].reshape(levels * height, LANES) for t in range(tiles)], axis=1
-        )
-        moved = permuted(values, matrix)
-        for t in range(tiles):
-            out[start : start + levels, t] = moved[:, t * LANES : (t + 1) * LANES].reshape(levels, height, LANES)
-        start += levels
+    levels, tiles, height, _ = pieces[0].shape
+    values = [
+        jnp.concatenate([piece[:, t].reshape(levels * height, LANES) for t in range(tiles)], axis=1)
+        for piece in pieces
+    ]
+    moved = permuted(jnp.concatenate(values, axis=0), matrix)
+    count = levels * len(pieces)
+    for t in range(tiles):
+        out[:count, t] = moved[:, t * LANES : (t + 1) * LANES].reshape(count, height, LANES)
 
 
 def chosen(balance, places, width):

time: 53.1 us -> 53.2 us (level)
  no operation moved by 1% of the time
where the time goes in v11:
time: 53.2 us; the launch traced here: 53 us
  Pallas kernels  19.9 us (37%)
  starting transfers between devices  15.8 us (30%)
  waiting for transfers between devices  14.2 us (27%)
  other arithmetic  1.58 us (3%)
  between operations  1.41 us (3%)
    ppermute x10, waiting for transfers between devices, crossed(): return lax.ppermute(block, axes, [(i, count - 1 - i) for i in range(count)])  13.9 us
    ppermute x10, starting transfers between devices, crossed(): return lax.ppermute(block, axes, [(i, count - 1 - i) for i in range(count)])  9.01 us
    pallas_call x1, Pallas kernels, diffuse(): pl.pallas_call(functools.partial(diffuse_kernel, halo, halves, blocks[0])...  8.71 us
    ppermute x2, starting transfers between devices, shifted(): lax.ppermute(block, 'lat', [(i, i + step) for i in range(strips) if 0 <=...  6.79 us
    pallas_call x2, Pallas kernels, balanced(): pl.pallas_call(functools.partial(share_kernel, places), out_shape=(jax.Sh...  3.88 us
    pallas_call x2, Pallas kernels, noise(): pl.pallas_call(functools.partial(noise_kernel, levels_here, halo, total_r...  3.83 us
    pallas_call x1, Pallas kernels, balanced(): pl.pallas_call(functools.partial(last_kernel, places), out_shape=jax.Shap...  2.75 us
    mul x1, other arithmetic, per_device(): part(diffusivity, member * 2 + c, share, 0)  1.54 us
  transfers between devices with their start and end apart: 12, of which 7 were waited for; matrix products, arithmetic and copies ran while one was open for 0% of the time, Pallas kernels for 15%

profile of v11, /device:TPU:0, one launch (start us, length us, event | category | flops | bytes accessed | tf_op | source)
XLA Modules:
  0.0 53.0 jit_solution(375130013317984604)
XLA Ops:
  0.0 1.5 %convert_multiply_fusion = (f32[9,32,384]{2,1,0:T(8,128)S(1)}, f32[9,32,384]{2,1,0:T(8,128)S(1)}) fusion(s32[36,32,384]{2,1,0:T(8,128)} %param.5, s32[]{:T(128)S(6)} %select_n.9, f32[36,32,384]{2,1,0:T(8,128)} %param.6, s32[]{:T(128)S(6)} %select_n.8), kind=kLoop, calls=%fused_computation.2 | loop fusion | flops 442368 | bytes 2654216 | tf_op jit(solution)/shard_map/mul | solution.py:408
  1.5 0.7 %shard_map.55 = (f32[9,3,32,128]{3,2,1,0:T(8,128)S(1)}, f32[9,3,32,128]{3,2,1,0:T(8,128)S(1)}, f32[2,3,112,128]{3,2,1,0:T(8,128)S(1)}, f32[2,3,112,128]{3,2,1,0:T(8,128)S(1)}) custom-call(f32[9,32,384]{2,1,0:T(8,128)S(1)} %get-tuple-element.38.kept, f32[9,32,384]{2,1,0:T(8,128)S(1)} %get-tuple-element.37.other), custom_call_target="tpu_custom_call" | custom-call | tf_op jit(solution)/shard_map/pallas_call | solution.py:94
  2.3 0.5 collective-permute-start.1
  2.9 1.2 %collective-permute-done.1 = f32[2,3,112,128]{3,2,1,0:T(8,128)S(1)} collective-permute-done((f32[2,3,112,128]{3,2,1,0:T(8,128)S(1)}, f32[2,3,112,128]{3,2,1,0:T(8,128)S(1)}, u32[]{:S(2)}, u32[]{:S(2)}) %collective-permute-start.1) | collective-permute-done | bytes 344096 | tf_op jit(solution)/shard_map/ppermute | solution.py:367
  4.1 1.3 %collective-permute-start.3 = (f32[2,3,112,128]{3,2,1,0:T(8,128)S(1)}, f32[2,3,112,128]{3,2,1,0:T(8,128)S(1)}, u32[]{:S(2)}, u32[]{:S(2)}) collective-permute-start(f32[2,3,112,128]{3,2,1,0:T(8,128)S(1)} %get-tuple-element.39), channel_id=1, source_target_pairs={{4,0},{8,4},{12,8},{5,1},{9,5},{13,9},{6,2},{10,6},{14,10},{7,3},{... | collective-permute-start | bytes 1032200 | tf_op jit(solution)/shard_map/ppermute | solution.py:372
  5.4 5.5 %collective-permute-start.2 = (f32[2,3,112,128]{3,2,1,0:T(8,128)S(1)}, f32[2,3,112,128]{3,2,1,0:T(8,128)S(1)}, u32[]{:S(2)}, u32[]{:S(2)}) collective-permute-start(f32[2,3,112,128]{3,2,1,0:T(8,128)S(1)} %get-tuple-element.40), channel_id=1, source_target_pairs={{0,4},{4,8},{8,12},{1,5},{5,9},{9,13},{2,6},{6,10},{10,14},{3,7},{... | collective-permute-start | bytes 1032200 | tf_op jit(solution)/shard_map/ppermute | solution.py:372
  12.3 2.0 %collective-permute-start.4 = (s32[8,128]{1,0:T(8,128)S(1)}, s32[8,128]{1,0:T(8,128)S(1)}, u32[]{:S(2)}, u32[]{:S(2)}) collective-permute-start(s32[8,128]{1,0:T(8,128)S(1)} %broadcast_in_dim.3.base), channel_id=1, source_target_pairs={{0,16},{16,0},{1,17},{17,1},{2,18},{18,2},{3,19},{19,3},{4,20},{20... | collective-permute-start | bytes 12296 | tf_op jit(solution)/shard_map/ppermute | solution.py:367
  14.3 1.9 %shard_map.57.own_source = f32[9,6,7,8,128]{4,3,2,1,0:T(8,128)S(1)} custom-call(s32[8,128]{1,0:T(8,128)S(1)} %broadcast_in_dim.3.base), custom_call_target="tpu_custom_call" | custom-call | tf_op jit(solution)/shard_map/pallas_call | solution.py:123
  16.2 1.9 %shard_map.56.other_source = f32[9,6,7,8,128]{4,3,2,1,0:T(8,128)S(1)} custom-call(s32[8,128]{1,0:T(8,128)S(1)} %collective-permute-done.4.base), custom_call_target="tpu_custom_call" | custom-call | tf_op jit(solution)/shard_map/pallas_call | solution.py:123
  18.1 0.4 collective-permute-done.2.top
  18.5 8.7 %shard_map.58 = (f32[9,3,16,128]{3,2,1,0:T(8,128)S(1)}, f32[9,3,16,128]{3,2,1,0:T(8,128)S(1)}, f32[9,3,16,128]{3,2,1,0:T(8,128)S(1)}, f32[9,3,16,128]{3,2,1,0:T(...) custom-call(f32[9,3,32,128]{3,2,1,0:T(8,128)S(1)} %get-tuple-element, ...), custom_call_target="tpu_custom_call" | custom-call | tf_op jit(solution)/shard_map/pallas_call | solution.py:244
  27.3 2.7 %collective-permute-start.6 = (f32[9,3,16,128]{3,2,1,0:T(8,128)S(1)}, f32[9,3,16,128]{3,2,1,0:T(8,128)S(1)}, u32[]{:S(2)}, u32[]{:S(2)}) collective-permute-start(f32[9,3,16,128]{3,2,1,0:T(8,128)S(1)} %get-tuple-element.27), channel_id=1, source_target_pairs={{0,18},{2,16},{16,2},{18,0},{1,19},{3,17},{17,3},{19,1},{4,22},{6,... | collective-permute-start | bytes 663560 | tf_op jit(solution)/shard_map/ppermute | solution.py:367
  30.0 0.1 collective-permute-start.7
  30.1 1.6 %collective-permute-start.8 = (f32[9,3,16,128]{3,2,1,0:T(8,128)S(1)}, f32[9,3,16,128]{3,2,1,0:T(8,128)S(1)}, u32[]{:S(2)}, u32[]{:S(2)}) collective-permute-start(f32[9,3,16,128]{3,2,1,0:T(8,128)S(1)} %get-tuple-element.31), channel_id=1, source_target_pairs={{0,2},{2,0},{1,3},{3,1},{4,6},{6,4},{5,7},{7,5},{8,10},{10,8},{9,1... | collective-permute-start | bytes 663560 | tf_op jit(solution)/shard_map/ppermute | solution.py:367
  31.7 1.5 %collective-permute-start.9 = (f32[9,3,16,128]{3,2,1,0:T(8,128)S(1)}, f32[9,3,16,128]{3,2,1,0:T(8,128)S(1)}, u32[]{:S(2)}, u32[]{:S(2)}) collective-permute-start(f32[9,3,16,128]{3,2,1,0:T(8,128)S(1)} %get-tuple-element.32), channel_id=1, source_target_pairs={{0,16},{16,0},{1,17},{17,1},{2,18},{18,2},{3,19},{19,3},{4,20},{20... | collective-permute-start | bytes 663560 | tf_op jit(solution)/shard_map/ppermute | solution.py:367
  33.3 3.4 %collective-permute-done.6.refs_2_ = f32[9,3,16,128]{3,2,1,0:T(8,128)S(1)} collective-permute-done((f32[9,3,16,128]{3,2,1,0:T(8,128)S(1)}, f32[9,3,16,128]{3,2,1,0:T(8,128)S(1)}, u32[]{:S(2)}, u32[]{:S(2)}) %collective-permute-start.6) | collective-permute-done | bytes 221216 | tf_op jit(solution)/shard_map/ppermute | solution.py:367
  36.6 0.4 collective-permute-start.11
  37.0 3.5 %collective-permute-done.7.refs_3_ = f32[9,3,16,128]{3,2,1,0:T(8,128)S(1)} collective-permute-done((f32[9,3,16,128]{3,2,1,0:T(8,128)S(1)}, f32[9,3,16,128]{3,2,1,0:T(8,128)S(1)}, u32[]{:S(2)}, u32[]{:S(2)}) %collective-permute-start.7) | collective-permute-done | bytes 221216 | tf_op jit(solution)/shard_map/ppermute | solution.py:367
  40.5 2.0 %shard_map.59 = (f32[3456,128]{1,0:T(8,128)S(1)}, bf16[384,384]{1,0:T(8,128)(2,1)S(1)}) custom-call(f32[72,72]{1,0:T(8,128)S(1)} %copy-done, f32[9,3,16,128]{3,2,1,0:T(8,128)S(1)} %get-tuple-element.25.refs_0_, f32[9,3,16,128]{3,2,1,0:T(8,128)S(1)} %collective-permute-done.5.refs_1_, f32[9,3,16,128]{3,2,1,0:T(8,128)S(1)} %collective-permute-done.6.refs_2_, ...), custom_call_target="tpu_custom_call" | custom-call | tf_op jit(solution)/shard_map/pallas_call | solution.py:347
  42.5 3.8 %collective-permute-done.8.refs_2_ = f32[9,3,16,128]{3,2,1,0:T(8,128)S(1)} collective-permute-done((f32[9,3,16,128]{3,2,1,0:T(8,128)S(1)}, f32[9,3,16,128]{3,2,1,0:T(8,128)S(1)}, u32[]{:S(2)}, u32[]{:S(2)}) %collective-permute-start.8) | collective-permute-done | bytes 221216 | tf_op jit(solution)/shard_map/ppermute | solution.py:367
  46.3 1.9 %shard_map.60 = (f32[3456,128]{1,0:T(8,128)S(1)}, bf16[384,384]{1,0:T(8,128)(2,1)S(1)}) custom-call(f32[72,72]{1,0:T(8,128)S(1)} %copy-done, f32[3456,128]{1,0:T(8,128)S(1)} %get-tuple-element.29.refs_0_, bf16[384,384]{1,0:T(8,128)(2,1)S(1)} %get-tuple-element.30.refs_1_, f32[9,3,16,128]{3,2,1,0:T(8,128)S(1)} %collective-permute-done.8.refs_2_, ...), custom_call_target="tpu_custom_call" | custom-call | tf_op jit(solution)/shard_map/pallas_call | solution.py:347
  48.2 1.9 %collective-permute-done.10.refs_0_ = f32[9,3,16,128]{3,2,1,0:T(8,128)S(1)} collective-permute-done((f32[9,3,16,128]{3,2,1,0:T(8,128)S(1)}, f32[9,3,16,128]{3,2,1,0:T(8,128)S(1)}, u32[]{:S(2)}, u32[]{:S(2)}) %collective-permute-start.10) | collective-permute-done | bytes 221216 | tf_op jit(solution)/shard_map/ppermute | solution.py:367
  50.1 0.1 collective-permute-done.11.refs_1_
  50.2 2.7 %shard_map.61 = f32[72,16,384]{2,1,0:T(8,128)} custom-call(f32[72,72]{1,0:T(8,128)S(1)} %copy-done, f32[3456,128]{1,0:T(8,128)S(1)} %get-tuple-element.33.earlier, bf16[384,384]{1,0:T(8,128)(2,1)S(1)} %get-tuple-element.34.matrix, f32[9,3,16,128]{3,2,1,0:T(8,128)S(1)} %collective-permute-done.10.refs_0_, f32[9,3,16,128]{3,2,1,0:T(8,128)S(1)} %collective-permute-done.11.refs_1_), custom_call_target="tpu_custom_call" | custom-call | tf_op jit(solution)/shard_map/pallas_call | solution.py:355
  (12 shorter events, 0.2 us)
Async XLA Ops:
  2.3 1.8 %collective-permute-start.1 = (f32[2,3,112,128]{3,2,1,0:T(8,128)S(1)}, f32[2,3,112,128]{3,2,1,0:T(8,128)S(1)}, u32[]{:S(2)}, u32[]{:S(2)}) collective-permute-start(f32[2,3,112,128]{3,2,1,0:T(8,128)S(1)} %get-tuple-element.24), channel_id=1, source_target_pairs={{0,1},{1,0},{2,3},{3,2},{4,5},{5,4},{6,7},{7,6},{8,9},{9,8},{10,11... | collective-permute-start | bytes 1032200 | tf_op jit(solution)/shard_map/ppermute | solution.py:367
  2.8 15.3 %collective-permute-start = (f32[9,3,32,128]{3,2,1,0:T(8,128)S(1)}, f32[9,3,32,128]{3,2,1,0:T(8,128)S(1)}, u32[]{:S(2)}, u32[]{:S(2)}) collective-permute-start(f32[9,3,32,128]{3,2,1,0:T(8,128)S(1)} %get-tuple-element.22), channel_id=1, source_target_pairs={{0,1},{1,0},{2,3},{3,2},{4,5},{5,4},{6,7},{7,6},{8,9},{9,8},{10,11... | collective-permute-start | bytes 1327112 | tf_op jit(solution)/shard_map/ppermute | solution.py:367
  4.1 14.0 %collective-permute-start.3 = (f32[2,3,112,128]{3,2,1,0:T(8,128)S(1)}, f32[2,3,112,128]{3,2,1,0:T(8,128)S(1)}, u32[]{:S(2)}, u32[]{:S(2)}) collective-permute-start(f32[2,3,112,128]{3,2,1,0:T(8,128)S(1)} %get-tuple-element.39), channel_id=1, source_target_pairs={{4,0},{8,4},{12,8},{5,1},{9,5},{13,9},{6,2},{10,6},{14,10},{7,3},{... | collective-permute-start | bytes 1032200 | tf_op jit(solution)/shard_map/ppermute | solution.py:372
  5.4 13.1 %collective-permute-start.2 = (f32[2,3,112,128]{3,2,1,0:T(8,128)S(1)}, f32[2,3,112,128]{3,2,1,0:T(8,128)S(1)}, u32[]{:S(2)}, u32[]{:S(2)}) collective-permute-start(f32[2,3,112,128]{3,2,1,0:T(8,128)S(1)} %get-tuple-element.40), channel_id=1, source_target_pairs={{0,4},{4,8},{8,12},{1,5},{5,9},{9,13},{2,6},{6,10},{10,14},{3,7},{... | collective-permute-start | bytes 1032200 | tf_op jit(solution)/shard_map/ppermute | solution.py:372
  12.3 3.9 %collective-permute-start.4 = (s32[8,128]{1,0:T(8,128)S(1)}, s32[8,128]{1,0:T(8,128)S(1)}, u32[]{:S(2)}, u32[]{:S(2)}) collective-permute-start(s32[8,128]{1,0:T(8,128)S(1)} %broadcast_in_dim.3.base), channel_id=1, source_target_pairs={{0,16},{16,0},{1,17},{17,1},{2,18},{18,2},{3,19},{19,3},{4,20},{20... | collective-permute-start | bytes 12296 | tf_op jit(solution)/shard_map/ppermute | solution.py:367
  18.5 22.0 %copy-start = (f32[72,72]{1,0:T(8,128)S(1)}, f32[72,72]{1,0:T(8,128)}, u32[]{:S(2)}) copy-start(f32[72,72]{1,0:T(8,128)} %weights.5) | copy-start | bytes 62212
  27.3 6.0 %collective-permute-start.5 = (f32[9,3,16,128]{3,2,1,0:T(8,128)S(1)}, f32[9,3,16,128]{3,2,1,0:T(8,128)S(1)}, u32[]{:S(2)}, u32[]{:S(2)}) collective-permute-start(f32[9,3,16,128]{3,2,1,0:T(8,128)S(1)} %get-tuple-element.26), channel_id=1, source_target_pairs={{0,1},{1,0},{2,3},{3,2},{4,5},{5,4},{6,7},{7,6},{8,9},{9,8},{10,11... | collective-permute-start | bytes 663560 | tf_op jit(solution)/shard_map/ppermute | solution.py:367
  27.3 9.3 %collective-permute-start.6 = (f32[9,3,16,128]{3,2,1,0:T(8,128)S(1)}, f32[9,3,16,128]{3,2,1,0:T(8,128)S(1)}, u32[]{:S(2)}, u32[]{:S(2)}) collective-permute-start(f32[9,3,16,128]{3,2,1,0:T(8,128)S(1)} %get-tuple-element.27), channel_id=1, source_target_pairs={{0,18},{2,16},{16,2},{18,0},{1,19},{3,17},{17,3},{19,1},{4,22},{6,... | collective-permute-start | bytes 663560 | tf_op jit(solution)/shard_map/ppermute | solution.py:367
  30.0 10.5 %collective-permute-start.7 = (f32[9,3,16,128]{3,2,1,0:T(8,128)S(1)}, f32[9,3,16,128]{3,2,1,0:T(8,128)S(1)}, u32[]{:S(2)}, u32[]{:S(2)}) collective-permute-start(f32[9,3,16,128]{3,2,1,0:T(8,128)S(1)} %get-tuple-element.28), channel_id=1, source_target_pairs={{0,19},{1,18},{2,17},{3,16},{16,3},{17,2},{18,1},{19,0},{4,23},{5,... | collective-permute-start | bytes 663560 | tf_op jit(solution)/shard_map/ppermute | solution.py:367
  30.1 16.2 %collective-permute-start.8 = (f32[9,3,16,128]{3,2,1,0:T(8,128)S(1)}, f32[9,3,16,128]{3,2,1,0:T(8,128)S(1)}, u32[]{:S(2)}, u32[]{:S(2)}) collective-permute-start(f32[9,3,16,128]{3,2,1,0:T(8,128)S(1)} %get-tuple-element.31), channel_id=1, source_target_pairs={{0,2},{2,0},{1,3},{3,1},{4,6},{6,4},{5,7},{7,5},{8,10},{10,8},{9,1... | collective-permute-start | bytes 663560 | tf_op jit(solution)/shard_map/ppermute | solution.py:367
  31.7 14.5 %collective-permute-start.9 = (f32[9,3,16,128]{3,2,1,0:T(8,128)S(1)}, f32[9,3,16,128]{3,2,1,0:T(8,128)S(1)}, u32[]{:S(2)}, u32[]{:S(2)}) collective-permute-start(f32[9,3,16,128]{3,2,1,0:T(8,128)S(1)} %get-tuple-element.32), channel_id=1, source_target_pairs={{0,16},{16,0},{1,17},{17,1},{2,18},{18,2},{3,19},{19,3},{4,20},{20... | collective-permute-start | bytes 663560 | tf_op jit(solution)/shard_map/ppermute | solution.py:367
  33.3 16.8 %collective-permute-start.10 = (f32[9,3,16,128]{3,2,1,0:T(8,128)S(1)}, f32[9,3,16,128]{3,2,1,0:T(8,128)S(1)}, u32[]{:S(2)}, u32[]{:S(2)}) collective-permute-start(f32[9,3,16,128]{3,2,1,0:T(8,128)S(1)} %get-tuple-element.35), channel_id=1, source_target_pairs={{0,3},{1,2},{2,1},{3,0},{4,7},{5,6},{6,5},{7,4},{8,11},{9,10},{10,... | collective-permute-start | bytes 663560 | tf_op jit(solution)/shard_map/ppermute | solution.py:367
  36.6 13.6 %collective-permute-start.11 = (f32[9,3,16,128]{3,2,1,0:T(8,128)S(1)}, f32[9,3,16,128]{3,2,1,0:T(8,128)S(1)}, u32[]{:S(2)}, u32[]{:S(2)}) collective-permute-start(f32[9,3,16,128]{3,2,1,0:T(8,128)S(1)} %get-tuple-element.36), channel_id=1, source_target_pairs={{0,17},{1,16},{16,1},{17,0},{2,19},{3,18},{18,3},{19,2},{4,21},{5,... | collective-permute-start | bytes 663560 | tf_op jit(solution)/shard_map/ppermute | solution.py:367
